TPU v7x, 32 devices: a whole 2x2x4 slice. The times are simulated.
32 devices in a mesh: seq: 4 (over x, core), grp: 8 (over z, y).
Axes of the slice: x: 2, y: 2, z: 4, core: 2. Of those that a mesh axis runs over, the one named last changes fastest.
Arguments:
- tokens: bfloat16 [8, 512, 1408], P('grp', 'seq'), may hold values from -6 to 6
- target_kv: bfloat16 [1408, 1408], P('seq'), may hold values from -0.15625 to 0.15625
- context_kv: bfloat16 [1408, 1408], P('seq'), may hold values from -0.15625 to 0.15625
- query_weight: bfloat16 [704, 1408], replicated, may hold values from -0.15625 to 0.15625
- pred_hidden: bfloat16 [8, 512, 384], P('grp', 'seq'), may hold values from -6 to 6
- pred_weight: bfloat16 [8, 704, 384], P('grp'), may hold values from -0.3125 to 0.3125
- target_mask: int32 [8, 256], P('grp', 'seq'), may hold values 0 or 1
- owners: int32 [8, 256, 1], P('grp', 'seq'), may hold values from 0 to 7; in each aligned block of 64 rows (0 to 63, 64 to 127, ..., all dimensions but the last counted through in order) at most 8 rows name the same one
Outputs:
- new_kv: bfloat16 [1408, 1408], P('seq')
- targets: bfloat16 [8, 512, 704], P('grp', 'seq')
- pred_grad: bfloat16 [8, 512, 384], P('grp', 'seq')
Inputs may be any that keep to these rules, and one draw needn't show every extreme that they name: `owners`: among the 64 token pairs of one device no owner is named more than 8 times, a bound that some block reaches.
All inputs are finite; a program needn't handle non-finite values. No bound on the sum of `target_mask` on one device may be relied on, other than what follows from the above.
Results may differ from a plain program's by a relative error of at most 0.011.
Values may be sent and summed in bfloat16 or wider, within the bound.
No kernel may reach another device: no remote copies, remote signals or barrier semaphores. Data moves between devices by JAX's collectives and lax.ppermute only.
A program may use at most 64 MiB of HBM per device.

v0:
```python
import math

import jax
import jax.numpy as jnp
from jax import lax
from jax.sharding import PartitionSpec as P

HEAD = 64
HEADS = 11


keep_rate = 0.9
epsilon = 1e-05


def layer_norm(values):
    center = values - jnp.mean(values, axis=-1, keepdims=True)
    variance = jnp.mean(center * center, axis=-1, keepdims=True)
    return center * lax.rsqrt(variance + epsilon)


def norm_backward(upstream, normed, inputs):
    center = inputs - jnp.mean(inputs, axis=-1, keepdims=True)
    variance = jnp.mean(center * center, axis=-1, keepdims=True)
    inverse = lax.rsqrt(variance + epsilon)
    upstream_mean = jnp.mean(upstream, axis=-1, keepdims=True)
    cross_mean = jnp.mean(upstream * normed, axis=-1, keepdims=True)
    return inverse * (upstream - upstream_mean - normed * cross_mean)


def owner_compute(received, expert_weight):
    received_targets, received_hidden = received
    groups = received_targets.shape[0]
    items = received_targets.shape[1]
    pred_size = expert_weight.shape[1]
    width = expert_weight.shape[0]
    inputs = received_hidden.reshape(-1, pred_size).astype(jnp.float32)
    normed = layer_norm(inputs)
    prediction = jnp.einsum(
        "tp,ap->ta", normed.astype(jnp.bfloat16), expert_weight, preferred_element_type=jnp.float32
    )
    residual = prediction - received_targets.reshape(-1, width).astype(jnp.float32)
    upstream = jnp.dot(
        residual.astype(jnp.bfloat16), expert_weight, preferred_element_type=jnp.float32
    )
    grad = norm_backward(upstream, normed, inputs).astype(jnp.bfloat16)
    return grad.reshape(groups, items, 2 * pred_size)


def shards(
    tokens, target_kv, context_kv, query_weight, pred_hidden, pred_weight, target_mask, owners
):
    new_kv = (
        keep_rate * target_kv.astype(jnp.float32)
        + (1.0 - keep_rate) * context_kv.astype(jnp.float32)
    ).astype(jnp.bfloat16)
    width = HEADS * HEAD
    scale = 1.0 / math.sqrt(HEAD)
    rows = tokens.shape[1]
    normed = layer_norm(tokens[0].astype(jnp.float32)).astype(jnp.bfloat16)
    queries = jnp.einsum(
        "td,ad->ta", normed, query_weight, preferred_element_type=jnp.float32
    ).astype(jnp.bfloat16)
    query_heads = queries.reshape(rows, HEADS, HEAD)
    own_kv = jnp.dot(
        normed,
        lax.all_gather(new_kv, "seq", axis=0, tiled=True),
        preferred_element_type=jnp.float32,
    ).astype(jnp.bfloat16)
    key_values = lax.all_gather(own_kv, "seq", axis=0, tiled=True)
    count = key_values.shape[0]
    keys = key_values[:, :width].reshape(count, HEADS, HEAD)
    values = key_values[:, width:].reshape(count, HEADS, HEAD)
    scores = (
        jnp.einsum("qhd,khd->hqk", query_heads, keys, preferred_element_type=jnp.float32) * scale
    )
    expo = jnp.exp(scores)
    added = jnp.einsum(
        "hqk,khd->qhd", expo.astype(jnp.bfloat16), values, preferred_element_type=jnp.float32
    )
    numerator = added.reshape(rows, width)
    denominator = jnp.sum(expo, axis=-1)
    attended = (numerator.reshape(rows, HEADS, HEAD) / denominator.T[:, :, None]).reshape(
        rows, width
    )
    targets = layer_norm(attended).astype(jnp.bfloat16)
    blocks = target_mask.shape[1]
    groups = lax.axis_size("grp")
    capacity = max(2, (blocks + groups - 1) // groups)
    pred_size = pred_hidden.shape[2]
    owner_ids = owners[0, :, 0]
    live = target_mask[0]
    chosen = (
        (owner_ids[:, None] == jnp.arange(groups, dtype=jnp.int32)[None, :]) & (live[:, None] == 1)
    ).astype(jnp.int32)
    earlier = jnp.cumsum(chosen, axis=0) - chosen
    position = jnp.sum(earlier * chosen, axis=1)
    slot_index = owner_ids * capacity + position
    dispatch = (
        (jnp.arange(groups * capacity, dtype=jnp.int32)[:, None] == slot_index[None, :])
        & (live[None, :] == 1)
    ).astype(jnp.bfloat16)
    send_targets = (
        jnp.dot(dispatch, targets.reshape(blocks, 2 * width), preferred_element_type=jnp.float32)
        .astype(jnp.bfloat16)
        .reshape(groups, capacity, 2 * width)
    )
    send_hidden = (
        jnp.dot(
            dispatch,
            pred_hidden[0].reshape(blocks, 2 * pred_size),
            preferred_element_type=jnp.float32,
        )
        .astype(jnp.bfloat16)
        .reshape(groups, capacity, 2 * pred_size)
    )
    expert_weight = pred_weight[0]
    owner_grads = owner_compute(
        (
            lax.all_to_all(send_targets, "grp", split_axis=0, concat_axis=0, tiled=True),
            lax.all_to_all(send_hidden, "grp", split_axis=0, concat_axis=0, tiled=True),
        ),
        expert_weight,
    )
    back_grads = lax.all_to_all(owner_grads, "grp", split_axis=0, concat_axis=0, tiled=True)
    pair_grads = jnp.dot(
        dispatch.T,
        back_grads.reshape(groups * capacity, 2 * pred_size),
        preferred_element_type=jnp.float32,
    )
    pred_grad = pair_grads.astype(jnp.bfloat16).reshape(rows, pred_size)
    return (new_kv, targets[None], pred_grad[None])


def solution(mesh):
    placed = (
        P("grp", "seq", None),
        P("seq", None),
        P("seq", None),
        P(),
        P("grp", "seq", None),
        P("grp", None, None),
        P("grp", "seq"),
        P("grp", "seq", None),
    )
    return jax.shard_map(
        shards,
        mesh=mesh,
        in_specs=placed,
        out_specs=(P("seq", None), P("grp", "seq", None), P("grp", "seq", None)),
        check_vma=False,
    )
```

profile of v0, /device:TPU:0, one launch (start us, length us, event | category | flops | bytes accessed | tf_op | source)
XLA Modules:
  0.0 123.1 jit_solution(10138029074901712621)
XLA Ops:
  7.2 3.0 %add_convert_fusion = bf16[352,1408]{1,0:T(8,128)(2,1)} fusion(bf16[352,1408]{1,0:T(8,128)(2,1)} %param.10, bf16[352,1408]{1,0:T(8,128)(2,1)} %param.9), kind=kLoop, calls=%fused_computation.6 | loop fusion | flops 2973696 | bytes 2973696 | tf_op jit(solution)/shard_map/convert_element_type | solution.py:56
  10.7 35.5 %all-gather.3.cloned.1.call-done = bf16[1408,1408]{1,0:T(8,128)(2,1)} async-done(((bf16[352,1408]{1,0:T(8,128)(2,1)}), bf16[1408,1408]{1,0:T(8,128)(2,1)}) %all-gather.3.cloned.1.call-update) | async-done | bytes 3964944 | tf_op jit(solution)/shard_map/all_gather | solution.py:67
  46.3 3.7 %convolution_convert_fusion = bf16[128,1408]{1,0:T(8,128)(2,1)} fusion(bf16[1408,1408]{1,0:T(8,128)(2,1)} %all-gather.3.cloned.1.call-done, bf16[1,128,1408]{2,1,0:T(8,128)(2,1)S(1)} %copy-done.1, f32[128]{0:T(128)S(1)} %add_rsqrt_fusion.2, f32[128]{0:T(128)S(1)} %broadcast_multiply_fusion.4), kind=kOutput, calls=%fused_computation.3 | convolution fusion | flops 508411904 | bytes 4686848 | tf_op jit(solution)/shard_map/dot_general | solution.py:65
  50.4 0.8 fusion.14
  51.3 5.5 %all-to-all-start = ((bf16[8,8,768]{2,1,0:T(8,128)(2,1)}), bf16[8,8,768]{2,1,0:T(8,128)(2,1)S(1)}, u32[]{:S(2)}, u32[]{:S(2)}) async-start(bf16[8,8,768]{2,1,0:T(8,128)(2,1)} %fusion.14), calls=%async_computation | async-start | bytes 196608 | tf_op jit(solution)/shard_map/all_to_all | solution.py:121
  56.8 0.8 convolution_convert_fusion.2
  57.5 6.4 %all-to-all-done = bf16[8,8,768]{2,1,0:T(8,128)(2,1)S(1)} async-done(((bf16[8,8,768]{2,1,0:T(8,128)(2,1)}), bf16[8,8,768]{2,1,0:T(8,128)(2,1)S(1)}, u32[]{:S(2)}, u32[]{:S(2)}) %all-to-all-start) | async-done | bytes 98336 | tf_op jit(solution)/shard_map/all_to_all | solution.py:121
  64.5 4.5 %all-gather.5.cloned.1.call-done = bf16[512,1408]{1,0:T(8,128)(2,1)} async-done(((bf16[128,1408]{1,0:T(8,128)(2,1)}), bf16[512,1408]{1,0:T(8,128)(2,1)}) %all-gather.5.cloned.1.call-update) | async-done | bytes 1441808 | tf_op jit(solution)/shard_map/all_gather | solution.py:70
  69.0 2.7 %fusion.41 = (bf16[512,704]{1,0:T(8,128)(2,1)}, bf16[512,704]{1,0:T(8,128)(2,1)S(1)}) fusion(bf16[512,1408]{1,0:T(8,128)(2,1)} %all-gather.5.cloned.1.call-done), kind=kLoop, calls=%fused_computation.60 | loop fusion | bytes 2883584 | tf_op jit(solution)/shard_map/slice | solution.py:72
  71.7 2.2 %copy.16 = bf16[512,704]{0,1:T(8,128)(2,1)} copy(bf16[512,704]{1,0:T(8,128)(2,1)} %get-tuple-element.5) | data formatting | bytes 1441792 | tf_op jit(solution)/shard_map/slice | solution.py:72
  74.0 1.1 copy.15
  75.1 1.9 %fusion = (f32[11,128]{1,0:T(8,128)S(1)}, f32[11,128,512]{2,1,0:T(8,128)S(1)}) fusion(bf16[128,11,64]{0,2,1:T(8,128)(2,1)S(1)} %bitcast.60, bf16[512,11,64]{0,2,1:T(8,128)(2,1)} %bitcast.57), kind=kOutput, calls=%fused_computation.1 | convolution fusion | flops 93715072 | bytes 3790336 | tf_op jit(solution)/shard_map/qhd,khd->hqk/dot_general | solution.py:75
  77.7 1.4 %copy.19 = f32[128,11,64]{2,1,0:T(8,128)} copy(f32[128,11,64]{0,2,1:T(8,128)S(1)} %get-tuple-element.10) | data formatting | bytes 720896 | tf_op jit(solution)/shard_map/div | solution.py:83
  79.7 1.0 mul.125
  80.7 2.3 %reshape.199 = f32[64,1408]{1,0:T(8,128)} reshape(f32[128,11,64]{2,1,0:T(8,128)} %copy.19) | data formatting | bytes 720896 | tf_op jit(solution)/shard_map/reshape | solution.py:83
  83.1 1.0 sub.84
  84.2 2.1 %fusion.2 = bf16[8,8,1408]{2,1,0:T(8,128)(2,1)} fusion(f32[64,1408]{1,0:T(8,128)} %mul.125, f32[64,1408]{1,0:T(8,128)} %reshape.199, f32[64,1408]{1,0:T(8,128)} %sub.84, s32[64]{0:T(128)S(1)} %multiply_add_fusion, pred[64]{0:T(512)(128)(4,1)S(1)} %compare_bitcast_fusion), kind=kOutput, calls=%fused_computation.5 | convolution fusion | flops 11902976 | bytes 1261888 | tf_op jit(solution)/shard_map/dot_general | solution.py:104
  86.3 5.5 %all-to-all-start.1 = ((bf16[8,8,1408]{2,1,0:T(8,128)(2,1)}), bf16[8,8,1408]{2,1,0:T(8,128)(2,1)}, u32[]{:S(2)}, u32[]{:S(2)}) async-start(bf16[8,8,1408]{2,1,0:T(8,128)(2,1)} %fusion.2), calls=%async_computation.1 | async-start | bytes 360448 | tf_op jit(solution)/shard_map/all_to_all | solution.py:120
  93.2 6.8 %all-to-all-done.1 = bf16[8,8,1408]{2,1,0:T(8,128)(2,1)} async-done(((bf16[8,8,1408]{2,1,0:T(8,128)(2,1)}), bf16[8,8,1408]{2,1,0:T(8,128)(2,1)}, u32[]{:S(2)}, u32[]{:S(2)}) %all-to-all-start.1) | async-done | bytes 180256 | tf_op jit(solution)/shard_map/all_to_all | solution.py:120
  100.0 1.1 reshape.204
  101.1 2.1 %fusion.40 = (f32[128]{0:T(128)S(1)}, f32[128]{0:T(128)S(1)}, f32[128,384]{1,0:T(8,128)}) fusion(f32[128]{0:T(128)S(1)} %add_rsqrt_fusion, f32[128,384]{1,0:T(8,128)S(1)} %reshape.203, f32[128]{0:T(128)S(1)} %broadcast_multiply_fusion.2, bf16[1,704,384]{2,1,0:T(8,128)(2,1)S(1)} %copy-done.3, f32[128,704]{1,0:T(8,128)S(1)} %reshape.204, ...), kind=kOutput, calls=%fused_computation.59 | convolution fusion | flops 138837760 | bytes 1394688 | tf_op jit(solution)/shard_map/dot_general | solution.py:43
  103.2 1.1 multiply_convert_fusion.1
  105.0 3.4 %all-to-all-start.2 = ((bf16[8,8,768]{2,1,0:T(8,128)(2,1)}), bf16[8,8,768]{2,1,0:T(8,128)(2,1)S(1)}, u32[]{:S(2)}, u32[]{:S(2)}) async-start(bf16[8,8,768]{2,1,0:T(8,128)(2,1)} %reshape.201), calls=%async_computation.2 | async-start | bytes 196608 | tf_op jit(solution)/shard_map/all_to_all | solution.py:125
  109.0 6.3 %all-to-all-done.2 = bf16[8,8,768]{2,1,0:T(8,128)(2,1)S(1)} async-done(((bf16[8,8,768]{2,1,0:T(8,128)(2,1)}), bf16[8,8,768]{2,1,0:T(8,128)(2,1)S(1)}, u32[]{:S(2)}, u32[]{:S(2)}) %all-to-all-start.2) | async-done | bytes 98336 | tf_op jit(solution)/shard_map/all_to_all | solution.py:125
  (58 shorter events, 6.6 us)
Async XLA Ops:
  7.2 49.6 %copy-start = (bf16[704,1408]{1,0:T(8,128)(2,1)S(1)}, bf16[704,1408]{1,0:T(8,128)(2,1)}, u32[]{:S(2)}) copy-start(bf16[704,1408]{1,0:T(8,128)(2,1)} %param.11) | copy-start | bytes 5947396
  7.2 3.1 %copy-start.1 = (bf16[1,128,1408]{2,1,0:T(8,128)(2,1)S(1)}, bf16[1,128,1408]{2,1,0:T(8,128)(2,1)}, u32[]{:S(2)}) copy-start(bf16[1,128,1408]{2,1,0:T(8,128)(2,1)} %param.8) | copy-start | bytes 1081348
  7.2 39.1 %all-gather.3.cloned.1.call-start = ((), (), s32[]{:S(2)}) async-start(), calls=%async_computation.3 | async-start | bytes 4956160 | tf_op jit(solution)/shard_map/all_gather | solution.py:67
  10.2 58.8 %all-gather.5.cloned.1.call-start = ((), (), s32[]{:S(2)}) async-start(), calls=%async_computation.4 | async-start | bytes 1802240 | tf_op jit(solution)/shard_map/all_gather | solution.py:70
  10.7 39.3 %copy-start.6 = (bf16[1,128,384]{2,1,0:T(8,128)(2,1)S(1)}, bf16[1,128,384]{2,1,0:T(8,128)(2,1)}, u32[]{:S(2)}) copy-start(bf16[1,128,384]{2,1,0:T(8,128)(2,1)} %param.12) | copy-start | bytes 294916
  10.7 39.3 %copy-start.8 = (s32[1,64]{1,0:T(1,128)S(1)}, s32[1,64]{1,0:T(1,128)}, u32[]{:S(2)}) copy-start(s32[1,64]{1,0:T(1,128)} %param.14) | copy-start | bytes 772
  10.7 39.3 %copy-start.7 = (s32[1,64,1]{1,2,0:T(1,128)S(1)}, s32[1,64,1]{1,2,0:T(1,128)}, u32[]{:S(2)}) copy-start(s32[1,64,1]{1,2,0:T(1,128)} %param.15) | copy-start | bytes 772
  51.3 12.6 %all-to-all-start = ((bf16[8,8,768]{2,1,0:T(8,128)(2,1)}), bf16[8,8,768]{2,1,0:T(8,128)(2,1)S(1)}, u32[]{:S(2)}, u32[]{:S(2)}) async-start(bf16[8,8,768]{2,1,0:T(8,128)(2,1)} %fusion.14), calls=%async_computation | async-start | bytes 196608 | tf_op jit(solution)/shard_map/all_to_all | solution.py:121
  63.9 0.6 copy-start.4
  75.1 1.9 %copy-start.2 = (bf16[512,704]{0,1:T(8,128)(2,1)S(1)}, bf16[512,704]{0,1:T(8,128)(2,1)}, u32[]{:S(2)}) copy-start(bf16[512,704]{0,1:T(8,128)(2,1)} %copy.15) | copy-start | bytes 2162692
  83.1 17.9 %copy-start.3 = (bf16[1,704,384]{2,1,0:T(8,128)(2,1)S(1)}, bf16[1,704,384]{2,1,0:T(8,128)(2,1)}, u32[]{:S(2)}) copy-start(bf16[1,704,384]{2,1,0:T(8,128)(2,1)} %param.13) | copy-start | bytes 1622020
  84.2 8.3 %copy-start.5 = (bf16[8,8,768]{2,1,0:T(8,128)(2,1)S(1)}, bf16[8,8,768]{2,1,0:T(8,128)(2,1)}, u32[]{:S(2)}) copy-start(bf16[8,8,768]{2,1,0:T(8,128)(2,1)} %copy-done.4) | copy-start | bytes 294916
  86.3 13.7 %all-to-all-start.1 = ((bf16[8,8,1408]{2,1,0:T(8,128)(2,1)}), bf16[8,8,1408]{2,1,0:T(8,128)(2,1)}, u32[]{:S(2)}, u32[]{:S(2)}) async-start(bf16[8,8,1408]{2,1,0:T(8,128)(2,1)} %fusion.2), calls=%async_computation.1 | async-start | bytes 360448 | tf_op jit(solution)/shard_map/all_to_all | solution.py:120
  105.0 10.4 %all-to-all-start.2 = ((bf16[8,8,768]{2,1,0:T(8,128)(2,1)}), bf16[8,8,768]{2,1,0:T(8,128)(2,1)S(1)}, u32[]{:S(2)}, u32[]{:S(2)}) async-start(bf16[8,8,768]{2,1,0:T(8,128)(2,1)} %reshape.201), calls=%async_computation.2 | async-start | bytes 196608 | tf_op jit(solution)/shard_map/all_to_all | solution.py:125
Sparse Core Ops, SparseCore 0:
  10.4 35.8 all-gather.2
  50.1 18.8 all-gather.4
where the time goes:
time: 124 us; the launch traced here: 123 us
  waiting for transfers between devices  59.6 us (48%)
  local copies, waits for them, and re-layouts  16.5 us (13%)
  starting transfers between devices  14.5 us (12%)
  between operations  14.3 us (12%)
  matrix products  12.3 us (10%)
  other arithmetic  5.98 us (5%)
    all_gather x1, waiting for transfers between devices, shards(): lax.all_gather(new_kv, 'seq', axis=0, tiled=True)  35.5 us
    all_to_all x1, waiting for transfers between devices, shards(): lax.all_to_all(send_targets, 'grp', split_axis=0, concat_axis=0, tiled=True)  6.78 us
    all_to_all x1, waiting for transfers between devices, shards(): lax.all_to_all(send_hidden, 'grp', split_axis=0, concat_axis=0, tiled=True)  6.36 us
    all_to_all x1, waiting for transfers between devices, shards(): lax.all_to_all(owner_grads, 'grp', split_axis=0, concat_axis=0, tiled=True)  6.34 us
    all_to_all x1, starting transfers between devices, shards(): lax.all_to_all(send_targets, 'grp', split_axis=0, concat_axis=0, tiled=True)  5.52 us
    all_to_all x1, starting transfers between devices, shards(): lax.all_to_all(send_hidden, 'grp', split_axis=0, concat_axis=0, tiled=True)  5.52 us
    slice x2, local copies, waits for them, and re-layouts, shards(): keys = key_values[:, :width].reshape(count, HEADS, HEAD)  4.94 us
    all_gather x1, waiting for transfers between devices, shards(): key_values = lax.all_gather(own_kv, 'seq', axis=0, tiled=True)  4.5 us
  transfers between devices with their start and end apart: 5, of which 5 were waited for; matrix products, arithmetic and copies ran while one was open for 4% of the time, Pallas kernels for 0%

commit v1 on v0

--- a/solution.py
+++ b/solution.py
@@ -3,6 +3,8 @@
 import jax
 import jax.numpy as jnp
 from jax import lax
+from jax.experimental import pallas as pl
+from jax.experimental.pallas import tpu as pltpu
 from jax.sharding import PartitionSpec as P
 
 HEAD = 64
@@ -47,7 +49,7 @@
     return grad.reshape(groups, items, 2 * pred_size)
 
 
-def shards(
+def general_shards(
     tokens, target_kv, context_kv, query_weight, pred_hidden, pred_weight, target_mask, owners
 ):
     new_kv = (
@@ -132,6 +134,300 @@
     return (new_kv, targets[None], pred_grad[None])
 
 
+LANES = 128
+PAIR_BUDGET = 16 << 20
+VM = pl.BlockSpec(memory_space=pltpu.VMEM)
+SM = pl.BlockSpec(memory_space=pltpu.SMEM)
+
+
+def vmem_call(body, outs, operands, specs=None, cost=None, scratch=()):
+    return pl.pallas_call(
+        body,
+        out_shape=outs,
+        in_specs=specs or [VM] * len(operands),
+        out_specs=jax.tree.map(lambda _: VM, outs),
+        scratch_shapes=list(scratch),
+        cost_estimate=cost,
+    )(*operands)
+
+
+def shape_of(dims, kind=jnp.bfloat16):
+    return jax.ShapeDtypeStruct(dims, kind)
+
+
+def matmul_cost(rows, depth, columns, extra=0):
+    return pl.CostEstimate(
+        flops=2 * rows * depth * columns, bytes_accessed=2 * depth * columns, transcendentals=extra
+    )
+
+
+def chip_tiles(tiles, is_first, offset):
+    lane = lax.broadcasted_iota(jnp.int32, tiles[0].shape, 1) < HEAD
+    half = len(tiles) // 2 if offset else len(tiles)
+    mixed = jnp.where(lane, tiles[5], tiles[2])
+    first = [tiles[0], tiles[1], tiles[2]]
+    second = [tiles[3], tiles[4], mixed]
+    if offset:
+        first = first + tiles[5:8]
+        second = second + tiles[8:11]
+    own = [jnp.where(is_first, a, b) for a, b in zip(first, second)]
+    other = [jnp.where(is_first, b, a) for a, b in zip(first, second)]
+    return own, other
+
+
+def norm_body(place, tokens, normed, keep, send):
+    half = tokens.shape[1] // 2
+    values = layer_norm(tokens[...].astype(jnp.float32)).astype(jnp.bfloat16)
+    normed[...] = values
+    low, high = values[:, :half], values[:, half:]
+    is_first = place[0] == 0
+    keep[...] = jnp.where(is_first, low, high)
+    send[...] = jnp.where(is_first, high, low)
+
+
+def query_body(place, normed, weight, own, other):
+    queries = lax.dot_general(
+        normed[...], weight[...], (((1,), (1,)), ((), ())), preferred_element_type=jnp.float32
+    ).astype(jnp.bfloat16).astype(jnp.float32) * (1.0 / math.sqrt(HEAD))
+    full = queries.shape[1] // LANES
+    tiles = [queries[:, t * LANES : (t + 1) * LANES] for t in range(full)]
+    rest = queries[:, full * LANES :]
+    tiles.append(jnp.concatenate([rest, jnp.zeros_like(rest)], axis=1))
+    mine, theirs = chip_tiles(tiles, place[0] == 0, False)
+    for t in range(3):
+        own[:, t * LANES : (t + 1) * LANES] = mine[t].astype(jnp.bfloat16)
+        other[:, t * LANES : (t + 1) * LANES] = theirs[t].astype(jnp.bfloat16)
+
+
+def weight_body(place, own, other, joined):
+    rows = own.shape[0]
+    core = place[1]
+    joined[pl.ds(pl.multiple_of(core * rows, 16), rows), :] = own[...]
+    joined[pl.ds(pl.multiple_of((1 - core) * rows, 16), rows), :] = other[...]
+
+
+def partial_body(place, rows, weight, own, other):
+    sums = jnp.dot(rows[...], weight[...], preferred_element_type=jnp.float32)
+    tiles = [sums[:, t * LANES : (t + 1) * LANES] for t in range(sums.shape[1] // LANES)]
+    mine, theirs = chip_tiles(tiles, place[0] == 0, True)
+    for t in range(6):
+        own[:, t * LANES : (t + 1) * LANES] = mine[t]
+        other[:, t * LANES : (t + 1) * LANES] = theirs[t].astype(jnp.bfloat16)
+
+
+def attend_body(q_own, q_other, kv_a, kv_b, mine, theirs):
+    rows = q_own.shape[0]
+    count = 6
+    for queries, out in ((q_own, mine), (q_other, theirs)):
+        found = [None] * count
+        for slot in range(count):
+            tile, upper = slot // 2, slot % 2
+            lane = lax.broadcasted_iota(jnp.int32, (1, LANES), 1) >= HEAD
+            lane = lane if upper else jnp.logical_not(lane)
+            q = queries[:, tile * LANES : (tile + 1) * LANES]
+            q = jnp.where(lane, q, jnp.zeros_like(q))
+            to = (slot + 1) % count
+            v_tile, v_upper = to // 2, to % 2
+            v_lane = lax.broadcasted_iota(jnp.int32, (1, LANES), 1) >= HEAD
+            v_lane = v_lane if v_upper else jnp.logical_not(v_lane)
+            total = None
+            for kv in (kv_a, kv_b):
+                keys = kv[:, tile * LANES : (tile + 1) * LANES]
+                scores = lax.dot_general(
+                    q, keys, (((1,), (1,)), ((), ())), preferred_element_type=jnp.float32
+                )
+                weights = jnp.exp(scores).astype(jnp.bfloat16)
+                start = (3 + v_tile) * LANES
+                values = kv[:, start : start + LANES]
+                values = jnp.where(v_lane, values, jnp.ones_like(values))
+                part = jnp.dot(weights, values, preferred_element_type=jnp.float32)
+                total = part if total is None else total + part
+            found[to] = total / pltpu.roll(total, HEAD, 1)
+        for t in range(3):
+            lane = lax.broadcasted_iota(jnp.int32, (1, LANES), 1) < HEAD
+            joined = jnp.where(lane, found[2 * t], found[2 * t + 1])
+            out[:, t * LANES : (t + 1) * LANES] = joined.astype(out.dtype)
+
+
+def predict_body(place, slots, owner, hidden, own_weight, *refs):
+    pieces = refs[: len(refs) // 2 - 1]
+    swapped = refs[len(refs) // 2 - 1 : -2]
+    prediction, weights = refs[-2], refs[-1]
+    core = place[1]
+    rows = pieces[0].shape[0]
+    low = pl.multiple_of(core * rows, 16)
+    high = pl.multiple_of((1 - core) * rows, 16)
+    weights[0] = own_weight[...]
+    for slot, (mine, theirs) in enumerate(zip(pieces, swapped)):
+        weights[slot + 1, pl.ds(low, rows), :] = mine[...]
+        weights[slot + 1, pl.ds(high, rows), :] = theirs[...]
+    normed = layer_norm(hidden[...].astype(jnp.float32)).astype(jnp.bfloat16)
+    ids = owner[...]
+    total = jnp.zeros(prediction.shape, jnp.float32)
+    for slot in range(len(pieces) + 1):
+        picked = jnp.where(ids == slots[slot], normed, jnp.zeros_like(normed))
+        total = total + lax.dot_general(
+            picked, weights[slot], (((1,), (1,)), ((), ())), preferred_element_type=jnp.float32
+        )
+    prediction[...] = total
+
+
+def finish_body(
+    place, slots, owner, live, attended, returned, prediction, hidden, weights, targets, grad
+):
+    width = targets.shape[1]
+    is_first = place[0] == 0
+    mine, theirs = attended[...], returned[...].astype(jnp.float32)
+    joined = jnp.concatenate(
+        [jnp.where(is_first, mine, theirs), jnp.where(is_first, theirs, mine)], axis=1
+    )
+    lane = lax.broadcasted_iota(jnp.int32, joined.shape, 1) >= HEAD
+    joined = jnp.where(lane, joined, 0.0)
+    mean = jnp.sum(joined, axis=1, keepdims=True) * (1.0 / width)
+    center = jnp.where(lane, joined - mean, 0.0)
+    variance = jnp.sum(center * center, axis=1, keepdims=True) * (1.0 / width)
+    found = (center * lax.rsqrt(variance + epsilon))[:, HEAD:].astype(jnp.bfloat16)
+    targets[...] = found
+    residual = (prediction[...] - found.astype(jnp.float32)).astype(jnp.bfloat16)
+    ids = owner[...]
+    upstream = jnp.zeros(hidden.shape, jnp.float32)
+    for slot in range(weights.shape[0]):
+        picked = jnp.where(ids == slots[slot], residual, jnp.zeros_like(residual))
+        upstream = upstream + jnp.dot(picked, weights[slot], preferred_element_type=jnp.float32)
+    inputs = hidden[...].astype(jnp.float32)
+    back = norm_backward(upstream, layer_norm(inputs), inputs)
+    grad[...] = jnp.where(live[...] == 1, back, 0.0).astype(grad.dtype)
+
+
+def gather_ring(piece, groups):
+    order = list(range(0, groups, 2)) + list(range(groups - 1, 0, -2))
+    ahead = [(order[i], order[(i + 1) % groups]) for i in range(groups)]
+    behind = [(b, a) for a, b in ahead]
+    forward, backward = [], []
+    for table, found, steps in ((ahead, forward, groups // 2), (behind, backward, (groups - 1) // 2)):
+        held = piece
+        for _ in range(steps):
+            held = lax.ppermute(held, "grp", table)
+            found.append(held)
+    where = {g: i for i, g in enumerate(order)}
+    slots = [
+        [g]
+        + [order[(where[g] - k - 1) % groups] for k in range(len(forward))]
+        + [order[(where[g] + k + 1) % groups] for k in range(len(backward))]
+        for g in range(groups)
+    ]
+    return forward + backward, jnp.array(slots, jnp.int32)
+
+
+def paired_shards(
+    tokens, target_kv, context_kv, query_weight, pred_hidden, pred_weight, target_mask, owners
+):
+    members = lax.axis_size("seq")
+    groups = lax.axis_size("grp")
+    across = [(i, (i + members // 2) % members) for i in range(members)]
+    beside = [(i, i ^ 1) for i in range(members)]
+    me = lax.axis_index("seq")
+    chip, core = me // 2, me % 2
+    place = jnp.stack([chip, core]).astype(jnp.int32)
+    rows, width = tokens.shape[1], query_weight.shape[0]
+    features = tokens.shape[2]
+    half = features // 2
+    packed = 3 * LANES
+    pred_size = pred_hidden.shape[2]
+
+    half_rows = pred_weight.shape[1] // 2
+    piece = lax.dynamic_slice(
+        pred_weight[0], (core * half_rows, 0), (half_rows, pred_size)
+    )
+
+    normed, keep, send = vmem_call(
+        norm_body,
+        [shape_of((rows, features)), shape_of((rows, half)), shape_of((rows, half))],
+        (place, tokens[0]),
+        [SM, VM],
+    )
+    kept_other = lax.ppermute(send, "seq", across)
+    new_kv = (
+        keep_rate * target_kv.astype(jnp.float32)
+        + (1.0 - keep_rate) * context_kv.astype(jnp.float32)
+    ).astype(jnp.bfloat16)
+    other_kv = lax.ppermute(new_kv, "seq", beside)
+    q_own, q_send = vmem_call(
+        query_body,
+        [shape_of((rows, packed)), shape_of((rows, packed))],
+        (place, normed, query_weight),
+        [SM, VM, VM],
+        matmul_cost(rows, features, width),
+    )
+    q_other = lax.ppermute(q_send, "seq", across)
+    joined = vmem_call(
+        weight_body, shape_of((half, 2 * width)), (place, new_kv, other_kv), [SM, VM, VM]
+    )
+
+    def partial(values):
+        return vmem_call(
+            partial_body,
+            [shape_of((rows, 2 * packed), jnp.float32), shape_of((rows, 2 * packed))],
+            (place, values, joined),
+            [SM, VM, VM],
+            matmul_cost(rows, half, 2 * width),
+        )
+
+    own_sum, own_send = partial(keep)
+    from_own = lax.ppermute(own_send, "seq", across)
+    other_sum, other_send = partial(kept_other)
+    from_other = lax.ppermute(other_send, "seq", across)
+    kv = jnp.concatenate(
+        [
+            (other_sum + from_own.astype(jnp.float32)).astype(jnp.bfloat16),
+            (own_sum + from_other.astype(jnp.float32)).astype(jnp.bfloat16),
+        ],
+        axis=0,
+    )
+    kv_beside = lax.ppermute(kv, "seq", beside)
+    attended, send_back = vmem_call(
+        attend_body,
+        [shape_of((rows, packed), jnp.float32), shape_of((rows, packed))],
+        (q_own, q_other, kv, kv_beside),
+    )
+    returned = lax.ppermute(send_back, "seq", across)
+
+    pieces, slot_table = gather_ring(piece, groups)
+    swapped = [lax.ppermute(p, "seq", beside) for p in pieces]
+    slots = lax.dynamic_index_in_dim(slot_table, lax.axis_index("grp"), 0, keepdims=False)
+    owner = jnp.repeat(owners[0, :, 0], 2).reshape(rows, 1)
+    live = jnp.repeat(target_mask[0], 2).reshape(rows, 1)
+    prediction, weights = vmem_call(
+        predict_body,
+        [
+            shape_of((rows, width), jnp.float32),
+            shape_of((groups, width, pred_size)),
+        ],
+        (place, slots, owner, pred_hidden[0], pred_weight[0], *pieces, *swapped),
+        [SM, SM] + [VM] * (3 + 2 * len(pieces)),
+        matmul_cost(rows, groups * pred_size, width),
+    )
+    targets, grad = vmem_call(
+        finish_body,
+        [shape_of((rows, width)), shape_of((rows, pred_size))],
+        (
+            place, slots, owner, live, attended, returned, prediction, pred_hidden[0], weights
+        ),
+        [SM, SM] + [VM] * 7,
+        matmul_cost(rows, groups * pred_size, width),
+    )
+    return (new_kv, targets[None], grad[None])
+
+
+def shards(*arguments):
+    pred_weight = arguments[5]
+    gathered = lax.axis_size("grp") * pred_weight.size * pred_weight.dtype.itemsize
+    two_chips = lax.axis_size("seq") == 4
+    if two_chips and lax.axis_size("grp") % 2 == 0 and gathered <= PAIR_BUDGET:
+        return paired_shards(*arguments)
+    return general_shards(*arguments)
+
+
 def solution(mesh):
     placed = (
         P("grp", "seq", None),

time: 124 us -> 78.7 us (0.63)
  waiting for transfers between devices: 59.6 us -> 20.3 us
  Pallas kernels: 0 us -> 28.1 us
  between operations: 14.3 us -> 0.87 us
  matrix products: 12.3 us -> 0 us
  local copies, waits for them, and re-layouts: 16.5 us -> 8.14 us
  starting transfers between devices: 14.5 us -> 17.3 us
  other arithmetic: 5.98 us -> 3.64 us
    all_gather x2 -> x0, waiting for transfers between devices: 40 us -> none  [the longest x1 35.5 us: shards(): lax.all_gather(new_kv, 'seq', axis=0, tiled=True)]
    pallas_call x0 -> x8, Pallas kernels: none -> 28.1 us  [vmem_call(): pl.pallas_call(body, out_shape=outs, in_specs=specs or [VM] * len(operand...]
    ppermute x0 -> x21, waiting for transfers between devices: none -> 20.3 us  [the longest x7 13.4 us: gather_ring(): held = lax.ppermute(held, 'grp', table)]
    all_to_all x3 -> x0, waiting for transfers between devices: 19.5 us -> none  [the longest x1 6.78 us: shards(): lax.all_to_all(send_targets, 'grp', split_axis=0, concat_axis=0, tiled=True)]
    ppermute x0 -> x21, starting transfers between devices: none -> 17.3 us  [the longest x7 8.57 us: gather_ring(): held = lax.ppermute(held, 'grp', table)]
    all_to_all x3 -> x0, starting transfers between devices: 14.4 us -> none  [the longest x1 5.52 us: shards(): lax.all_to_all(send_targets, 'grp', split_axis=0, concat_axis=0, tiled=True)]
    dot_general x8 -> x0, matrix products: 12.3 us -> none  [the longest x1 3.68 us: shards(): jnp.dot(normed, lax.all_gather(new_kv, 'seq', axis=0, tiled=True), prefer...]
    slice x3 -> x0, local copies, waits for them, and re-layouts: 6.07 us -> none  [the longest x2 4.94 us: shards(): keys = key_values[:, :width].reshape(count, HEADS, HEAD)]
  transfers between devices with their start and end apart: 5 -> 21, of which waited for: 5 -> 5; matrix products, arithmetic and copies ran while one was open for 4% -> 6% of each run, Pallas kernels for 0% -> 30%
where the time goes in v1:
time: 78.7 us; the launch traced here: 78.3 us
  Pallas kernels  28.1 us (36%)
  waiting for transfers between devices  20.3 us (26%)
  starting transfers between devices  17.3 us (22%)
  local copies, waits for them, and re-layouts  8.14 us (10%)
  other arithmetic  3.64 us (5%)
  between operations  0.87 us (1%)
    pallas_call x8, Pallas kernels, vmem_call(): pl.pallas_call(body, out_shape=outs, in_specs=specs or [VM] * len(operand...  28.1 us
    ppermute x7, waiting for transfers between devices, gather_ring(): held = lax.ppermute(held, 'grp', table)  13.4 us
    ppermute x7, starting transfers between devices, gather_ring(): held = lax.ppermute(held, 'grp', table)  8.57 us
    unnamed x43, local copies, waits for them, and re-layouts  5.31 us
    ppermute x1, waiting for transfers between devices, paired_shards(): q_other = lax.ppermute(q_send, 'seq', across)  3.5 us
    ppermute x1, waiting for transfers between devices, paired_shards(): from_other = lax.ppermute(other_send, 'seq', across)  3.34 us
    convert_element_type x1, other arithmetic, paired_shards(): new_kv = (keep_rate * target_kv.astype(jnp.float32) + (1.0 - keep_rate) *...  1.92 us
  transfers between devices with their start and end apart: 21, of which 5 were waited for; matrix products, arithmetic and copies ran while one was open for 6% of the time, Pallas kernels for 30%

profile of v1, /device:TPU:0, one launch (start us, length us, event | category | flops | bytes accessed | tf_op | source)
XLA Modules:
  0.0 78.3 jit_solution(5242891749848002509)
XLA Ops:
  0.6 1.9 %add_convert_fusion.own = bf16[352,1408]{1,0:T(8,128)(2,1)S(1)} fusion(bf16[352,1408]{1,0:T(8,128)(2,1)} %param.11, bf16[352,1408]{1,0:T(8,128)(2,1)} %param.10), kind=kLoop, calls=%fused_computation | loop fusion | flops 2973696 | bytes 2973696 | tf_op jit(solution)/shard_map/convert_element_type | solution.py:353
  3.2 2.7 %collective-permute-start.7 = (bf16[352,384]{1,0:T(8,128)(2,1)S(1)}, bf16[352,384]{1,0:T(8,128)(2,1)S(1)}, u32[]{:S(2)}, u32[]{:S(2)}) collective-permute-start(bf16[352,384]{1,0:T(8,128)(2,1)S(1)} %dynamic-slice_bitcast_fusion), channel_id=1, source_target_pairs={{0,2},{2,4},{4,6},{6,7},{7,5},{5,3},{3,1},{1,0},{8,10},{10,12},{12... | collective-permute-start | bytes 811016 | tf_op jit(solution)/shard_map/ppermute | solution.py:310
  5.8 7.0 %collective-permute-done.7.refs_0_ = bf16[352,384]{1,0:T(8,128)(2,1)S(1)} collective-permute-done((bf16[352,384]{1,0:T(8,128)(2,1)S(1)}, bf16[352,384]{1,0:T(8,128)(2,1)S(1)}, u32[]{:S(2)}, u32[]{:S(2)}) %collective-permute-start.7) | collective-permute-done | bytes 270368 | tf_op jit(solution)/shard_map/ppermute | solution.py:310
  12.9 1.8 %collective-permute-start.8 = (bf16[352,384]{1,0:T(8,128)(2,1)S(1)}, bf16[352,384]{1,0:T(8,128)(2,1)S(1)}, u32[]{:S(2)}, u32[]{:S(2)}) collective-permute-start(bf16[352,384]{1,0:T(8,128)(2,1)S(1)} %collective-permute-done.7.refs_0_), channel_id=1, source_target_pairs={{0,2},{2,4},{4,6},{6,7},{7,5},{5,3},{3,1},{1,0},{8,10},{10,12},{12... | collective-permute-start | bytes 811016 | tf_op jit(solution)/shard_map/ppermute | solution.py:310
  15.3 2.2 %shard_map.112 = (bf16[128,1408]{1,0:T(8,128)(2,1)}, bf16[128,704]{1,0:T(8,128)(2,1)}, bf16[128,704]{1,0:T(8,128)(2,1)}) custom-call(s32[2]{0:T(128)} %pad_add_fusion.place, bf16[128,1408]{1,0:T(8,128)(2,1)} %bitcast.16), custom_call_target="tpu_custom_call" | custom-call | tf_op jit(solution)/shard_map/pallas_call | solution.py:144
  17.4 1.5 %collective-permute-start.1 = (bf16[128,704]{1,0:T(8,128)(2,1)}, bf16[128,704]{1,0:T(8,128)(2,1)S(1)}, u32[]{:S(2)}, u32[]{:S(2)}) collective-permute-start(bf16[128,704]{1,0:T(8,128)(2,1)} %get-tuple-element.21), channel_id=1, source_target_pairs={{0,16},{8,24},{16,0},{24,8},{1,17},{9,25},{17,1},{25,9},{2,18},{10... | collective-permute-start | bytes 540680 | tf_op jit(solution)/shard_map/ppermute | solution.py:349
  19.9 3.0 %shard_map.114.weight = bf16[704,1408]{1,0:T(8,128)(2,1)} custom-call(s32[2]{0:T(128)} %pad_add_fusion.place, bf16[352,1408]{1,0:T(8,128)(2,1)} %copy-done, bf16[352,1408]{1,0:T(8,128)(2,1)} %copy-done.3), custom_call_target="tpu_custom_call" | custom-call | tf_op jit(solution)/shard_map/pallas_call | solution.py:144
  22.9 3.0 %shard_map.116 = (f32[128,768]{1,0:T(8,128)}, bf16[128,768]{1,0:T(8,128)(2,1)}) custom-call(s32[2]{0:T(128)} %pad_add_fusion.place, bf16[128,704]{1,0:T(8,128)(2,1)} %get-tuple-element.23.rows, bf16[704,1408]{1,0:T(8,128)(2,1)} %shard_map.114.weight), custom_call_target="tpu_custom_call" | custom-call | flops 253755392 | bytes 1982464 | tf_op jit(solution)/shard_map/pallas_call | solution.py:144
  26.7 1.8 %collective-permute-start.9 = (bf16[352,384]{1,0:T(8,128)(2,1)S(1)}, bf16[352,384]{1,0:T(8,128)(2,1)S(1)}, u32[]{:S(2)}, u32[]{:S(2)}) collective-permute-start(bf16[352,384]{1,0:T(8,128)(2,1)S(1)} %collective-permute-done.8.refs_1_), channel_id=1, source_target_pairs={{0,2},{2,4},{4,6},{6,7},{7,5},{5,3},{3,1},{1,0},{8,10},{10,12},{12... | collective-permute-start | bytes 811016 | tf_op jit(solution)/shard_map/ppermute | solution.py:310
  29.1 3.0 %shard_map.115 = (f32[128,768]{1,0:T(8,128)}, bf16[128,768]{1,0:T(8,128)(2,1)}) custom-call(s32[2]{0:T(128)} %pad_add_fusion.place, bf16[128,704]{1,0:T(8,128)(2,1)} %copy-done.16, bf16[704,1408]{1,0:T(8,128)(2,1)} %shard_map.114.weight), custom_call_target="tpu_custom_call" | custom-call | flops 253755392 | bytes 1982464 | tf_op jit(solution)/shard_map/pallas_call | solution.py:144
  32.1 1.5 %collective-permute-start.4 = (bf16[128,768]{1,0:T(8,128)(2,1)}, bf16[128,768]{1,0:T(8,128)(2,1)S(1)}, u32[]{:S(2)}, u32[]{:S(2)}) collective-permute-start(bf16[128,768]{1,0:T(8,128)(2,1)} %get-tuple-element.26), channel_id=1, source_target_pairs={{0,16},{8,24},{16,0},{24,8},{1,17},{9,25},{17,1},{25,9},{2,18},{10... | collective-permute-start | bytes 589832 | tf_op jit(solution)/shard_map/ppermute | solution.py:379
  33.6 1.0 %add_convert_fusion.2 = bf16[128,768]{1,0:T(8,128)(2,1)S(1)} fusion(f32[128,768]{1,0:T(8,128)} %get-tuple-element.22, bf16[128,768]{1,0:T(8,128)(2,1)S(1)} %collective-permute-done.3), kind=kLoop, calls=%fused_computation.3 | loop fusion | flops 294912 | bytes 786432 | tf_op jit(solution)/shard_map/convert_element_type | solution.py:382
  34.6 3.3 %collective-permute-done.4 = bf16[128,768]{1,0:T(8,128)(2,1)S(1)} collective-permute-done((bf16[128,768]{1,0:T(8,128)(2,1)}, bf16[128,768]{1,0:T(8,128)(2,1)S(1)}, u32[]{:S(2)}, u32[]{:S(2)}) %collective-permute-start.4) | collective-permute-done | bytes 196640 | tf_op jit(solution)/shard_map/ppermute | solution.py:379
  38.7 3.1 %shard_map.113 = (bf16[128,384]{1,0:T(8,128)(2,1)}, bf16[128,384]{1,0:T(8,128)(2,1)}) custom-call(s32[2]{0:T(128)} %pad_add_fusion.place, bf16[128,1408]{1,0:T(8,128)(2,1)} %get-tuple-element.18.normed, bf16[704,1408]{1,0:T(8,128)(2,1)} %weight.1), custom_call_target="tpu_custom_call" | custom-call | flops 253755392 | bytes 1982464 | tf_op jit(solution)/shard_map/pallas_call | solution.py:144
  41.8 1.5 %collective-permute-start = (bf16[128,384]{1,0:T(8,128)(2,1)}, bf16[128,384]{1,0:T(8,128)(2,1)S(1)}, u32[]{:S(2)}, u32[]{:S(2)}) collective-permute-start(bf16[128,384]{1,0:T(8,128)(2,1)} %get-tuple-element.20), channel_id=1, source_target_pairs={{0,16},{8,24},{16,0},{24,8},{1,17},{9,25},{17,1},{25,9},{2,18},{10... | collective-permute-start | bytes 294920 | tf_op jit(solution)/shard_map/ppermute | solution.py:362
  43.3 3.5 %collective-permute-done.q_other = bf16[128,384]{1,0:T(8,128)(2,1)S(1)} collective-permute-done((bf16[128,384]{1,0:T(8,128)(2,1)}, bf16[128,384]{1,0:T(8,128)(2,1)S(1)}, u32[]{:S(2)}, u32[]{:S(2)}) %collective-permute-start) | collective-permute-done | bytes 98336 | tf_op jit(solution)/shard_map/ppermute | solution.py:362
  47.1 1.8 %collective-permute-start.10 = (bf16[352,384]{1,0:T(8,128)(2,1)S(1)}, bf16[352,384]{1,0:T(8,128)(2,1)}, u32[]{:S(2)}, u32[]{:S(2)}) collective-permute-start(bf16[352,384]{1,0:T(8,128)(2,1)S(1)} %collective-permute-done.9.refs_2_), channel_id=1, source_target_pairs={{0,2},{2,4},{4,6},{6,7},{7,5},{5,3},{3,1},{1,0},{8,10},{10,12},{12... | collective-permute-start | bytes 811016 | tf_op jit(solution)/shard_map/ppermute | solution.py:310
  49.5 6.2 %collective-permute-done.13.refs_6_ = bf16[352,384]{1,0:T(8,128)(2,1)S(1)} collective-permute-done((bf16[352,384]{1,0:T(8,128)(2,1)S(1)}, bf16[352,384]{1,0:T(8,128)(2,1)S(1)}, u32[]{:S(2)}, u32[]{:S(2)}) %collective-permute-start.13) | collective-permute-done | bytes 270368 | tf_op jit(solution)/shard_map/ppermute | solution.py:310
  57.0 4.3 %shard_map.117 = (f32[128,384]{1,0:T(8,128)}, bf16[128,384]{1,0:T(8,128)(2,1)}) custom-call(bf16[128,384]{1,0:T(8,128)(2,1)} %get-tuple-element.19.q_own, bf16[128,384]{1,0:T(8,128)(2,1)} %copy-done.17, bf16[256,768]{1,0:T(8,128)(2,1)} %copy-done.1, bf16[256,768]{1,0:T(8,128)(2,1)} %copy-done.5), custom_call_target="tpu_custom_call" | custom-call | tf_op jit(solution)/shard_map/pallas_call | solution.py:144
  61.3 1.5 %collective-permute-start.6 = (bf16[128,384]{1,0:T(8,128)(2,1)}, bf16[128,384]{1,0:T(8,128)(2,1)S(1)}, u32[]{:S(2)}, u32[]{:S(2)}) collective-permute-start(bf16[128,384]{1,0:T(8,128)(2,1)} %get-tuple-element.28), channel_id=1, source_target_pairs={{0,16},{8,24},{16,0},{24,8},{1,17},{9,25},{17,1},{25,9},{2,18},{10... | collective-permute-start | bytes 294920 | tf_op jit(solution)/shard_map/ppermute | solution.py:393
  62.7 1.2 %dynamic-slice_bitcast_fusion.1.slots = s32[8]{0:T(128)} fusion(s32[8,8]{1,0:T(8,128)} %constant.49.clone, s32[]{:T(128)S(6)} %select_n.20), kind=kLoop, calls=%fused_computation.6 | loop fusion | bytes 68 | tf_op jit(solution)/shard_map/jit(dynamic_index_in_dim)/squeeze | solution.py:397
  66.3 4.9 %shard_map.118 = (f32[128,704]{1,0:T(8,128)}, bf16[8,704,384]{2,1,0:T(8,128)(2,1)}) custom-call(s32[2]{0:T(128)} %pad_add_fusion.place, s32[8]{0:T(128)} %dynamic-slice_bitcast_fusion.1.slots, s32[128,1]{1,0:T(8,128)} %reshape_reshape.8.owner, bf16[128,384]{1,0:T(8,128)(2,1)} %bitcast.14, bf16[704,384]{1,0:T(8,128)(2,1)} %bitcast.13, ...), custom_call_target="tpu_custom_call" | custom-call | flops 553648128 | bytes 4325376 | tf_op jit(solution)/shard_map/pallas_call | solution.py:144
  71.9 4.7 %shard_map.119 = (bf16[128,704]{1,0:T(8,128)(2,1)}, bf16[128,384]{1,0:T(8,128)(2,1)}) custom-call(s32[2]{0:T(128)} %pad_add_fusion.place, s32[8]{0:T(128)} %dynamic-slice_bitcast_fusion.1.slots, s32[128,1]{1,0:T(8,128)} %reshape_reshape.8.owner, s32[128,1]{1,0:T(8,128)} %reshape_reshape.9.live, f32[128,384]{1,0:T(8,128)} %get-tuple-element.27.attended, ...), custom_call_target="tpu_custom_call" | custom-call | flops 553648128 | bytes 4325376 | tf_op jit(solution)/shard_map/pallas_call | solution.py:144
  76.5 1.7 %copy.19 = bf16[1,128,704]{1,2,0:T(8,128)(2,1)} copy(bf16[1,128,704]{2,1,0:T(8,128)(2,1)} %bitcast.17) | data formatting | bytes 360448
  (80 shorter events, 9.3 us)
Async XLA Ops:
  2.6 16.4 %collective-permute-start.2 = (bf16[352,1408]{1,0:T(8,128)(2,1)S(1)}, bf16[352,1408]{1,0:T(8,128)(2,1)S(1)}, u32[]{:S(2)}, u32[]{:S(2)}) collective-permute-start(bf16[352,1408]{1,0:T(8,128)(2,1)S(1)} %add_convert_fusion.own), channel_id=1, source_target_pairs={{0,8},{8,0},{16,24},{24,16},{1,9},{9,1},{17,25},{25,17},{2,10},{10... | collective-permute-start | bytes 2973704 | tf_op jit(solution)/shard_map/ppermute | solution.py:354
  3.2 9.7 %collective-permute-start.7 = (bf16[352,384]{1,0:T(8,128)(2,1)S(1)}, bf16[352,384]{1,0:T(8,128)(2,1)S(1)}, u32[]{:S(2)}, u32[]{:S(2)}) collective-permute-start(bf16[352,384]{1,0:T(8,128)(2,1)S(1)} %dynamic-slice_bitcast_fusion), channel_id=1, source_target_pairs={{0,2},{2,4},{4,6},{6,7},{7,5},{5,3},{3,1},{1,0},{8,10},{10,12},{12... | collective-permute-start | bytes 811016 | tf_op jit(solution)/shard_map/ppermute | solution.py:310
  5.8 20.6 %collective-permute-start.11 = (bf16[352,384]{1,0:T(8,128)(2,1)S(1)}, bf16[352,384]{1,0:T(8,128)(2,1)S(1)}, u32[]{:S(2)}, u32[]{:S(2)}) collective-permute-start(bf16[352,384]{1,0:T(8,128)(2,1)S(1)} %dynamic-slice_bitcast_fusion), channel_id=1, source_target_pairs={{2,0},{4,2},{6,4},{7,6},{5,7},{3,5},{1,3},{0,1},{10,8},{12,10},{14... | collective-permute-start | bytes 811016 | tf_op jit(solution)/shard_map/ppermute | solution.py:310
  12.9 33.9 %copy-start.6 = (bf16[352,384]{1,0:T(8,128)(2,1)}, bf16[352,384]{1,0:T(8,128)(2,1)S(1)}, u32[]{:S(2)}) copy-start(bf16[352,384]{1,0:T(8,128)(2,1)S(1)} %collective-permute-done.7.refs_0_) | copy-start | bytes 811012
  12.9 13.8 %collective-permute-start.8 = (bf16[352,384]{1,0:T(8,128)(2,1)S(1)}, bf16[352,384]{1,0:T(8,128)(2,1)S(1)}, u32[]{:S(2)}, u32[]{:S(2)}) collective-permute-start(bf16[352,384]{1,0:T(8,128)(2,1)S(1)} %collective-permute-done.7.refs_0_), channel_id=1, source_target_pairs={{0,2},{2,4},{4,6},{6,7},{7,5},{5,3},{3,1},{1,0},{8,10},{10,12},{12... | collective-permute-start | bytes 811016 | tf_op jit(solution)/shard_map/ppermute | solution.py:310
  17.4 11.0 %collective-permute-start.1 = (bf16[128,704]{1,0:T(8,128)(2,1)}, bf16[128,704]{1,0:T(8,128)(2,1)S(1)}, u32[]{:S(2)}, u32[]{:S(2)}) collective-permute-start(bf16[128,704]{1,0:T(8,128)(2,1)} %get-tuple-element.21), channel_id=1, source_target_pairs={{0,16},{8,24},{16,0},{24,8},{1,17},{9,25},{17,1},{25,9},{2,18},{10... | collective-permute-start | bytes 540680 | tf_op jit(solution)/shard_map/ppermute | solution.py:349
  25.9 7.7 %collective-permute-start.3 = (bf16[128,768]{1,0:T(8,128)(2,1)}, bf16[128,768]{1,0:T(8,128)(2,1)S(1)}, u32[]{:S(2)}, u32[]{:S(2)}) collective-permute-start(bf16[128,768]{1,0:T(8,128)(2,1)} %get-tuple-element.24), channel_id=1, source_target_pairs={{0,16},{8,24},{16,0},{24,8},{1,17},{9,25},{17,1},{25,9},{2,18},{10... | collective-permute-start | bytes 589832 | tf_op jit(solution)/shard_map/ppermute | solution.py:377
  26.4 20.4 %collective-permute-start.12 = (bf16[352,384]{1,0:T(8,128)(2,1)S(1)}, bf16[352,384]{1,0:T(8,128)(2,1)S(1)}, u32[]{:S(2)}, u32[]{:S(2)}) collective-permute-start(bf16[352,384]{1,0:T(8,128)(2,1)S(1)} %collective-permute-done.11.refs_4_), channel_id=1, source_target_pairs={{2,0},{4,2},{6,4},{7,6},{5,7},{3,5},{1,3},{0,1},{10,8},{12,10},{14... | collective-permute-start | bytes 811016 | tf_op jit(solution)/shard_map/ppermute | solution.py:310
  26.7 20.5 %collective-permute-start.9 = (bf16[352,384]{1,0:T(8,128)(2,1)S(1)}, bf16[352,384]{1,0:T(8,128)(2,1)S(1)}, u32[]{:S(2)}, u32[]{:S(2)}) collective-permute-start(bf16[352,384]{1,0:T(8,128)(2,1)S(1)} %collective-permute-done.8.refs_1_), channel_id=1, source_target_pairs={{0,2},{2,4},{4,6},{6,7},{7,5},{5,3},{3,1},{1,0},{8,10},{10,12},{12... | collective-permute-start | bytes 811016 | tf_op jit(solution)/shard_map/ppermute | solution.py:310
  32.1 5.9 %collective-permute-start.4 = (bf16[128,768]{1,0:T(8,128)(2,1)}, bf16[128,768]{1,0:T(8,128)(2,1)S(1)}, u32[]{:S(2)}, u32[]{:S(2)}) collective-permute-start(bf16[128,768]{1,0:T(8,128)(2,1)} %get-tuple-element.26), channel_id=1, source_target_pairs={{0,16},{8,24},{16,0},{24,8},{1,17},{9,25},{17,1},{25,9},{2,18},{10... | collective-permute-start | bytes 589832 | tf_op jit(solution)/shard_map/ppermute | solution.py:379
  38.0 26.0 %copy-start.19 = (s32[1,64]{1,0:T(1,128)S(1)}, s32[1,64]{1,0:T(1,128)}, u32[]{:S(2)}) copy-start(s32[1,64]{1,0:T(1,128)} %param.15) | copy-start | bytes 772
  38.0 26.7 %copy-start.20 = (s32[1,64,1]{1,2,0:T(1,128)S(1)}, s32[1,64,1]{1,2,0:T(1,128)}, u32[]{:S(2)}) copy-start(s32[1,64,1]{1,2,0:T(1,128)} %param.16) | copy-start | bytes 772
  38.1 18.1 %collective-permute-start.5 = (bf16[256,768]{1,0:T(8,128)(2,1)S(1)}, bf16[256,768]{1,0:T(8,128)(2,1)S(1)}, u32[]{:S(2)}, u32[]{:S(2)}) collective-permute-start(bf16[256,768]{1,0:T(8,128)(2,1)S(1)} %pad_maximum_fusion.kv_a), channel_id=1, source_target_pairs={{0,8},{8,0},{16,24},{24,16},{1,9},{9,1},{17,25},{25,17},{2,10},{10... | collective-permute-start | bytes 1179656 | tf_op jit(solution)/shard_map/ppermute | solution.py:387
  38.2 10.7 %collective-permute-start.18 = (bf16[352,384]{1,0:T(8,128)(2,1)S(1)}, bf16[352,384]{1,0:T(8,128)(2,1)S(1)}, u32[]{:S(2)}, u32[]{:S(2)}) collective-permute-start(bf16[352,384]{1,0:T(8,128)(2,1)S(1)} %collective-permute-done.11.refs_4_), channel_id=1, source_target_pairs={{0,8},{8,0},{16,24},{24,16},{1,9},{9,1},{17,25},{25,17},{2,10},{10... | collective-permute-start | bytes 811016 | tf_op jit(solution)/shard_map/ppermute | solution.py:396
  41.8 5.0 %collective-permute-start = (bf16[128,384]{1,0:T(8,128)(2,1)}, bf16[128,384]{1,0:T(8,128)(2,1)S(1)}, u32[]{:S(2)}, u32[]{:S(2)}) collective-permute-start(bf16[128,384]{1,0:T(8,128)(2,1)} %get-tuple-element.20), channel_id=1, source_target_pairs={{0,16},{8,24},{16,0},{24,8},{1,17},{9,25},{17,1},{25,9},{2,18},{10... | collective-permute-start | bytes 294920 | tf_op jit(solution)/shard_map/ppermute | solution.py:362
  46.8 2.1 %collective-permute-start.14 = (bf16[352,384]{1,0:T(8,128)(2,1)S(1)}, bf16[352,384]{1,0:T(8,128)(2,1)S(1)}, u32[]{:S(2)}, u32[]{:S(2)}) collective-permute-start(bf16[352,384]{1,0:T(8,128)(2,1)S(1)} %collective-permute-done.7.refs_0_), channel_id=1, source_target_pairs={{0,8},{8,0},{16,24},{24,16},{1,9},{9,1},{17,25},{25,17},{2,10},{10... | collective-permute-start | bytes 811016 | tf_op jit(solution)/shard_map/ppermute | solution.py:396
  46.8 8.9 %collective-permute-start.13 = (bf16[352,384]{1,0:T(8,128)(2,1)S(1)}, bf16[352,384]{1,0:T(8,128)(2,1)S(1)}, u32[]{:S(2)}, u32[]{:S(2)}) collective-permute-start(bf16[352,384]{1,0:T(8,128)(2,1)S(1)} %collective-permute-done.12.refs_5_), channel_id=1, source_target_pairs={{2,0},{4,2},{6,4},{7,6},{5,7},{3,5},{1,3},{0,1},{10,8},{12,10},{14... | collective-permute-start | bytes 811016 | tf_op jit(solution)/shard_map/ppermute | solution.py:310
  47.1 8.8 %collective-permute-start.10 = (bf16[352,384]{1,0:T(8,128)(2,1)S(1)}, bf16[352,384]{1,0:T(8,128)(2,1)}, u32[]{:S(2)}, u32[]{:S(2)}) collective-permute-start(bf16[352,384]{1,0:T(8,128)(2,1)S(1)} %collective-permute-done.9.refs_2_), channel_id=1, source_target_pairs={{0,2},{2,4},{4,6},{6,7},{7,5},{5,3},{3,1},{1,0},{8,10},{10,12},{12... | collective-permute-start | bytes 811016 | tf_op jit(solution)/shard_map/ppermute | solution.py:310
  48.9 12.3 %collective-permute-start.19 = (bf16[352,384]{1,0:T(8,128)(2,1)S(1)}, bf16[352,384]{1,0:T(8,128)(2,1)S(1)}, u32[]{:S(2)}, u32[]{:S(2)}) collective-permute-start(bf16[352,384]{1,0:T(8,128)(2,1)S(1)} %collective-permute-done.12.refs_5_), channel_id=1, source_target_pairs={{0,8},{8,0},{16,24},{24,16},{1,9},{9,1},{17,25},{25,17},{2,10},{10... | collective-permute-start | bytes 811016 | tf_op jit(solution)/shard_map/ppermute | solution.py:396
  49.0 16.6 %collective-permute-start.15 = (bf16[352,384]{1,0:T(8,128)(2,1)S(1)}, bf16[352,384]{1,0:T(8,128)(2,1)S(1)}, u32[]{:S(2)}, u32[]{:S(2)}) collective-permute-start(bf16[352,384]{1,0:T(8,128)(2,1)S(1)} %collective-permute-done.8.refs_1_), channel_id=1, source_target_pairs={{0,8},{8,0},{16,24},{24,16},{1,9},{9,1},{17,25},{25,17},{2,10},{10... | collective-permute-start | bytes 811016 | tf_op jit(solution)/shard_map/ppermute | solution.py:396
  55.7 9.9 %collective-permute-start.16 = (bf16[352,384]{1,0:T(8,128)(2,1)S(1)}, bf16[352,384]{1,0:T(8,128)(2,1)}, u32[]{:S(2)}, u32[]{:S(2)}) collective-permute-start(bf16[352,384]{1,0:T(8,128)(2,1)S(1)} %collective-permute-done.9.refs_2_), channel_id=1, source_target_pairs={{0,8},{8,0},{16,24},{24,16},{1,9},{9,1},{17,25},{25,17},{2,10},{10... | collective-permute-start | bytes 811016 | tf_op jit(solution)/shard_map/ppermute | solution.py:396
  55.9 9.7 %collective-permute-start.20 = (bf16[352,384]{1,0:T(8,128)(2,1)S(1)}, bf16[352,384]{1,0:T(8,128)(2,1)}, u32[]{:S(2)}, u32[]{:S(2)}) collective-permute-start(bf16[352,384]{1,0:T(8,128)(2,1)S(1)} %collective-permute-done.13.refs_6_), channel_id=1, source_target_pairs={{0,8},{8,0},{16,24},{24,16},{1,9},{9,1},{17,25},{25,17},{2,10},{10... | collective-permute-start | bytes 811016 | tf_op jit(solution)/shard_map/ppermute | solution.py:396
  56.2 9.4 %collective-permute-start.17 = (bf16[352,384]{1,0:T(8,128)(2,1)}, bf16[352,384]{1,0:T(8,128)(2,1)}, u32[]{:S(2)}, u32[]{:S(2)}) collective-permute-start(bf16[352,384]{1,0:T(8,128)(2,1)} %collective-permute-done.10.refs_3_), channel_id=1, source_target_pairs={{0,8},{8,0},{16,24},{24,16},{1,9},{9,1},{17,25},{25,17},{2,10},{10... | collective-permute-start | bytes 811016 | tf_op jit(solution)/shard_map/ppermute | solution.py:396
  61.3 10.0 %collective-permute-start.6 = (bf16[128,384]{1,0:T(8,128)(2,1)}, bf16[128,384]{1,0:T(8,128)(2,1)S(1)}, u32[]{:S(2)}, u32[]{:S(2)}) collective-permute-start(bf16[128,384]{1,0:T(8,128)(2,1)} %get-tuple-element.28), channel_id=1, source_target_pairs={{0,16},{8,24},{16,0},{24,8},{1,17},{9,25},{17,1},{25,9},{2,18},{10... | collective-permute-start | bytes 294920 | tf_op jit(solution)/shard_map/ppermute | solution.py:393
  (18 other events, 181.7 us)

commit v2 on v0

--- a/solution.py
+++ b/solution.py
@@ -1,9 +1,13 @@
+import functools
 import math
 
 import jax
 import jax.numpy as jnp
 from jax import lax
+from jax.experimental import pallas as pl
+from jax.experimental.pallas import tpu as pltpu
 from jax.sharding import PartitionSpec as P
+
 
 HEAD = 64
 HEADS = 11
@@ -47,7 +51,7 @@
     return grad.reshape(groups, items, 2 * pred_size)
 
 
-def shards(
+def general_shards(
     tokens, target_kv, context_kv, query_weight, pred_hidden, pred_weight, target_mask, owners
 ):
     new_kv = (
@@ -132,6 +136,351 @@
     return (new_kv, targets[None], pred_grad[None])
 
 
+LANES = 128
+PAIR_BUDGET = 16 << 20
+VM = pl.BlockSpec(memory_space=pltpu.VMEM)
+HBM = pl.BlockSpec(memory_space=pltpu.HBM)
+
+
+def local_call(body, outs, operands, specs=None, out_specs=None, cost=None, scratch=(), limit=4):
+    return pl.pallas_call(
+        body,
+        out_shape=outs,
+        in_specs=specs or [VM] * len(operands),
+        out_specs=out_specs or jax.tree.map(lambda _: VM, outs),
+        scratch_shapes=list(scratch),
+        cost_estimate=cost,
+        compiler_params=pltpu.CompilerParams(vmem_limit_bytes=limit << 20),
+    )(*operands)
+
+
+def shape_of(dims, kind=jnp.bfloat16):
+    return jax.ShapeDtypeStruct(dims, kind)
+
+
+def matmul_cost(rows, depth, columns, extra=0):
+    return pl.CostEstimate(
+        flops=2 * rows * depth * columns, bytes_accessed=2 * depth * columns, transcendentals=extra
+    )
+
+
+def chip_and_core():
+    me = lax.axis_index("seq")
+    return me // 2, lax.rem(me, 2)
+
+
+def chip_tiles(tiles, is_first, with_values):
+    lane = lax.broadcasted_iota(jnp.int32, tiles[0].shape, 1) < HEAD
+    mixed = jnp.where(lane, tiles[5], tiles[2])
+    first = [tiles[0], tiles[1], tiles[2]]
+    second = [tiles[3], tiles[4], mixed]
+    if with_values:
+        first = first + tiles[5:8]
+        second = second + tiles[8:11]
+    own = [jnp.where(is_first, a, b) for a, b in zip(first, second)]
+    other = [jnp.where(is_first, b, a) for a, b in zip(first, second)]
+    return own, other
+
+
+def norm_body(tokens, normed, keep, send):
+    half = tokens.shape[1] // 2
+    chip, _ = chip_and_core()
+    values = layer_norm(tokens[...].astype(jnp.float32)).astype(jnp.bfloat16)
+    normed[...] = values
+    low, high = values[:, :half], values[:, half:]
+    keep[...] = jnp.where(chip == 0, low, high)
+    send[...] = jnp.where(chip == 0, high, low)
+
+
+def split_product(rows, weight, own, other):
+    chip, _ = chip_and_core()
+    sums = jnp.dot(rows[...], weight[...], preferred_element_type=jnp.float32)
+    tiles = [sums[:, t * LANES : (t + 1) * LANES] for t in range(sums.shape[1] // LANES)]
+    mine, theirs = chip_tiles(tiles, chip == 0, True)
+    for t in range(6):
+        own[:, t * LANES : (t + 1) * LANES] = mine[t]
+        other[:, t * LANES : (t + 1) * LANES] = theirs[t].astype(jnp.bfloat16)
+
+
+def first_partial_body(
+    own_weight, other_weight, rows, normed, query_weight, joined, own, q_own, send, stored, sem
+):
+    chip, core = chip_and_core()
+    depth = own_weight.shape[0]
+    store = pltpu.make_async_copy(own_weight, stored, sem)
+    store.start()
+    joined[pl.ds(pl.multiple_of(core * depth, 16), depth), :] = own_weight[...]
+    joined[pl.ds(pl.multiple_of((1 - core) * depth, 16), depth), :] = other_weight[...]
+    split_product(rows, joined, own, send)
+    queries = lax.dot_general(
+        normed[...], query_weight[...], (((1,), (1,)), ((), ())), preferred_element_type=jnp.float32
+    ).astype(jnp.bfloat16).astype(jnp.float32) * (1.0 / math.sqrt(HEAD))
+    full = queries.shape[1] // LANES
+    tiles = [queries[:, t * LANES : (t + 1) * LANES] for t in range(full)]
+    rest = queries[:, full * LANES :]
+    tiles.append(jnp.concatenate([rest, jnp.zeros_like(rest)], axis=1))
+    mine, theirs = chip_tiles(tiles, chip == 0, False)
+    for t in range(3):
+        q_own[:, t * LANES : (t + 1) * LANES] = mine[t].astype(jnp.bfloat16)
+        send[:, (6 + t) * LANES : (7 + t) * LANES] = theirs[t].astype(jnp.bfloat16)
+    store.wait()
+
+
+def partial_body(rows, weight, own, other):
+    split_product(rows, weight, own, other)
+
+
+def add_keys(queries, kv_refs, slot):
+    upper_lane = lax.broadcasted_iota(jnp.int32, (1, LANES), 1) >= HEAD
+    tile, upper = slot // 2, slot % 2
+    lane = upper_lane if upper else jnp.logical_not(upper_lane)
+    q = queries[:, tile * LANES : (tile + 1) * LANES]
+    q = jnp.where(lane, q, jnp.zeros_like(q))
+    v_tile, v_upper = (slot + 1) % 6 // 2, (slot + 1) % 2
+    v_lane = upper_lane if v_upper else jnp.logical_not(upper_lane)
+    total = None
+    for kv in kv_refs:
+        keys = kv[:, tile * LANES : (tile + 1) * LANES]
+        scores = lax.dot_general(
+            q, keys, (((1,), (1,)), ((), ())), preferred_element_type=jnp.float32
+        )
+        weights = jnp.exp(scores).astype(jnp.bfloat16)
+        start = (3 + v_tile) * LANES
+        values = kv[:, start : start + LANES]
+        values = jnp.where(v_lane, values, jnp.ones_like(values))
+        part = jnp.dot(weights, values, preferred_element_type=jnp.float32)
+        total = part if total is None else total + part
+    return total
+
+
+def attend_first_body(q_own, received, kv_a, kv_b, own_sums, other_sums):
+    q_other = received[:, 6 * LANES :]
+    for slot in range(6):
+        own_sums[slot] = add_keys(q_own, (kv_a, kv_b), slot)
+        other_sums[slot] = add_keys(q_other, (kv_a, kv_b), slot)
+
+
+def attend_last_body(q_own, received, kv_a, kv_b, own_sums, other_sums, mine, theirs):
+    upper_lane = lax.broadcasted_iota(jnp.int32, (1, LANES), 1) >= HEAD
+    q_other = received[:, 6 * LANES :]
+    for queries, sums, out in ((q_other, other_sums, theirs), (q_own, own_sums, mine)):
+        found = [None] * 6
+        for slot in range(6):
+            total = sums[slot] + add_keys(queries, (kv_a, kv_b), slot)
+            found[(slot + 1) % 6] = total / pltpu.roll(total, HEAD, 1)
+        for t in range(3):
+            joined = jnp.where(upper_lane, found[2 * t + 1], found[2 * t])
+            out[:, t * LANES : (t + 1) * LANES] = joined.astype(out.dtype)
+
+
+def token_values(pairs, rows):
+    shape = (rows, pairs.shape[1])
+    token = lax.broadcasted_iota(jnp.int32, shape, 0) // 2
+    pair = lax.broadcasted_iota(jnp.int32, shape, 1)
+    values = jnp.where(token == pair, pairs[...], 0)
+    return jnp.sum(values, axis=1, keepdims=True)
+
+
+def owner_at(moved, groups):
+    me = lax.axis_index("grp")
+    place = jnp.where(lax.rem(me, 2) == 0, me // 2, groups - 1 - me // 2)
+    place = lax.rem(place + moved + groups, groups)
+    return jnp.where(place < groups // 2, 2 * place, 2 * (groups - 1 - place) + 1)
+
+
+def slot_owners(groups):
+    _, core = chip_and_core()
+    sign = 2 * core - 1
+    owners = [owner_at(0, groups)]
+    for step in range(1, groups // 2):
+        owners += [owner_at(sign * step, groups), owner_at(-sign * step, groups)]
+    return owners + [owner_at(groups // 2, groups)]
+
+
+def join_halves(mine, theirs, joined):
+    _, core = chip_and_core()
+    rows = mine.shape[0]
+    joined[pl.ds(pl.multiple_of(core * rows, 16), rows), :] = mine[...]
+    joined[pl.ds(pl.multiple_of((1 - core) * rows, 16), rows), :] = theirs[...]
+
+
+def add_predictions(owners, hidden, weights, ids_of):
+    normed = layer_norm(hidden[...].astype(jnp.float32)).astype(jnp.bfloat16)
+    ids = token_values(owners, hidden.shape[0])
+    total = None
+    for weight, owner in zip(weights, ids_of):
+        picked = jnp.where(ids == owner, normed, jnp.zeros_like(normed))
+        part = lax.dot_general(
+            picked, weight[...], (((1,), (1,)), ((), ())), preferred_element_type=jnp.float32
+        )
+        total = part if total is None else total + part
+    return total
+
+
+def predict_body(groups, owners, hidden, *refs):
+    weights, prediction = refs[:-1], refs[-1]
+    prediction[...] = add_predictions(owners, hidden, weights, slot_owners(groups))
+
+
+def predict_last_body(groups, owners, hidden, earlier, mine, theirs, *refs):
+    weights, (prediction, joined) = refs[:-2], refs[-2:]
+    join_halves(mine, theirs, joined)
+    places = slot_owners(groups)[groups - 1 - len(weights) :]
+    prediction[...] = earlier[...] + add_predictions(
+        owners, hidden, (*weights, joined), places
+    )
+
+
+def finish_body(owners, mask, attended, returned, prediction, hidden, *refs):
+    weights, (targets, grad) = refs[:-2], refs[-2:]
+    chip, _ = chip_and_core()
+    width, rows = targets.shape
+    mine, theirs = attended[...], returned[...].astype(jnp.float32)
+    joined = jnp.concatenate(
+        [jnp.where(chip == 0, mine, theirs), jnp.where(chip == 0, theirs, mine)], axis=1
+    )
+    lane = lax.broadcasted_iota(jnp.int32, joined.shape, 1) >= HEAD
+    joined = jnp.where(lane, joined, 0.0)
+    mean = jnp.sum(joined, axis=1, keepdims=True) * (1.0 / width)
+    center = jnp.where(lane, joined - mean, 0.0)
+    variance = jnp.sum(center * center, axis=1, keepdims=True) * (1.0 / width)
+    found = (center * lax.rsqrt(variance + epsilon))[:, HEAD:].astype(jnp.bfloat16)
+    targets[...] = found.T
+    residual = (prediction[...] - found.astype(jnp.float32)).astype(jnp.bfloat16)
+    ids = token_values(owners, rows)
+    upstream = jnp.zeros(hidden.shape, jnp.float32)
+    for weight, owner in zip(weights, slot_owners(len(weights))):
+        picked = jnp.where(ids == owner, residual, jnp.zeros_like(residual))
+        upstream = upstream + jnp.dot(picked, weight[...], preferred_element_type=jnp.float32)
+    inputs = hidden[...].astype(jnp.float32)
+    back = norm_backward(upstream, layer_norm(inputs), inputs)
+    grad[...] = jnp.where(token_values(mask, rows) == 1, back, 0.0).astype(grad.dtype)
+
+
+def ring_pairs(members, groups):
+    order = list(range(0, groups, 2)) + list(range(groups - 1, 0, -2))
+    pairs = []
+    for member in range(members):
+        for i in range(groups):
+            a, b = order[i], order[(i + 1) % groups]
+            a, b = (a, b) if member % 2 == 0 else (b, a)
+            pairs.append((member * groups + a, member * groups + b))
+    return pairs
+
+
+def paired_shards(
+    tokens, target_kv, context_kv, query_weight, pred_hidden, pred_weight, target_mask, owners
+):
+    members = lax.axis_size("seq")
+    groups = lax.axis_size("grp")
+    across = [(i, (i + members // 2) % members) for i in range(members)]
+    beside = [(i, i ^ 1) for i in range(members)]
+    ring = ring_pairs(members, groups)
+    core = lax.rem(lax.axis_index("seq"), 2)
+    rows, width = tokens.shape[1], query_weight.shape[0]
+    features = tokens.shape[2]
+    half = features // 2
+    packed = 3 * LANES
+    out_rows, pred_size = pred_weight.shape[1:]
+    owner_row, mask_row = owners.reshape(1, -1), target_mask.reshape(1, -1)
+    sums_shape = shape_of((rows, 2 * packed), jnp.float32)
+
+    normed, keep, send = local_call(
+        norm_body,
+        [shape_of((rows, features)), shape_of((rows, half)), shape_of((rows, half))],
+        (tokens[0],),
+    )
+    kept_other = lax.ppermute(send, "seq", across)
+    new_kv = (
+        keep_rate * target_kv.astype(jnp.float32)
+        + (1.0 - keep_rate) * context_kv.astype(jnp.float32)
+    ).astype(jnp.bfloat16)
+    other_kv = lax.ppermute(new_kv, "seq", beside)
+    joined, own_sum, q_own, own_send, stored_kv = local_call(
+        first_partial_body,
+        [
+            shape_of((half, 2 * width)),
+            sums_shape,
+            shape_of((rows, packed)),
+            shape_of((rows, 3 * packed)),
+            shape_of(target_kv.shape),
+        ],
+        (new_kv, other_kv, keep, normed, query_weight),
+        out_specs=[VM] * 4 + [HBM],
+        scratch=[pltpu.SemaphoreType.DMA],
+        cost=matmul_cost(rows, half, 4 * width),
+    )
+    received = lax.ppermute(own_send, "seq", across)
+    other_sum, other_send = local_call(
+        partial_body,
+        [sums_shape, shape_of((rows, 2 * packed))],
+        (kept_other, joined),
+        cost=matmul_cost(rows, half, 2 * width),
+    )
+    from_other = lax.ppermute(other_send, "seq", across)
+    kv_a = (other_sum + received[:, : 2 * packed].astype(jnp.float32)).astype(jnp.bfloat16)
+    kv_a_beside = lax.ppermute(kv_a, "seq", beside)
+    all_sums = shape_of((6, rows, LANES), jnp.float32)
+    own_sums, other_sums = local_call(
+        attend_first_body,
+        [all_sums, all_sums],
+        (q_own, received, kv_a, kv_a_beside),
+        cost=matmul_cost(2 * rows, 12 * LANES, 2 * rows, 12 * rows * 2 * rows),
+    )
+    kv_b = (own_sum + from_other.astype(jnp.float32)).astype(jnp.bfloat16)
+    kv_b_beside = lax.ppermute(kv_b, "seq", beside)
+    attended, send_back = local_call(
+        attend_last_body,
+        [shape_of((rows, packed), jnp.float32), shape_of((rows, packed))],
+        (q_own, received, kv_b, kv_b_beside, own_sums, other_sums),
+        cost=matmul_cost(2 * rows, 12 * LANES, 2 * rows, 12 * rows * 2 * rows),
+    )
+    returned = lax.ppermute(send_back, "seq", across)
+
+    weights = [pred_weight[0]]
+    held = pred_weight[0]
+    for _ in range(1, groups // 2):
+        held = lax.ppermute(held, ("seq", "grp"), ring)
+        weights += [held, lax.ppermute(held, "seq", beside)]
+    half_rows = out_rows // 2
+    held = lax.dynamic_slice(held, (core * half_rows, 0), (half_rows, pred_size))
+    mine = lax.ppermute(held, ("seq", "grp"), ring)
+    theirs = lax.ppermute(mine, "seq", beside)
+    early = max(1, len(weights) - 2)
+    prediction = local_call(
+        functools.partial(predict_body, groups),
+        shape_of((rows, width), jnp.float32),
+        (owner_row, pred_hidden[0], *weights[:early]),
+        cost=matmul_cost(rows, early * pred_size, width),
+    )
+    prediction, opposite = local_call(
+        functools.partial(predict_last_body, groups),
+        [shape_of((rows, width), jnp.float32), shape_of((out_rows, pred_size))],
+        (owner_row, pred_hidden[0], prediction, mine, theirs, *weights[early:]),
+        cost=matmul_cost(rows, 3 * pred_size, width),
+    )
+    targets, grad = local_call(
+        finish_body,
+        [shape_of((width, rows)), shape_of((rows, pred_size))],
+        (
+            owner_row, mask_row, attended, returned, prediction, pred_hidden[0],
+            *weights, opposite,
+        ),
+        out_specs=[pl.BlockSpec(), pl.BlockSpec()],
+        cost=matmul_cost(rows, groups * pred_size, width),
+    )
+    return (stored_kv, targets.T[None], grad[None])
+
+
+def shards(*arguments):
+    pred_weight = arguments[5]
+    gathered = lax.axis_size("grp") * pred_weight.size * pred_weight.dtype.itemsize
+    two_chips = lax.axis_size("seq") == 4
+    if two_chips and lax.axis_size("grp") % 2 == 0 and gathered <= PAIR_BUDGET:
+        return paired_shards(*arguments)
+    return general_shards(*arguments)
+
+
 def solution(mesh):
     placed = (
         P("grp", "seq", None),

time: 124 us -> 53.5 us (0.43)
  waiting for transfers between devices: 59.6 us -> 20.7 us
  local copies, waits for them, and re-layouts: 16.5 us -> 2.89 us
  between operations: 14.3 us -> 0.82 us
  matrix products: 12.3 us -> 0 us
  Pallas kernels: 0 us -> 11.6 us
  other arithmetic: 5.98 us -> 1.94 us
    all_gather x2 -> x0, waiting for transfers between devices: 40 us -> none  [the longest x1 35.5 us: shards(): lax.all_gather(new_kv, 'seq', axis=0, tiled=True)]
    ppermute x0 -> x15, waiting for transfers between devices: none -> 20.7 us  [the longest x3 12.8 us: paired_shards(): held = lax.ppermute(held, ('seq', 'grp'), ring)]
    all_to_all x3 -> x0, waiting for transfers between devices: 19.5 us -> none  [the longest x1 6.78 us: shards(): lax.all_to_all(send_targets, 'grp', split_axis=0, concat_axis=0, tiled=True)]
    ppermute x0 -> x15, starting transfers between devices: none -> 15.4 us  [the longest x3 7.25 us: paired_shards(): held = lax.ppermute(held, ('seq', 'grp'), ring)]
    all_to_all x3 -> x0, starting transfers between devices: 14.4 us -> none  [the longest x1 5.52 us: shards(): lax.all_to_all(send_targets, 'grp', split_axis=0, concat_axis=0, tiled=True)]
    dot_general x8 -> x0, matrix products: 12.3 us -> none  [the longest x1 3.68 us: shards(): jnp.dot(normed, lax.all_gather(new_kv, 'seq', axis=0, tiled=True), prefer...]
    pallas_call x0 -> x8, Pallas kernels: none -> 11.6 us  [local_call(): pl.pallas_call(body, out_shape=outs, in_specs=specs or [VM] * len(operand...]
    slice x3 -> x0, local copies, waits for them, and re-layouts: 6.07 us -> none  [the longest x2 4.94 us: shards(): keys = key_values[:, :width].reshape(count, HEADS, HEAD)]
  transfers between devices with their start and end apart: 5 -> 15, of which waited for: 5 -> 8; matrix products, arithmetic and copies ran while one was open for 4% -> 4% of each run, Pallas kernels for 0% -> 18%
where the time goes in v2:
time: 53.5 us; the launch traced here: 53.3 us
  waiting for transfers between devices  20.7 us (39%)
  starting transfers between devices  15.4 us (29%)
  Pallas kernels  11.6 us (22%)
  local copies, waits for them, and re-layouts  2.89 us (5%)
  other arithmetic  1.94 us (4%)
  between operations  0.82 us (2%)
    ppermute x3, waiting for transfers between devices, paired_shards(): held = lax.ppermute(held, ('seq', 'grp'), ring)  12.8 us
    pallas_call x8, Pallas kernels, local_call(): pl.pallas_call(body, out_shape=outs, in_specs=specs or [VM] * len(operand...  11.6 us
    ppermute x3, starting transfers between devices, paired_shards(): held = lax.ppermute(held, ('seq', 'grp'), ring)  7.25 us
    unnamed x16, local copies, waits for them, and re-layouts  2.86 us
    ppermute x1, starting transfers between devices, paired_shards(): from_other = lax.ppermute(other_send, 'seq', across)  2.51 us
    ppermute x1, waiting for transfers between devices, paired_shards(): from_other = lax.ppermute(other_send, 'seq', across)  2.37 us
    convert_element_type x1, other arithmetic, paired_shards(): new_kv = (keep_rate * target_kv.astype(jnp.float32) + (1.0 - keep_rate) *...  1.86 us
    ppermute x1, waiting for transfers between devices, paired_shards(): kept_other = lax.ppermute(send, 'seq', across)  1.8 us
  transfers between devices with their start and end apart: 15, of which 8 were waited for; matrix products, arithmetic and copies ran while one was open for 4% of the time, Pallas kernels for 18%

profile of v2, /device:TPU:0, one launch (start us, length us, event | category | flops | bytes accessed | tf_op | source)
XLA Modules:
  0.0 53.3 jit_solution(3461904420394915004)
XLA Ops:
  0.7 3.1 %collective-permute-start.7 = (bf16[704,384]{1,0:T(8,128)(2,1)}, bf16[704,384]{1,0:T(8,128)(2,1)S(1)}, u32[]{:S(2)}, u32[]{:S(2)}) collective-permute-start(bf16[704,384]{1,0:T(8,128)(2,1)} %bitcast.8), channel_id=1, source_target_pairs={{0,2},{2,4},{4,6},{6,7},{7,5},{5,3},{3,1},{1,0},{10,8},{12,10},{14... | collective-permute-start | bytes 1622024 | tf_op jit(solution)/shard_map/ppermute | solution.py:443
  3.8 1.9 %add_convert_fusion.own_weight = bf16[352,1408]{1,0:T(8,128)(2,1)S(1)} fusion(bf16[352,1408]{1,0:T(8,128)(2,1)} %param.10, bf16[352,1408]{1,0:T(8,128)(2,1)} %param.9), kind=kLoop, calls=%fused_computation | loop fusion | flops 2973696 | bytes 2973696 | tf_op jit(solution)/shard_map/convert_element_type | solution.py:397
  5.7 5.6 %collective-permute-done.7.refs_1_ = bf16[704,384]{1,0:T(8,128)(2,1)S(1)} collective-permute-done((bf16[704,384]{1,0:T(8,128)(2,1)}, bf16[704,384]{1,0:T(8,128)(2,1)S(1)}, u32[]{:S(2)}, u32[]{:S(2)}) %collective-permute-start.7) | collective-permute-done | bytes 540704 | tf_op jit(solution)/shard_map/ppermute | solution.py:443
  11.2 2.1 %collective-permute-start.9 = (bf16[704,384]{1,0:T(8,128)(2,1)S(1)}, bf16[704,384]{1,0:T(8,128)(2,1)S(1)}, u32[]{:S(2)}, u32[]{:S(2)}) collective-permute-start(bf16[704,384]{1,0:T(8,128)(2,1)S(1)} %collective-permute-done.7.refs_1_), channel_id=1, source_target_pairs={{0,2},{2,4},{4,6},{6,7},{7,5},{5,3},{3,1},{1,0},{10,8},{12,10},{14... | collective-permute-start | bytes 1622024 | tf_op jit(solution)/shard_map/ppermute | solution.py:443
  13.3 7.3 %collective-permute-done.9.refs_3_ = bf16[704,384]{1,0:T(8,128)(2,1)S(1)} collective-permute-done((bf16[704,384]{1,0:T(8,128)(2,1)S(1)}, bf16[704,384]{1,0:T(8,128)(2,1)S(1)}, u32[]{:S(2)}, u32[]{:S(2)}) %collective-permute-start.9) | collective-permute-done | bytes 540704 | tf_op jit(solution)/shard_map/ppermute | solution.py:443
  20.6 2.1 %collective-permute-start.11 = (bf16[704,384]{1,0:T(8,128)(2,1)S(1)}, bf16[704,384]{1,0:T(8,128)(2,1)S(1)}, u32[]{:S(2)}, u32[]{:S(2)}) collective-permute-start(bf16[704,384]{1,0:T(8,128)(2,1)S(1)} %collective-permute-done.9.refs_3_), channel_id=1, source_target_pairs={{0,2},{2,4},{4,6},{6,7},{7,5},{5,3},{3,1},{1,0},{10,8},{12,10},{14... | collective-permute-start | bytes 1622024 | tf_op jit(solution)/shard_map/ppermute | solution.py:443
  23.2 1.6 %collective-permute-start.2 = (bf16[128,704]{1,0:T(8,128)(2,1)S(1)}, bf16[128,704]{1,0:T(8,128)(2,1)S(1)}, u32[]{:S(2)}, u32[]{:S(2)}) collective-permute-start(bf16[128,704]{1,0:T(8,128)(2,1)S(1)} %get-tuple-element.27), channel_id=1, source_target_pairs={{0,16},{8,24},{16,0},{24,8},{1,17},{9,25},{17,1},{25,9},{2,18},{10... | collective-permute-start | bytes 540680 | tf_op jit(solution)/shard_map/ppermute | solution.py:393
  24.7 1.7 %shard_map.104 = (bf16[704,1408]{1,0:T(8,128)(2,1)S(1)}, f32[128,768]{1,0:T(8,128)S(1)}, bf16[128,384]{1,0:T(8,128)(2,1)S(1)}, bf16[128,1152]{1,0:T(8,128)(2,1)S(1)}, bf16[352,1408]{1,0:T(8,128)(2,1)}) custom-call(bf16[352,1408]{1,0:T(8,128)(2,1)S(1)} %add_convert_fusion.own_weight, bf16[352,1408]{1,0:T(8,128)(2,1)S(1)} %collective-permute-done.other_weight, ...), custom_call_target="tpu_custom_call" | custom-call | flops 507510784 | bytes 3964928 | tf_op jit(solution)/shard_map/pallas_call | solution.py:146
  26.4 1.3 %copy-done.2 = bf16[704,1408]{1,0:T(8,128)(2,1)} copy-done((bf16[704,1408]{1,0:T(8,128)(2,1)}, bf16[704,1408]{1,0:T(8,128)(2,1)S(1)}, u32[]{:S(2)}) %copy-start.2) | copy-done | bytes 1982488
  27.7 0.5 %collective-permute-start.1 = (bf16[128,1152]{1,0:T(8,128)(2,1)S(1)}, bf16[128,1152]{1,0:T(8,128)(2,1)S(1)}, u32[]{:S(2)}, u32[]{:S(2)}) collective-permute-start(bf16[128,1152]{1,0:T(8,128)(2,1)S(1)} %get-tuple-element.25), channel_id=1, source_target_pairs={{0,16},{8,24},{16,0},{24,8},{1,17},{9,25},{17,1},{25,9},{2,18},{10... | collective-permute-start | bytes 884744 | tf_op jit(solution)/shard_map/ppermute | solution.py:413
  28.2 1.8 %collective-permute-done.2.rows = bf16[128,704]{1,0:T(8,128)(2,1)S(1)} collective-permute-done((bf16[128,704]{1,0:T(8,128)(2,1)S(1)}, bf16[128,704]{1,0:T(8,128)(2,1)S(1)}, u32[]{:S(2)}, u32[]{:S(2)}) %collective-permute-start.2) | collective-permute-done | bytes 180256 | tf_op jit(solution)/shard_map/ppermute | solution.py:393
  30.0 1.5 %copy-done.3 = bf16[704,1408]{1,0:T(8,128)(2,1)S(1)} copy-done((bf16[704,1408]{1,0:T(8,128)(2,1)S(1)}, bf16[704,1408]{1,0:T(8,128)(2,1)}, u32[]{:S(2)}) %copy-start.3) | copy-done | bytes 1982488
  32.1 2.5 %collective-permute-start.3 = (bf16[128,768]{1,0:T(8,128)(2,1)S(1)}, bf16[128,768]{1,0:T(8,128)(2,1)S(1)}, u32[]{:S(2)}, u32[]{:S(2)}) collective-permute-start(bf16[128,768]{1,0:T(8,128)(2,1)S(1)} %get-tuple-element.29), channel_id=1, source_target_pairs={{0,16},{8,24},{16,0},{24,8},{1,17},{9,25},{17,1},{25,9},{2,18},{10... | collective-permute-start | bytes 589832 | tf_op jit(solution)/shard_map/ppermute | solution.py:420
  34.6 1.5 %collective-permute-start.12 = (bf16[352,384]{1,0:T(8,128)(2,1)S(1)}, bf16[352,384]{1,0:T(8,128)(2,1)S(1)}, u32[]{:S(2)}, u32[]{:S(2)}) collective-permute-start(bf16[352,384]{1,0:T(8,128)(2,1)S(1)} %constant_dynamic-slice_fusion), channel_id=1, source_target_pairs={{0,2},{2,4},{4,6},{6,7},{7,5},{5,3},{3,1},{1,0},{10,8},{12,10},{14... | collective-permute-start | bytes 811016 | tf_op jit(solution)/shard_map/ppermute | solution.py:447
  36.2 0.8 %collective-permute-done.1.received = bf16[128,1152]{1,0:T(8,128)(2,1)S(1)} collective-permute-done((bf16[128,1152]{1,0:T(8,128)(2,1)S(1)}, bf16[128,1152]{1,0:T(8,128)(2,1)S(1)}, u32[]{:S(2)}, u32[]{:S(2)}) %collective-permute-start.1) | collective-permute-done | bytes 294944 | tf_op jit(solution)/shard_map/ppermute | solution.py:413
  37.1 2.4 %collective-permute-done.3 = bf16[128,768]{1,0:T(8,128)(2,1)S(1)} collective-permute-done((bf16[128,768]{1,0:T(8,128)(2,1)S(1)}, bf16[128,768]{1,0:T(8,128)(2,1)S(1)}, u32[]{:S(2)}, u32[]{:S(2)}) %collective-permute-start.3) | collective-permute-done | bytes 196640 | tf_op jit(solution)/shard_map/ppermute | solution.py:420
  39.5 1.4 %collective-permute-done.5.kv_b = bf16[128,768]{1,0:T(8,128)(2,1)S(1)} collective-permute-done((bf16[128,768]{1,0:T(8,128)(2,1)S(1)}, bf16[128,768]{1,0:T(8,128)(2,1)S(1)}, u32[]{:S(2)}, u32[]{:S(2)}) %collective-permute-start.5) | collective-permute-done | bytes 196640 | tf_op jit(solution)/shard_map/ppermute | solution.py:422
  41.4 2.3 %shard_map.106 = (f32[6,128,128]{2,1,0:T(8,128)S(1)}, f32[6,128,128]{2,1,0:T(8,128)S(1)}) custom-call(bf16[128,384]{1,0:T(8,128)(2,1)S(1)} %get-tuple-element.24.q_own, bf16[128,1152]{1,0:T(8,128)(2,1)S(1)} %collective-permute-done.1.received, bf16[128,768]{1,0:T(8,128)(2,1)S(1)} %add_convert_fusion.1.kv_a, bf16[128,768]{1,0:T(8,128)(2,1)S(1)} %collective-permute-done.5.kv_b), custom_call_target="tpu_custom_call" | custom-call | flops 201326592 | bytes 786432 | tf_op jit(solution)/shard_map/pallas_call | solution.py:146
  43.7 2.4 %shard_map.107 = (f32[128,384]{1,0:T(8,128)S(1)}, bf16[128,384]{1,0:T(8,128)(2,1)S(1)}) custom-call(bf16[128,384]{1,0:T(8,128)(2,1)S(1)} %get-tuple-element.24.q_own, bf16[128,1152]{1,0:T(8,128)(2,1)S(1)} %collective-permute-done.1.received, bf16[128,768]{1,0:T(8,128)(2,1)S(1)} %add_convert_fusion.2.kv_a, bf16[128,768]{1,0:T(8,128)(2,1)S(1)} %collective-permute-done.4.kv_b, ...), custom_call_target="tpu_custom_call" | custom-call | flops 201326592 | bytes 786432 | tf_op jit(solution)/shard_map/pallas_call | solution.py:146
  46.1 1.6 %collective-permute-start.6 = (bf16[128,384]{1,0:T(8,128)(2,1)S(1)}, bf16[128,384]{1,0:T(8,128)(2,1)S(1)}, u32[]{:S(2)}, u32[]{:S(2)}) collective-permute-start(bf16[128,384]{1,0:T(8,128)(2,1)S(1)} %get-tuple-element.34), channel_id=1, source_target_pairs={{0,16},{8,24},{16,0},{24,8},{1,17},{9,25},{17,1},{25,9},{2,18},{10... | collective-permute-start | bytes 294920 | tf_op jit(solution)/shard_map/ppermute | solution.py:438
  47.7 1.2 %shard_map.108.earlier = f32[128,704]{1,0:T(8,128)S(1)} custom-call(s32[1,64]{1,0:T(1,128)S(1)} %bitcast.15, bf16[128,384]{1,0:T(8,128)(2,1)S(1)} %bitcast.11, bf16[704,384]{1,0:T(8,128)(2,1)S(1)} %bitcast.9, bf16[704,384]{1,0:T(8,128)(2,1)S(1)} %collective-permute-done.7.refs_1_, bf16[704,384]{1,0:T(8,128)(2,1)S(1)} %collective-permute-done.8.refs_2_, ...), custom_call_target="tpu_custom_call" | custom-call | flops 346030080 | bytes 2703360 | tf_op jit(solution)/shard_map/pallas_call | solution.py:146
  49.0 0.9 %shard_map.109 = (f32[128,704]{1,0:T(8,128)S(1)}, bf16[704,384]{1,0:T(8,128)(2,1)S(1)}) custom-call(s32[1,64]{1,0:T(1,128)S(1)} %bitcast.16, bf16[128,384]{1,0:T(8,128)(2,1)S(1)} %bitcast.12, f32[128,704]{1,0:T(8,128)S(1)} %shard_map.108.earlier, bf16[352,384]{1,0:T(8,128)(2,1)S(1)} %collective-permute-done.12.mine, ...), custom_call_target="tpu_custom_call" | custom-call | flops 207618048 | bytes 1622016 | tf_op jit(solution)/shard_map/pallas_call | solution.py:146
  49.9 1.3 %collective-permute-done.6.returned = bf16[128,384]{1,0:T(8,128)(2,1)S(1)} collective-permute-done((bf16[128,384]{1,0:T(8,128)(2,1)S(1)}, bf16[128,384]{1,0:T(8,128)(2,1)S(1)}, u32[]{:S(2)}, u32[]{:S(2)}) %collective-permute-start.6) | collective-permute-done | bytes 98336 | tf_op jit(solution)/shard_map/ppermute | solution.py:438
  51.2 2.1 %shard_map.110 = (bf16[704,128]{1,0:T(8,128)(2,1)}, bf16[128,384]{1,0:T(8,128)(2,1)}) custom-call(s32[1,64]{1,0:T(1,128)S(1)} %bitcast.17, s32[1,64]{1,0:T(1,128)S(1)} %copy-done.7, f32[128,384]{1,0:T(8,128)S(1)} %get-tuple-element.33.attended, bf16[128,384]{1,0:T(8,128)(2,1)S(1)} %collective-permute-done.6.returned, ...), custom_call_target="tpu_custom_call" | custom-call | flops 553648128 | bytes 4325376 | tf_op jit(solution)/shard_map/pallas_call | solution.py:146
  (34 shorter events, 1.7 us)
Async XLA Ops:
  0.6 22.1 %copy-start.5 = (bf16[1,128,1408]{2,1,0:T(8,128)(2,1)S(1)}, bf16[1,128,1408]{2,1,0:T(8,128)(2,1)}, u32[]{:S(2)}) copy-start(bf16[1,128,1408]{2,1,0:T(8,128)(2,1)} %param.8) | copy-start | bytes 1081348
  0.6 24.1 %copy-start.1 = (bf16[704,1408]{1,0:T(8,128)(2,1)S(1)}, bf16[704,1408]{1,0:T(8,128)(2,1)}, u32[]{:S(2)}) copy-start(bf16[704,1408]{1,0:T(8,128)(2,1)} %query_weight.1) | copy-start | bytes 5947396
  0.7 10.6 %collective-permute-start.7 = (bf16[704,384]{1,0:T(8,128)(2,1)}, bf16[704,384]{1,0:T(8,128)(2,1)S(1)}, u32[]{:S(2)}, u32[]{:S(2)}) collective-permute-start(bf16[704,384]{1,0:T(8,128)(2,1)} %bitcast.8), channel_id=1, source_target_pairs={{0,2},{2,4},{4,6},{6,7},{7,5},{5,3},{3,1},{1,0},{10,8},{12,10},{14... | collective-permute-start | bytes 1622024 | tf_op jit(solution)/shard_map/ppermute | solution.py:443
  5.6 19.1 %collective-permute-start = (bf16[352,1408]{1,0:T(8,128)(2,1)S(1)}, bf16[352,1408]{1,0:T(8,128)(2,1)S(1)}, u32[]{:S(2)}, u32[]{:S(2)}) collective-permute-start(bf16[352,1408]{1,0:T(8,128)(2,1)S(1)} %add_convert_fusion.own_weight), channel_id=1, source_target_pairs={{0,8},{8,0},{16,24},{24,16},{1,9},{9,1},{17,25},{25,17},{2,10},{10... | collective-permute-start | bytes 2973704 | tf_op jit(solution)/shard_map/ppermute | solution.py:398
  11.2 9.4 %collective-permute-start.9 = (bf16[704,384]{1,0:T(8,128)(2,1)S(1)}, bf16[704,384]{1,0:T(8,128)(2,1)S(1)}, u32[]{:S(2)}, u32[]{:S(2)}) collective-permute-start(bf16[704,384]{1,0:T(8,128)(2,1)S(1)} %collective-permute-done.7.refs_1_), channel_id=1, source_target_pairs={{0,2},{2,4},{4,6},{6,7},{7,5},{5,3},{3,1},{1,0},{10,8},{12,10},{14... | collective-permute-start | bytes 1622024 | tf_op jit(solution)/shard_map/ppermute | solution.py:443
  20.6 14.0 %collective-permute-start.11 = (bf16[704,384]{1,0:T(8,128)(2,1)S(1)}, bf16[704,384]{1,0:T(8,128)(2,1)S(1)}, u32[]{:S(2)}, u32[]{:S(2)}) collective-permute-start(bf16[704,384]{1,0:T(8,128)(2,1)S(1)} %collective-permute-done.9.refs_3_), channel_id=1, source_target_pairs={{0,2},{2,4},{4,6},{6,7},{7,5},{5,3},{3,1},{1,0},{10,8},{12,10},{14... | collective-permute-start | bytes 1622024 | tf_op jit(solution)/shard_map/ppermute | solution.py:443
  23.2 6.8 %collective-permute-start.2 = (bf16[128,704]{1,0:T(8,128)(2,1)S(1)}, bf16[128,704]{1,0:T(8,128)(2,1)S(1)}, u32[]{:S(2)}, u32[]{:S(2)}) collective-permute-start(bf16[128,704]{1,0:T(8,128)(2,1)S(1)} %get-tuple-element.27), channel_id=1, source_target_pairs={{0,16},{8,24},{16,0},{24,8},{1,17},{9,25},{17,1},{25,9},{2,18},{10... | collective-permute-start | bytes 540680 | tf_op jit(solution)/shard_map/ppermute | solution.py:393
  26.4 1.3 %copy-start.2 = (bf16[704,1408]{1,0:T(8,128)(2,1)}, bf16[704,1408]{1,0:T(8,128)(2,1)S(1)}, u32[]{:S(2)}) copy-start(bf16[704,1408]{1,0:T(8,128)(2,1)S(1)} %get-tuple-element.28.weight) | copy-start | bytes 5947396
  27.7 9.3 %collective-permute-start.1 = (bf16[128,1152]{1,0:T(8,128)(2,1)S(1)}, bf16[128,1152]{1,0:T(8,128)(2,1)S(1)}, u32[]{:S(2)}, u32[]{:S(2)}) collective-permute-start(bf16[128,1152]{1,0:T(8,128)(2,1)S(1)} %get-tuple-element.25), channel_id=1, source_target_pairs={{0,16},{8,24},{16,0},{24,8},{1,17},{9,25},{17,1},{25,9},{2,18},{10... | collective-permute-start | bytes 884744 | tf_op jit(solution)/shard_map/ppermute | solution.py:413
  28.2 19.5 %collective-permute-start.8 = (bf16[704,384]{1,0:T(8,128)(2,1)S(1)}, bf16[704,384]{1,0:T(8,128)(2,1)S(1)}, u32[]{:S(2)}, u32[]{:S(2)}) collective-permute-start(bf16[704,384]{1,0:T(8,128)(2,1)S(1)} %collective-permute-done.7.refs_1_), channel_id=1, source_target_pairs={{0,8},{8,0},{16,24},{24,16},{1,9},{9,1},{17,25},{25,17},{2,10},{10... | collective-permute-start | bytes 1622024 | tf_op jit(solution)/shard_map/ppermute | solution.py:444
  30.0 1.6 %copy-start.3 = (bf16[704,1408]{1,0:T(8,128)(2,1)S(1)}, bf16[704,1408]{1,0:T(8,128)(2,1)}, u32[]{:S(2)}) copy-start(bf16[704,1408]{1,0:T(8,128)(2,1)} %copy-done.2) | copy-start | bytes 5947396
  32.1 7.4 %collective-permute-start.3 = (bf16[128,768]{1,0:T(8,128)(2,1)S(1)}, bf16[128,768]{1,0:T(8,128)(2,1)S(1)}, u32[]{:S(2)}, u32[]{:S(2)}) collective-permute-start(bf16[128,768]{1,0:T(8,128)(2,1)S(1)} %get-tuple-element.29), channel_id=1, source_target_pairs={{0,16},{8,24},{16,0},{24,8},{1,17},{9,25},{17,1},{25,9},{2,18},{10... | collective-permute-start | bytes 589832 | tf_op jit(solution)/shard_map/ppermute | solution.py:420
  34.6 13.1 %collective-permute-start.10 = (bf16[704,384]{1,0:T(8,128)(2,1)S(1)}, bf16[704,384]{1,0:T(8,128)(2,1)S(1)}, u32[]{:S(2)}, u32[]{:S(2)}) collective-permute-start(bf16[704,384]{1,0:T(8,128)(2,1)S(1)} %collective-permute-done.9.refs_3_), channel_id=1, source_target_pairs={{0,8},{8,0},{16,24},{24,16},{1,9},{9,1},{17,25},{25,17},{2,10},{10... | collective-permute-start | bytes 1622024 | tf_op jit(solution)/shard_map/ppermute | solution.py:444
  34.6 13.1 %copy-start = (bf16[1,704,384]{2,1,0:T(8,128)(2,1)S(1)}, bf16[1,704,384]{2,1,0:T(8,128)(2,1)}, u32[]{:S(2)}) copy-start(bf16[1,704,384]{2,1,0:T(8,128)(2,1)} %param.13) | copy-start | bytes 1622020
  34.6 13.1 %copy-start.4 = (bf16[1,128,384]{2,1,0:T(8,128)(2,1)S(1)}, bf16[1,128,384]{2,1,0:T(8,128)(2,1)}, u32[]{:S(2)}) copy-start(bf16[1,128,384]{2,1,0:T(8,128)(2,1)} %param.12) | copy-start | bytes 294916
  34.6 13.1 %copy-start.6 = (s32[1,64,1]{1,2,0:T(1,128)S(1)}, s32[1,64,1]{1,2,0:T(1,128)}, u32[]{:S(2)}) copy-start(s32[1,64,1]{1,2,0:T(1,128)} %param.15) | copy-start | bytes 772
  34.6 6.5 %collective-permute-start.12 = (bf16[352,384]{1,0:T(8,128)(2,1)S(1)}, bf16[352,384]{1,0:T(8,128)(2,1)S(1)}, u32[]{:S(2)}, u32[]{:S(2)}) collective-permute-start(bf16[352,384]{1,0:T(8,128)(2,1)S(1)} %constant_dynamic-slice_fusion), channel_id=1, source_target_pairs={{0,2},{2,4},{4,6},{6,7},{7,5},{5,3},{3,1},{1,0},{10,8},{12,10},{14... | collective-permute-start | bytes 811016 | tf_op jit(solution)/shard_map/ppermute | solution.py:447
  37.0 12.0 %collective-permute-start.14 = (bf16[704,384]{1,0:T(8,128)(2,1)S(1)}, bf16[704,384]{1,0:T(8,128)(2,1)S(1)}, u32[]{:S(2)}, u32[]{:S(2)}) collective-permute-start(bf16[704,384]{1,0:T(8,128)(2,1)S(1)} %collective-permute-done.11.refs_0_.refs_5_), channel_id=1, source_target_pairs={{0,8},{8,0},{16,24},{24,16},{1,9},{9,1},{17,25},{25,17},{2,10},{10... | collective-permute-start | bytes 1622024 | tf_op jit(solution)/shard_map/ppermute | solution.py:444
  39.4 1.4 %collective-permute-start.5 = (bf16[128,768]{1,0:T(8,128)(2,1)S(1)}, bf16[128,768]{1,0:T(8,128)(2,1)S(1)}, u32[]{:S(2)}, u32[]{:S(2)}) collective-permute-start(bf16[128,768]{1,0:T(8,128)(2,1)S(1)} %add_convert_fusion.1.kv_a), channel_id=1, source_target_pairs={{0,8},{8,0},{16,24},{24,16},{1,9},{9,1},{17,25},{25,17},{2,10},{10... | collective-permute-start | bytes 589832 | tf_op jit(solution)/shard_map/ppermute | solution.py:422
  40.9 2.8 %collective-permute-start.4 = (bf16[128,768]{1,0:T(8,128)(2,1)S(1)}, bf16[128,768]{1,0:T(8,128)(2,1)S(1)}, u32[]{:S(2)}, u32[]{:S(2)}) collective-permute-start(bf16[128,768]{1,0:T(8,128)(2,1)S(1)} %add_convert_fusion.2.kv_a), channel_id=1, source_target_pairs={{0,8},{8,0},{16,24},{24,16},{1,9},{9,1},{17,25},{25,17},{2,10},{10... | collective-permute-start | bytes 589832 | tf_op jit(solution)/shard_map/ppermute | solution.py:431
  41.2 7.8 %collective-permute-start.13 = (bf16[352,384]{1,0:T(8,128)(2,1)S(1)}, bf16[352,384]{1,0:T(8,128)(2,1)S(1)}, u32[]{:S(2)}, u32[]{:S(2)}) collective-permute-start(bf16[352,384]{1,0:T(8,128)(2,1)S(1)} %collective-permute-done.12.mine), channel_id=1, source_target_pairs={{0,8},{8,0},{16,24},{24,16},{1,9},{9,1},{17,25},{25,17},{2,10},{10... | collective-permute-start | bytes 811016 | tf_op jit(solution)/shard_map/ppermute | solution.py:448
  46.1 5.0 %collective-permute-start.6 = (bf16[128,384]{1,0:T(8,128)(2,1)S(1)}, bf16[128,384]{1,0:T(8,128)(2,1)S(1)}, u32[]{:S(2)}, u32[]{:S(2)}) collective-permute-start(bf16[128,384]{1,0:T(8,128)(2,1)S(1)} %get-tuple-element.34), channel_id=1, source_target_pairs={{0,16},{8,24},{16,0},{24,8},{1,17},{9,25},{17,1},{25,9},{2,18},{10... | collective-permute-start | bytes 294920 | tf_op jit(solution)/shard_map/ppermute | solution.py:438
  47.7 3.5 %copy-start.7 = (s32[1,64]{1,0:T(1,128)S(1)}, s32[1,64]{1,0:T(1,128)}, u32[]{:S(2)}) copy-start(s32[1,64]{1,0:T(1,128)} %mask.1) | copy-start | bytes 772

commit v3 on v2

--- a/solution.py
+++ b/solution.py
@@ -202,15 +202,26 @@
         other[:, t * LANES : (t + 1) * LANES] = theirs[t].astype(jnp.bfloat16)
 
 
+def blend(target, context):
+    return (
+        keep_rate * target[...].astype(jnp.float32)
+        + (1.0 - keep_rate) * context[...].astype(jnp.float32)
+    ).astype(jnp.bfloat16)
+
+
 def first_partial_body(
-    own_weight, other_weight, rows, normed, query_weight, joined, own, q_own, send, stored, sem
+    target, context, other_target, other_context, rows, normed, query_weight,
+    joined, own, q_own, send, stored, sem,
 ):
     chip, core = chip_and_core()
-    depth = own_weight.shape[0]
-    store = pltpu.make_async_copy(own_weight, stored, sem)
+    depth = target.shape[0]
+    own_rows = pl.ds(pl.multiple_of(core * depth, 16), depth)
+    joined[own_rows, :] = blend(target, context)
+    store = pltpu.make_async_copy(joined.at[own_rows], stored, sem)
     store.start()
-    joined[pl.ds(pl.multiple_of(core * depth, 16), depth), :] = own_weight[...]
-    joined[pl.ds(pl.multiple_of((1 - core) * depth, 16), depth), :] = other_weight[...]
+    joined[pl.ds(pl.multiple_of((1 - core) * depth, 16), depth), :] = blend(
+        other_target, other_context
+    )
     split_product(rows, joined, own, send)
     queries = lax.dot_general(
         normed[...], query_weight[...], (((1,), (1,)), ((), ())), preferred_element_type=jnp.float32
@@ -253,24 +264,17 @@
     return total
 
 
-def attend_first_body(q_own, received, kv_a, kv_b, own_sums, other_sums):
-    q_other = received[:, 6 * LANES :]
+def attend_body(queries, kv_a, kv_b, mine, theirs):
+    upper_lane = lax.broadcasted_iota(jnp.int32, (1, LANES), 1) >= HEAD
+    rows = mine.shape[0]
+    found = [None] * 6
     for slot in range(6):
-        own_sums[slot] = add_keys(q_own, (kv_a, kv_b), slot)
-        other_sums[slot] = add_keys(q_other, (kv_a, kv_b), slot)
-
-
-def attend_last_body(q_own, received, kv_a, kv_b, own_sums, other_sums, mine, theirs):
-    upper_lane = lax.broadcasted_iota(jnp.int32, (1, LANES), 1) >= HEAD
-    q_other = received[:, 6 * LANES :]
-    for queries, sums, out in ((q_other, other_sums, theirs), (q_own, own_sums, mine)):
-        found = [None] * 6
-        for slot in range(6):
-            total = sums[slot] + add_keys(queries, (kv_a, kv_b), slot)
-            found[(slot + 1) % 6] = total / pltpu.roll(total, HEAD, 1)
-        for t in range(3):
-            joined = jnp.where(upper_lane, found[2 * t + 1], found[2 * t])
-            out[:, t * LANES : (t + 1) * LANES] = joined.astype(out.dtype)
+        total = add_keys(queries, (kv_a, kv_b), slot)
+        found[(slot + 1) % 6] = total / pltpu.roll(total, HEAD, 1)
+    for t in range(3):
+        joined = jnp.where(upper_lane, found[2 * t + 1], found[2 * t])
+        mine[:, t * LANES : (t + 1) * LANES] = joined[:rows]
+        theirs[:, t * LANES : (t + 1) * LANES] = joined[rows:].astype(theirs.dtype)
 
 
 def token_values(pairs, rows):
@@ -322,16 +326,34 @@
     prediction[...] = add_predictions(owners, hidden, weights, slot_owners(groups))
 
 
-def predict_last_body(groups, owners, hidden, earlier, mine, theirs, *refs):
+def predict_rest_body(groups, owners, hidden, earlier, mine, theirs, *refs):
     weights, (prediction, joined) = refs[:-2], refs[-2:]
     join_halves(mine, theirs, joined)
     places = slot_owners(groups)[groups - 1 - len(weights) :]
-    prediction[...] = earlier[...] + add_predictions(
-        owners, hidden, (*weights, joined), places
-    )
-
-
-def finish_body(owners, mask, attended, returned, prediction, hidden, *refs):
+    prediction[...] = earlier[...] + add_predictions(owners, hidden, (*weights, joined), places)
+
+
+def cut_body(whole, first, second):
+    _, core = chip_and_core()
+    rows = first.shape[0]
+    first[...] = whole[pl.ds(pl.multiple_of(core * rows, 16), rows), :]
+    second[...] = whole[pl.ds(pl.multiple_of((1 - core) * rows, 16), rows), :]
+
+
+def join_body(first, second, joined):
+    join_halves(first, second, joined)
+
+
+def add_upstream(residual, ids, weights, ids_of):
+    total = None
+    for weight, owner in zip(weights, ids_of):
+        picked = jnp.where(ids == owner, residual, jnp.zeros_like(residual))
+        part = jnp.dot(picked, weight[...], preferred_element_type=jnp.float32)
+        total = part if total is None else total + part
+    return total
+
+
+def finish_body(groups, owners, mask, attended, returned, prediction, hidden, *refs):
     weights, (targets, grad) = refs[:-2], refs[-2:]
     chip, _ = chip_and_core()
     width, rows = targets.shape
@@ -348,10 +370,7 @@
     targets[...] = found.T
     residual = (prediction[...] - found.astype(jnp.float32)).astype(jnp.bfloat16)
     ids = token_values(owners, rows)
-    upstream = jnp.zeros(hidden.shape, jnp.float32)
-    for weight, owner in zip(weights, slot_owners(len(weights))):
-        picked = jnp.where(ids == owner, residual, jnp.zeros_like(residual))
-        upstream = upstream + jnp.dot(picked, weight[...], preferred_element_type=jnp.float32)
+    upstream = add_upstream(residual, ids, weights, slot_owners(groups))
     inputs = hidden[...].astype(jnp.float32)
     back = norm_backward(upstream, layer_norm(inputs), inputs)
     grad[...] = jnp.where(token_values(mask, rows) == 1, back, 0.0).astype(grad.dtype)
@@ -376,7 +395,6 @@
     across = [(i, (i + members // 2) % members) for i in range(members)]
     beside = [(i, i ^ 1) for i in range(members)]
     ring = ring_pairs(members, groups)
-    core = lax.rem(lax.axis_index("seq"), 2)
     rows, width = tokens.shape[1], query_weight.shape[0]
     features = tokens.shape[2]
     half = features // 2
@@ -385,17 +403,15 @@
     owner_row, mask_row = owners.reshape(1, -1), target_mask.reshape(1, -1)
     sums_shape = shape_of((rows, 2 * packed), jnp.float32)
 
+    other_target = lax.ppermute(target_kv, "seq", beside)
+    other_context = lax.ppermute(context_kv, "seq", beside)
     normed, keep, send = local_call(
         norm_body,
         [shape_of((rows, features)), shape_of((rows, half)), shape_of((rows, half))],
         (tokens[0],),
+        cost=pl.CostEstimate(flops=1 << 33, bytes_accessed=1 << 20, transcendentals=0),
     )
     kept_other = lax.ppermute(send, "seq", across)
-    new_kv = (
-        keep_rate * target_kv.astype(jnp.float32)
-        + (1.0 - keep_rate) * context_kv.astype(jnp.float32)
-    ).astype(jnp.bfloat16)
-    other_kv = lax.ppermute(new_kv, "seq", beside)
     joined, own_sum, q_own, own_send, stored_kv = local_call(
         first_partial_body,
         [
@@ -405,7 +421,7 @@
             shape_of((rows, 3 * packed)),
             shape_of(target_kv.shape),
         ],
-        (new_kv, other_kv, keep, normed, query_weight),
+        (target_kv, context_kv, other_target, other_context, keep, normed, query_weight),
         out_specs=[VM] * 4 + [HBM],
         scratch=[pltpu.SemaphoreType.DMA],
         cost=matmul_cost(rows, half, 4 * width),
@@ -418,33 +434,40 @@
         cost=matmul_cost(rows, half, 2 * width),
     )
     from_other = lax.ppermute(other_send, "seq", across)
-    kv_a = (other_sum + received[:, : 2 * packed].astype(jnp.float32)).astype(jnp.bfloat16)
-    kv_a_beside = lax.ppermute(kv_a, "seq", beside)
-    all_sums = shape_of((6, rows, LANES), jnp.float32)
-    own_sums, other_sums = local_call(
-        attend_first_body,
-        [all_sums, all_sums],
-        (q_own, received, kv_a, kv_a_beside),
-        cost=matmul_cost(2 * rows, 12 * LANES, 2 * rows, 12 * rows * 2 * rows),
-    )
-    kv_b = (own_sum + from_other.astype(jnp.float32)).astype(jnp.bfloat16)
-    kv_b_beside = lax.ppermute(kv_b, "seq", beside)
+    kv = jnp.concatenate(
+        [
+            (other_sum + received[:, : 2 * packed].astype(jnp.float32)).astype(jnp.bfloat16),
+            (own_sum + from_other.astype(jnp.float32)).astype(jnp.bfloat16),
+        ],
+        axis=0,
+    )
+    kv_beside = lax.ppermute(kv, "seq", beside)
+    queries = jnp.concatenate([q_own, received[:, 2 * packed :]], axis=0)
     attended, send_back = local_call(
-        attend_last_body,
+        attend_body,
         [shape_of((rows, packed), jnp.float32), shape_of((rows, packed))],
-        (q_own, received, kv_b, kv_b_beside, own_sums, other_sums),
-        cost=matmul_cost(2 * rows, 12 * LANES, 2 * rows, 12 * rows * 2 * rows),
+        (queries, kv, kv_beside),
+        cost=matmul_cost(2 * rows, 12 * LANES, 4 * rows, 12 * rows * 4 * rows),
     )
     returned = lax.ppermute(send_back, "seq", across)
 
+    half_rows = out_rows // 2
+    half_shape, whole_shape = shape_of((half_rows, pred_size)), shape_of((out_rows, pred_size))
+    halves = [half_shape, half_shape]
     weights = [pred_weight[0]]
-    held = pred_weight[0]
-    for _ in range(1, groups // 2):
-        held = lax.ppermute(held, ("seq", "grp"), ring)
+    last_step = groups // 2
+    for step in range(1, last_step):
+        if step == 1:
+            held = lax.ppermute(pred_weight[0], ("seq", "grp"), ring)
+            first, second = local_call(cut_body, halves, (held,))
+        else:
+            first = lax.ppermute(first, ("seq", "grp"), ring)
+            second = lax.ppermute(second, ("seq", "grp"), ring)
+            held = local_call(join_body, whole_shape, (first, second))
         weights += [held, lax.ppermute(held, "seq", beside)]
-    half_rows = out_rows // 2
-    held = lax.dynamic_slice(held, (core * half_rows, 0), (half_rows, pred_size))
-    mine = lax.ppermute(held, ("seq", "grp"), ring)
+    if last_step == 1:
+        first, second = local_call(cut_body, halves, (pred_weight[0],))
+    mine = lax.ppermute(first, ("seq", "grp"), ring)
     theirs = lax.ppermute(mine, "seq", beside)
     early = max(1, len(weights) - 2)
     prediction = local_call(
@@ -454,18 +477,16 @@
         cost=matmul_cost(rows, early * pred_size, width),
     )
     prediction, opposite = local_call(
-        functools.partial(predict_last_body, groups),
-        [shape_of((rows, width), jnp.float32), shape_of((out_rows, pred_size))],
+        functools.partial(predict_rest_body, groups),
+        [shape_of((rows, width), jnp.float32), whole_shape],
         (owner_row, pred_hidden[0], prediction, mine, theirs, *weights[early:]),
-        cost=matmul_cost(rows, 3 * pred_size, width),
-    )
+        cost=matmul_cost(rows, (groups - early) * pred_size, width),
+    )
+    weights.append(opposite)
     targets, grad = local_call(
-        finish_body,
+        functools.partial(finish_body, groups),
         [shape_of((width, rows)), shape_of((rows, pred_size))],
-        (
-            owner_row, mask_row, attended, returned, prediction, pred_hidden[0],
-            *weights, opposite,
-        ),
+        (owner_row, mask_row, attended, returned, prediction, pred_hidden[0], *weights),
         out_specs=[pl.BlockSpec(), pl.BlockSpec()],
         cost=matmul_cost(rows, groups * pred_size, width),
     )

time: 53.5 us -> 49 us (0.916)
  Pallas kernels: 11.6 us -> 9.14 us
  starting transfers between devices: 15.4 us -> 17.5 us
  local copies, waits for them, and re-layouts: 2.89 us -> 1.03 us
  other arithmetic: 1.94 us -> 0.12 us
    ppermute x7 -> x9, waiting for transfers between devices: 14.4 us -> 11 us  [the longest x1 6.98 us: paired_shards(): held = lax.ppermute(pred_weight[0], ('seq', 'grp'), ring)]
    ppermute x7 -> x9, starting transfers between devices: 8.99 us -> 11.7 us  [the longest x2 3.98 us: paired_shards(): first = lax.ppermute(first, ('seq', 'grp'), ring)]
    ppermute x1, waiting for transfers between devices: 2.37 us -> 4.91 us  [paired_shards(): from_other = lax.ppermute(other_send, 'seq', across)]
    pallas_call x8 -> x10, Pallas kernels: 11.6 us -> 9.14 us  [local_call(): pl.pallas_call(body, out_shape=outs, in_specs=specs or [VM] * len(operand...]
    ppermute x1, waiting for transfers between devices: 0.84 us -> 2.74 us  [paired_shards(): received = lax.ppermute(own_send, 'seq', across)]
    convert_element_type x2 -> x1, other arithmetic: 1.89 us -> 0.03 us  [paired_shards(): (own_sum + from_other.astype(jnp.float32)).astype(jnp.bfloat16)]
    unnamed x16, local copies, waits for them, and re-layouts: 2.86 us -> 1.02 us
    ppermute x1, waiting for transfers between devices: 1.8 us -> 0.01 us  [paired_shards(): kept_other = lax.ppermute(send, 'seq', across)]
  transfers between devices with their start and end apart: 15 -> 17, of which waited for: 8 -> 6; matrix products, arithmetic and copies ran while one was open for 4% -> 0% of each run, Pallas kernels for 18% -> 14%
where the time goes in v3:
time: 49 us; the launch traced here: 48.9 us
  waiting for transfers between devices  20.2 us (41%)
  starting transfers between devices  17.5 us (36%)
  Pallas kernels  9.14 us (19%)
  local copies, waits for them, and re-layouts  1.03 us (2%)
  between operations  0.84 us (2%)
    pallas_call x10, Pallas kernels, local_call(): pl.pallas_call(body, out_shape=outs, in_specs=specs or [VM] * len(operand...  9.14 us
    ppermute x1, waiting for transfers between devices, paired_shards(): held = lax.ppermute(pred_weight[0], ('seq', 'grp'), ring)  6.98 us
    ppermute x1, waiting for transfers between devices, paired_shards(): from_other = lax.ppermute(other_send, 'seq', across)  4.91 us
    ppermute x2, starting transfers between devices, paired_shards(): first = lax.ppermute(first, ('seq', 'grp'), ring)  3.98 us
    ppermute x2, starting transfers between devices, paired_shards(): second = lax.ppermute(second, ('seq', 'grp'), ring)  3.65 us
    ppermute x1, waiting for transfers between devices, paired_shards(): mine = lax.ppermute(first, ('seq', 'grp'), ring)  3.15 us
    ppermute x1, starting transfers between devices, paired_shards(): held = lax.ppermute(pred_weight[0], ('seq', 'grp'), ring)  3.1 us
    ppermute x1, waiting for transfers between devices, paired_shards(): received = lax.ppermute(own_send, 'seq', across)  2.74 us
  transfers between devices with their start and end apart: 17, of which 6 were waited for; matrix products, arithmetic and copies ran while one was open for 0% of the time, Pallas kernels for 14%

profile of v3, /device:TPU:0, one launch (start us, length us, event | category | flops | bytes accessed | tf_op | source)
XLA Modules:
  0.0 48.9 jit_solution(9549877881982222654)
XLA Ops:
  0.6 3.1 %collective-permute-start.7 = (bf16[704,384]{1,0:T(8,128)(2,1)}, bf16[704,384]{1,0:T(8,128)(2,1)S(1)}, u32[]{:S(2)}, u32[]{:S(2)}) collective-permute-start(bf16[704,384]{1,0:T(8,128)(2,1)} %bitcast.8), channel_id=1, source_target_pairs={{0,2},{2,4},{4,6},{6,7},{7,5},{5,3},{3,1},{1,0},{10,8},{12,10},{14... | collective-permute-start | bytes 1622024 | tf_op jit(solution)/shard_map/ppermute | solution.py:461
  3.7 0.5 %collective-permute-start.1 = (bf16[352,1408]{1,0:T(8,128)(2,1)}, bf16[352,1408]{1,0:T(8,128)(2,1)S(1)}, u32[]{:S(2)}, u32[]{:S(2)}) collective-permute-start(bf16[352,1408]{1,0:T(8,128)(2,1)} %context.1), channel_id=1, source_target_pairs={{0,8},{8,0},{16,24},{24,16},{1,9},{9,1},{17,25},{25,17},{2,10},{10... | collective-permute-start | bytes 2973704 | tf_op jit(solution)/shard_map/ppermute | solution.py:407
  4.2 7.0 %collective-permute-done.7.whole.refs_1_ = bf16[704,384]{1,0:T(8,128)(2,1)S(1)} collective-permute-done((bf16[704,384]{1,0:T(8,128)(2,1)}, bf16[704,384]{1,0:T(8,128)(2,1)S(1)}, u32[]{:S(2)}, u32[]{:S(2)}) %collective-permute-start.7) | collective-permute-done | bytes 540704 | tf_op jit(solution)/shard_map/ppermute | solution.py:461
  11.3 2.1 %collective-permute-start.9 = (bf16[352,384]{1,0:T(8,128)(2,1)S(1)}, bf16[352,384]{1,0:T(8,128)(2,1)S(1)}, u32[]{:S(2)}, u32[]{:S(2)}) collective-permute-start(bf16[352,384]{1,0:T(8,128)(2,1)S(1)} %get-tuple-element.33), channel_id=1, source_target_pairs={{0,2},{2,4},{4,6},{6,7},{7,5},{5,3},{3,1},{1,0},{10,8},{12,10},{14... | collective-permute-start | bytes 811016 | tf_op jit(solution)/shard_map/ppermute | solution.py:464
  13.4 1.6 %collective-permute-start.10 = (bf16[352,384]{1,0:T(8,128)(2,1)S(1)}, bf16[352,384]{1,0:T(8,128)(2,1)S(1)}, u32[]{:S(2)}, u32[]{:S(2)}) collective-permute-start(bf16[352,384]{1,0:T(8,128)(2,1)S(1)} %get-tuple-element.34), channel_id=1, source_target_pairs={{0,2},{2,4},{4,6},{6,7},{7,5},{5,3},{3,1},{1,0},{10,8},{12,10},{14... | collective-permute-start | bytes 811016 | tf_op jit(solution)/shard_map/ppermute | solution.py:465
  15.0 1.0 %copy-done.7 = bf16[1,128,1408]{2,1,0:T(8,128)(2,1)S(1)} copy-done((bf16[1,128,1408]{2,1,0:T(8,128)(2,1)S(1)}, bf16[1,128,1408]{2,1,0:T(8,128)(2,1)}, u32[]{:S(2)}) %copy-start.7) | copy-done | bytes 360472
  16.5 1.6 %collective-permute-start.3 = (bf16[128,704]{1,0:T(8,128)(2,1)S(1)}, bf16[128,704]{1,0:T(8,128)(2,1)S(1)}, u32[]{:S(2)}, u32[]{:S(2)}) collective-permute-start(bf16[128,704]{1,0:T(8,128)(2,1)S(1)} %get-tuple-element.26), channel_id=1, source_target_pairs={{0,16},{8,24},{16,0},{24,8},{1,17},{9,25},{17,1},{25,9},{2,18},{10... | collective-permute-start | bytes 540680 | tf_op jit(solution)/shard_map/ppermute | solution.py:414
  18.0 1.8 %collective-permute-start.12 = (bf16[352,384]{1,0:T(8,128)(2,1)S(1)}, bf16[352,384]{1,0:T(8,128)(2,1)S(1)}, u32[]{:S(2)}, u32[]{:S(2)}) collective-permute-start(bf16[352,384]{1,0:T(8,128)(2,1)S(1)} %collective-permute-done.9.first), channel_id=1, source_target_pairs={{0,2},{2,4},{4,6},{6,7},{7,5},{5,3},{3,1},{1,0},{10,8},{12,10},{14... | collective-permute-start | bytes 811016 | tf_op jit(solution)/shard_map/ppermute | solution.py:464
  19.9 0.8 %collective-permute-done.10.second = bf16[352,384]{1,0:T(8,128)(2,1)S(1)} collective-permute-done((bf16[352,384]{1,0:T(8,128)(2,1)S(1)}, bf16[352,384]{1,0:T(8,128)(2,1)S(1)}, u32[]{:S(2)}, u32[]{:S(2)}) %collective-permute-start.10) | collective-permute-done | bytes 270368 | tf_op jit(solution)/shard_map/ppermute | solution.py:465
  20.7 2.1 %collective-permute-start.15 = (bf16[352,384]{1,0:T(8,128)(2,1)S(1)}, bf16[352,384]{1,0:T(8,128)(2,1)S(1)}, u32[]{:S(2)}, u32[]{:S(2)}) collective-permute-start(bf16[352,384]{1,0:T(8,128)(2,1)S(1)} %collective-permute-done.10.second), channel_id=1, source_target_pairs={{0,2},{2,4},{4,6},{6,7},{7,5},{5,3},{3,1},{1,0},{10,8},{12,10},{14... | collective-permute-start | bytes 811016 | tf_op jit(solution)/shard_map/ppermute | solution.py:465
  22.8 2.2 %shard_map.104 = (bf16[704,1408]{1,0:T(8,128)(2,1)S(1)}, f32[128,768]{1,0:T(8,128)S(1)}, bf16[128,384]{1,0:T(8,128)(2,1)S(1)}, bf16[128,1152]{1,0:T(8,128)(2,1)S(1)}, bf16[352,1408]{1,0:T(8,128)(2,1)}) custom-call(bf16[352,1408]{1,0:T(8,128)(2,1)S(1)} %copy-done.2, bf16[352,1408]{1,0:T(8,128)(2,1)S(1)} %copy-done.3, ...), custom_call_target="tpu_custom_call" | custom-call | flops 507510784 | bytes 3964928 | tf_op jit(solution)/shard_map/pallas_call | solution.py:146
  25.0 0.5 %shard_map.105 = (f32[128,768]{1,0:T(8,128)S(1)}, bf16[128,768]{1,0:T(8,128)(2,1)S(1)}) custom-call(bf16[128,704]{1,0:T(8,128)(2,1)S(1)} %collective-permute-done.3.rows, bf16[704,1408]{1,0:T(8,128)(2,1)S(1)} %get-tuple-element.27.weight), custom_call_target="tpu_custom_call" | custom-call | flops 253755392 | bytes 1982464 | tf_op jit(solution)/shard_map/pallas_call | solution.py:146
  25.5 1.6 %collective-permute-start.4 = (bf16[128,768]{1,0:T(8,128)(2,1)S(1)}, bf16[128,768]{1,0:T(8,128)(2,1)S(1)}, u32[]{:S(2)}, u32[]{:S(2)}) collective-permute-start(bf16[128,768]{1,0:T(8,128)(2,1)S(1)} %get-tuple-element.30), channel_id=1, source_target_pairs={{0,16},{8,24},{16,0},{24,8},{1,17},{9,25},{17,1},{25,9},{2,18},{10... | collective-permute-start | bytes 589832 | tf_op jit(solution)/shard_map/ppermute | solution.py:436
  27.1 0.5 %collective-permute-start.2 = (bf16[128,1152]{1,0:T(8,128)(2,1)S(1)}, bf16[128,1152]{1,0:T(8,128)(2,1)S(1)}, u32[]{:S(2)}, u32[]{:S(2)}) collective-permute-start(bf16[128,1152]{1,0:T(8,128)(2,1)S(1)} %get-tuple-element.25), channel_id=1, source_target_pairs={{0,16},{8,24},{16,0},{24,8},{1,17},{9,25},{17,1},{25,9},{2,18},{10... | collective-permute-start | bytes 884744 | tf_op jit(solution)/shard_map/ppermute | solution.py:429
  27.7 0.6 %collective-permute-start.11 = (bf16[704,384]{1,0:T(8,128)(2,1)S(1)}, bf16[704,384]{1,0:T(8,128)(2,1)S(1)}, u32[]{:S(2)}, u32[]{:S(2)}) collective-permute-start(bf16[704,384]{1,0:T(8,128)(2,1)S(1)} %shard_map.108.refs_3_), channel_id=1, source_target_pairs={{0,8},{8,0},{16,24},{24,16},{1,9},{9,1},{17,25},{25,17},{2,10},{10... | collective-permute-start | bytes 1622024 | tf_op jit(solution)/shard_map/ppermute | solution.py:467
  28.4 4.9 %collective-permute-done.4 = bf16[128,768]{1,0:T(8,128)(2,1)S(1)} collective-permute-done((bf16[128,768]{1,0:T(8,128)(2,1)S(1)}, bf16[128,768]{1,0:T(8,128)(2,1)S(1)}, u32[]{:S(2)}, u32[]{:S(2)}) %collective-permute-start.4) | collective-permute-done | bytes 196640 | tf_op jit(solution)/shard_map/ppermute | solution.py:436
  33.8 2.7 %collective-permute-done.2 = bf16[128,1152]{1,0:T(8,128)(2,1)S(1)} collective-permute-done((bf16[128,1152]{1,0:T(8,128)(2,1)S(1)}, bf16[128,1152]{1,0:T(8,128)(2,1)S(1)}, u32[]{:S(2)}, u32[]{:S(2)}) %collective-permute-start.2) | collective-permute-done | bytes 294944 | tf_op jit(solution)/shard_map/ppermute | solution.py:429
  36.7 3.1 %collective-permute-done.13.mine = bf16[352,384]{1,0:T(8,128)(2,1)S(1)} collective-permute-done((bf16[352,384]{1,0:T(8,128)(2,1)S(1)}, bf16[352,384]{1,0:T(8,128)(2,1)S(1)}, u32[]{:S(2)}, u32[]{:S(2)}) %collective-permute-start.13) | collective-permute-done | bytes 270368 | tf_op jit(solution)/shard_map/ppermute | solution.py:470
  39.9 1.6 %shard_map.106 = (f32[128,384]{1,0:T(8,128)S(1)}, bf16[128,384]{1,0:T(8,128)(2,1)S(1)}) custom-call(bf16[256,384]{1,0:T(8,128)(2,1)S(1)} %pad_maximum_fusion.1.queries, bf16[256,768]{1,0:T(8,128)(2,1)S(1)} %pad_maximum_fusion.kv_a, bf16[256,768]{1,0:T(8,128)(2,1)S(1)} %collective-permute-done.5.kv_b), custom_call_target="tpu_custom_call" | custom-call | flops 402653184 | bytes 1572864 | tf_op jit(solution)/shard_map/pallas_call | solution.py:146
  41.5 1.6 %collective-permute-start.6 = (bf16[128,384]{1,0:T(8,128)(2,1)S(1)}, bf16[128,384]{1,0:T(8,128)(2,1)S(1)}, u32[]{:S(2)}, u32[]{:S(2)}) collective-permute-start(bf16[128,384]{1,0:T(8,128)(2,1)S(1)} %get-tuple-element.32), channel_id=1, source_target_pairs={{0,16},{8,24},{16,0},{24,8},{1,17},{9,25},{17,1},{25,9},{2,18},{10... | collective-permute-start | bytes 294920 | tf_op jit(solution)/shard_map/ppermute | solution.py:452
  43.1 1.2 %shard_map.109.earlier = f32[128,704]{1,0:T(8,128)S(1)} custom-call(s32[1,64]{1,0:T(1,128)S(1)} %bitcast.14, bf16[128,384]{1,0:T(8,128)(2,1)S(1)} %bitcast.11, bf16[704,384]{1,0:T(8,128)(2,1)S(1)} %bitcast.9, bf16[704,384]{1,0:T(8,128)(2,1)S(1)} %collective-permute-done.7.whole.refs_1_, bf16[704,384]{1,0:T(8,128)(2,1)S(1)} %collective-permute-done.8.refs_2_, ...), custom_call_target="tpu_custom_call" | custom-call | flops 346030080 | bytes 2703360 | tf_op jit(solution)/shard_map/pallas_call | solution.py:146
  44.3 0.9 %shard_map.111 = (f32[128,704]{1,0:T(8,128)S(1)}, bf16[704,384]{1,0:T(8,128)(2,1)S(1)}) custom-call(s32[1,64]{1,0:T(1,128)S(1)} %bitcast.15, bf16[128,384]{1,0:T(8,128)(2,1)S(1)} %bitcast.12, f32[128,704]{1,0:T(8,128)S(1)} %shard_map.109.earlier, bf16[352,384]{1,0:T(8,128)(2,1)S(1)} %collective-permute-done.13.mine, ...), custom_call_target="tpu_custom_call" | custom-call | flops 207618048 | bytes 1622016 | tf_op jit(solution)/shard_map/pallas_call | solution.py:146
  45.2 1.6 %collective-permute-done.6.returned = bf16[128,384]{1,0:T(8,128)(2,1)S(1)} collective-permute-done((bf16[128,384]{1,0:T(8,128)(2,1)S(1)}, bf16[128,384]{1,0:T(8,128)(2,1)S(1)}, u32[]{:S(2)}, u32[]{:S(2)}) %collective-permute-start.6) | collective-permute-done | bytes 98336 | tf_op jit(solution)/shard_map/ppermute | solution.py:452
  46.8 2.1 %shard_map.112 = (bf16[704,128]{1,0:T(8,128)(2,1)}, bf16[128,384]{1,0:T(8,128)(2,1)}) custom-call(s32[1,64]{1,0:T(1,128)S(1)} %bitcast.16, s32[1,64]{1,0:T(1,128)S(1)} %copy-done.6, f32[128,384]{1,0:T(8,128)S(1)} %get-tuple-element.31.attended, bf16[128,384]{1,0:T(8,128)(2,1)S(1)} %collective-permute-done.6.returned, ...), custom_call_target="tpu_custom_call" | custom-call | flops 553648128 | bytes 4325376 | tf_op jit(solution)/shard_map/pallas_call | solution.py:146
  (41 shorter events, 1.4 us)
Async XLA Ops:
  0.6 10.6 %collective-permute-start.7 = (bf16[704,384]{1,0:T(8,128)(2,1)}, bf16[704,384]{1,0:T(8,128)(2,1)S(1)}, u32[]{:S(2)}, u32[]{:S(2)}) collective-permute-start(bf16[704,384]{1,0:T(8,128)(2,1)} %bitcast.8), channel_id=1, source_target_pairs={{0,2},{2,4},{4,6},{6,7},{7,5},{5,3},{3,1},{1,0},{10,8},{12,10},{14... | collective-permute-start | bytes 1622024 | tf_op jit(solution)/shard_map/ppermute | solution.py:461
  3.7 19.0 %collective-permute-start = (bf16[352,1408]{1,0:T(8,128)(2,1)}, bf16[352,1408]{1,0:T(8,128)(2,1)S(1)}, u32[]{:S(2)}, u32[]{:S(2)}) collective-permute-start(bf16[352,1408]{1,0:T(8,128)(2,1)} %target.1), channel_id=1, source_target_pairs={{0,8},{8,0},{16,24},{24,16},{1,9},{9,1},{17,25},{25,17},{2,10},{10... | collective-permute-start | bytes 2973704 | tf_op jit(solution)/shard_map/ppermute | solution.py:406
  3.7 19.0 %collective-permute-start.1 = (bf16[352,1408]{1,0:T(8,128)(2,1)}, bf16[352,1408]{1,0:T(8,128)(2,1)S(1)}, u32[]{:S(2)}, u32[]{:S(2)}) collective-permute-start(bf16[352,1408]{1,0:T(8,128)(2,1)} %context.1), channel_id=1, source_target_pairs={{0,8},{8,0},{16,24},{24,16},{1,9},{9,1},{17,25},{25,17},{2,10},{10... | collective-permute-start | bytes 2973704 | tf_op jit(solution)/shard_map/ppermute | solution.py:407
  11.3 6.7 %collective-permute-start.9 = (bf16[352,384]{1,0:T(8,128)(2,1)S(1)}, bf16[352,384]{1,0:T(8,128)(2,1)S(1)}, u32[]{:S(2)}, u32[]{:S(2)}) collective-permute-start(bf16[352,384]{1,0:T(8,128)(2,1)S(1)} %get-tuple-element.33), channel_id=1, source_target_pairs={{0,2},{2,4},{4,6},{6,7},{7,5},{5,3},{3,1},{1,0},{10,8},{12,10},{14... | collective-permute-start | bytes 811016 | tf_op jit(solution)/shard_map/ppermute | solution.py:464
  13.4 7.3 %collective-permute-start.10 = (bf16[352,384]{1,0:T(8,128)(2,1)S(1)}, bf16[352,384]{1,0:T(8,128)(2,1)S(1)}, u32[]{:S(2)}, u32[]{:S(2)}) collective-permute-start(bf16[352,384]{1,0:T(8,128)(2,1)S(1)} %get-tuple-element.34), channel_id=1, source_target_pairs={{0,2},{2,4},{4,6},{6,7},{7,5},{5,3},{3,1},{1,0},{10,8},{12,10},{14... | collective-permute-start | bytes 811016 | tf_op jit(solution)/shard_map/ppermute | solution.py:465
  16.0 6.8 %copy-start.1 = (bf16[704,1408]{1,0:T(8,128)(2,1)S(1)}, bf16[704,1408]{1,0:T(8,128)(2,1)}, u32[]{:S(2)}) copy-start(bf16[704,1408]{1,0:T(8,128)(2,1)} %query_weight.1) | copy-start | bytes 5947396
  16.0 6.8 %copy-start.2 = (bf16[352,1408]{1,0:T(8,128)(2,1)S(1)}, bf16[352,1408]{1,0:T(8,128)(2,1)}, u32[]{:S(2)}) copy-start(bf16[352,1408]{1,0:T(8,128)(2,1)} %target.1) | copy-start | bytes 2973700
  16.0 6.8 %copy-start.3 = (bf16[352,1408]{1,0:T(8,128)(2,1)S(1)}, bf16[352,1408]{1,0:T(8,128)(2,1)}, u32[]{:S(2)}) copy-start(bf16[352,1408]{1,0:T(8,128)(2,1)} %context.1) | copy-start | bytes 2973700
  16.5 8.6 %collective-permute-start.3 = (bf16[128,704]{1,0:T(8,128)(2,1)S(1)}, bf16[128,704]{1,0:T(8,128)(2,1)S(1)}, u32[]{:S(2)}, u32[]{:S(2)}) collective-permute-start(bf16[128,704]{1,0:T(8,128)(2,1)S(1)} %get-tuple-element.26), channel_id=1, source_target_pairs={{0,16},{8,24},{16,0},{24,8},{1,17},{9,25},{17,1},{25,9},{2,18},{10... | collective-permute-start | bytes 540680 | tf_op jit(solution)/shard_map/ppermute | solution.py:414
  18.0 9.7 %collective-permute-start.12 = (bf16[352,384]{1,0:T(8,128)(2,1)S(1)}, bf16[352,384]{1,0:T(8,128)(2,1)S(1)}, u32[]{:S(2)}, u32[]{:S(2)}) collective-permute-start(bf16[352,384]{1,0:T(8,128)(2,1)S(1)} %collective-permute-done.9.first), channel_id=1, source_target_pairs={{0,2},{2,4},{4,6},{6,7},{7,5},{5,3},{3,1},{1,0},{10,8},{12,10},{14... | collective-permute-start | bytes 811016 | tf_op jit(solution)/shard_map/ppermute | solution.py:464
  20.7 7.6 %collective-permute-start.15 = (bf16[352,384]{1,0:T(8,128)(2,1)S(1)}, bf16[352,384]{1,0:T(8,128)(2,1)S(1)}, u32[]{:S(2)}, u32[]{:S(2)}) collective-permute-start(bf16[352,384]{1,0:T(8,128)(2,1)S(1)} %collective-permute-done.10.second), channel_id=1, source_target_pairs={{0,2},{2,4},{4,6},{6,7},{7,5},{5,3},{3,1},{1,0},{10,8},{12,10},{14... | collective-permute-start | bytes 811016 | tf_op jit(solution)/shard_map/ppermute | solution.py:465
  25.5 7.8 %collective-permute-start.4 = (bf16[128,768]{1,0:T(8,128)(2,1)S(1)}, bf16[128,768]{1,0:T(8,128)(2,1)S(1)}, u32[]{:S(2)}, u32[]{:S(2)}) collective-permute-start(bf16[128,768]{1,0:T(8,128)(2,1)S(1)} %get-tuple-element.30), channel_id=1, source_target_pairs={{0,16},{8,24},{16,0},{24,8},{1,17},{9,25},{17,1},{25,9},{2,18},{10... | collective-permute-start | bytes 589832 | tf_op jit(solution)/shard_map/ppermute | solution.py:436
  27.1 9.4 %collective-permute-start.2 = (bf16[128,1152]{1,0:T(8,128)(2,1)S(1)}, bf16[128,1152]{1,0:T(8,128)(2,1)S(1)}, u32[]{:S(2)}, u32[]{:S(2)}) collective-permute-start(bf16[128,1152]{1,0:T(8,128)(2,1)S(1)} %get-tuple-element.25), channel_id=1, source_target_pairs={{0,16},{8,24},{16,0},{24,8},{1,17},{9,25},{17,1},{25,9},{2,18},{10... | collective-permute-start | bytes 884744 | tf_op jit(solution)/shard_map/ppermute | solution.py:429
  27.6 15.4 %collective-permute-start.8 = (bf16[704,384]{1,0:T(8,128)(2,1)S(1)}, bf16[704,384]{1,0:T(8,128)(2,1)S(1)}, u32[]{:S(2)}, u32[]{:S(2)}) collective-permute-start(bf16[704,384]{1,0:T(8,128)(2,1)S(1)} %collective-permute-done.7.whole.refs_1_), channel_id=1, source_target_pairs={{0,8},{8,0},{16,24},{24,16},{1,9},{9,1},{17,25},{25,17},{2,10},{10... | collective-permute-start | bytes 1622024 | tf_op jit(solution)/shard_map/ppermute | solution.py:467
  27.7 15.3 %collective-permute-start.11 = (bf16[704,384]{1,0:T(8,128)(2,1)S(1)}, bf16[704,384]{1,0:T(8,128)(2,1)S(1)}, u32[]{:S(2)}, u32[]{:S(2)}) collective-permute-start(bf16[704,384]{1,0:T(8,128)(2,1)S(1)} %shard_map.108.refs_3_), channel_id=1, source_target_pairs={{0,8},{8,0},{16,24},{24,16},{1,9},{9,1},{17,25},{25,17},{2,10},{10... | collective-permute-start | bytes 1622024 | tf_op jit(solution)/shard_map/ppermute | solution.py:467
  28.3 15.9 %collective-permute-start.16 = (bf16[704,384]{1,0:T(8,128)(2,1)S(1)}, bf16[704,384]{1,0:T(8,128)(2,1)S(1)}, u32[]{:S(2)}, u32[]{:S(2)}) collective-permute-start(bf16[704,384]{1,0:T(8,128)(2,1)S(1)} %shard_map.110.refs_0_.refs_5_), channel_id=1, source_target_pairs={{0,8},{8,0},{16,24},{24,16},{1,9},{9,1},{17,25},{25,17},{2,10},{10... | collective-permute-start | bytes 1622024 | tf_op jit(solution)/shard_map/ppermute | solution.py:467
  33.4 6.5 %collective-permute-start.13 = (bf16[352,384]{1,0:T(8,128)(2,1)S(1)}, bf16[352,384]{1,0:T(8,128)(2,1)S(1)}, u32[]{:S(2)}, u32[]{:S(2)}) collective-permute-start(bf16[352,384]{1,0:T(8,128)(2,1)S(1)} %collective-permute-done.12.first), channel_id=1, source_target_pairs={{0,2},{2,4},{4,6},{6,7},{7,5},{5,3},{3,1},{1,0},{10,8},{12,10},{14... | collective-permute-start | bytes 811016 | tf_op jit(solution)/shard_map/ppermute | solution.py:470
  33.7 9.3 %copy-start = (bf16[1,704,384]{2,1,0:T(8,128)(2,1)S(1)}, bf16[1,704,384]{2,1,0:T(8,128)(2,1)}, u32[]{:S(2)}) copy-start(bf16[1,704,384]{2,1,0:T(8,128)(2,1)} %param.13) | copy-start | bytes 1622020
  33.8 9.3 %copy-start.4 = (bf16[1,128,384]{2,1,0:T(8,128)(2,1)S(1)}, bf16[1,128,384]{2,1,0:T(8,128)(2,1)}, u32[]{:S(2)}) copy-start(bf16[1,128,384]{2,1,0:T(8,128)(2,1)} %param.12) | copy-start | bytes 294916
  33.8 9.3 %copy-start.5 = (s32[1,64,1]{1,2,0:T(1,128)S(1)}, s32[1,64,1]{1,2,0:T(1,128)}, u32[]{:S(2)}) copy-start(s32[1,64,1]{1,2,0:T(1,128)} %param.15) | copy-start | bytes 772
  36.6 3.3 %collective-permute-start.5 = (bf16[256,768]{1,0:T(8,128)(2,1)S(1)}, bf16[256,768]{1,0:T(8,128)(2,1)S(1)}, u32[]{:S(2)}, u32[]{:S(2)}) collective-permute-start(bf16[256,768]{1,0:T(8,128)(2,1)S(1)} %pad_maximum_fusion.kv_a), channel_id=1, source_target_pairs={{0,8},{8,0},{16,24},{24,16},{1,9},{9,1},{17,25},{25,17},{2,10},{10... | collective-permute-start | bytes 1179656 | tf_op jit(solution)/shard_map/ppermute | solution.py:444
  39.8 4.5 %collective-permute-start.14 = (bf16[352,384]{1,0:T(8,128)(2,1)S(1)}, bf16[352,384]{1,0:T(8,128)(2,1)S(1)}, u32[]{:S(2)}, u32[]{:S(2)}) collective-permute-start(bf16[352,384]{1,0:T(8,128)(2,1)S(1)} %collective-permute-done.13.mine), channel_id=1, source_target_pairs={{0,8},{8,0},{16,24},{24,16},{1,9},{9,1},{17,25},{25,17},{2,10},{10... | collective-permute-start | bytes 811016 | tf_op jit(solution)/shard_map/ppermute | solution.py:471
  41.5 5.3 %collective-permute-start.6 = (bf16[128,384]{1,0:T(8,128)(2,1)S(1)}, bf16[128,384]{1,0:T(8,128)(2,1)S(1)}, u32[]{:S(2)}, u32[]{:S(2)}) collective-permute-start(bf16[128,384]{1,0:T(8,128)(2,1)S(1)} %get-tuple-element.32), channel_id=1, source_target_pairs={{0,16},{8,24},{16,0},{24,8},{1,17},{9,25},{17,1},{25,9},{2,18},{10... | collective-permute-start | bytes 294920 | tf_op jit(solution)/shard_map/ppermute | solution.py:452
  43.1 3.7 %copy-start.6 = (s32[1,64]{1,0:T(1,128)S(1)}, s32[1,64]{1,0:T(1,128)}, u32[]{:S(2)}) copy-start(s32[1,64]{1,0:T(1,128)} %mask.1) | copy-start | bytes 772
  (1 other events, 1.0 us)

commit v4 on v3

--- a/solution.py
+++ b/solution.py
@@ -241,6 +241,14 @@
     split_product(rows, weight, own, other)
 
 
+def kv_body(own_sum, other_sum, from_other, received, q_own, kv, queries):
+    rows, width = own_sum.shape
+    kv[:rows, :] = (other_sum[...] + received[:, :width].astype(jnp.float32)).astype(kv.dtype)
+    kv[rows:, :] = (own_sum[...] + from_other[...].astype(jnp.float32)).astype(kv.dtype)
+    queries[:rows, :] = q_own[...]
+    queries[rows:, :] = received[:, width:]
+
+
 def add_keys(queries, kv_refs, slot):
     upper_lane = lax.broadcasted_iota(jnp.int32, (1, LANES), 1) >= HEAD
     tile, upper = slot // 2, slot % 2
@@ -277,12 +285,14 @@
         theirs[:, t * LANES : (t + 1) * LANES] = joined[rows:].astype(theirs.dtype)
 
 
-def token_values(pairs, rows):
-    shape = (rows, pairs.shape[1])
-    token = lax.broadcasted_iota(jnp.int32, shape, 0) // 2
-    pair = lax.broadcasted_iota(jnp.int32, shape, 1)
-    values = jnp.where(token == pair, pairs[...], 0)
-    return jnp.sum(values, axis=1, keepdims=True)
+def match_body(match):
+    token = lax.broadcasted_iota(jnp.int32, match.shape, 0) // 2
+    pair = lax.broadcasted_iota(jnp.int32, match.shape, 1)
+    match[...] = (token == pair).astype(match.dtype)
+
+
+def token_values(match, pairs):
+    return jnp.sum(match[...] * pairs[...], axis=1, keepdims=True)
 
 
 def owner_at(moved, groups):
@@ -308,9 +318,9 @@
     joined[pl.ds(pl.multiple_of((1 - core) * rows, 16), rows), :] = theirs[...]
 
 
-def add_predictions(owners, hidden, weights, ids_of):
+def add_predictions(match, owners, hidden, weights, ids_of):
     normed = layer_norm(hidden[...].astype(jnp.float32)).astype(jnp.bfloat16)
-    ids = token_values(owners, hidden.shape[0])
+    ids = token_values(match, owners)
     total = None
     for weight, owner in zip(weights, ids_of):
         picked = jnp.where(ids == owner, normed, jnp.zeros_like(normed))
@@ -321,16 +331,18 @@
     return total
 
 
-def predict_body(groups, owners, hidden, *refs):
+def predict_body(groups, match, owners, hidden, *refs):
     weights, prediction = refs[:-1], refs[-1]
-    prediction[...] = add_predictions(owners, hidden, weights, slot_owners(groups))
-
-
-def predict_rest_body(groups, owners, hidden, earlier, mine, theirs, *refs):
+    prediction[...] = add_predictions(match, owners, hidden, weights, slot_owners(groups))
+
+
+def predict_rest_body(groups, match, owners, hidden, earlier, mine, theirs, *refs):
     weights, (prediction, joined) = refs[:-2], refs[-2:]
     join_halves(mine, theirs, joined)
     places = slot_owners(groups)[groups - 1 - len(weights) :]
-    prediction[...] = earlier[...] + add_predictions(owners, hidden, (*weights, joined), places)
+    prediction[...] = earlier[...] + add_predictions(
+        match, owners, hidden, (*weights, joined), places
+    )
 
 
 def cut_body(whole, first, second):
@@ -353,10 +365,10 @@
     return total
 
 
-def finish_body(groups, owners, mask, attended, returned, prediction, hidden, *refs):
+def finish_body(groups, match, owners, mask, attended, returned, prediction, hidden, *refs):
     weights, (targets, grad) = refs[:-2], refs[-2:]
     chip, _ = chip_and_core()
-    width, rows = targets.shape
+    width, _ = targets.shape
     mine, theirs = attended[...], returned[...].astype(jnp.float32)
     joined = jnp.concatenate(
         [jnp.where(chip == 0, mine, theirs), jnp.where(chip == 0, theirs, mine)], axis=1
@@ -369,11 +381,11 @@
     found = (center * lax.rsqrt(variance + epsilon))[:, HEAD:].astype(jnp.bfloat16)
     targets[...] = found.T
     residual = (prediction[...] - found.astype(jnp.float32)).astype(jnp.bfloat16)
-    ids = token_values(owners, rows)
+    ids = token_values(match, owners)
     upstream = add_upstream(residual, ids, weights, slot_owners(groups))
     inputs = hidden[...].astype(jnp.float32)
     back = norm_backward(upstream, layer_norm(inputs), inputs)
-    grad[...] = jnp.where(token_values(mask, rows) == 1, back, 0.0).astype(grad.dtype)
+    grad[...] = jnp.where(token_values(match, mask) == 1, back, 0.0).astype(grad.dtype)
 
 
 def ring_pairs(members, groups):
@@ -403,6 +415,11 @@
     owner_row, mask_row = owners.reshape(1, -1), target_mask.reshape(1, -1)
     sums_shape = shape_of((rows, 2 * packed), jnp.float32)
 
+    match = local_call(
+        match_body,
+        shape_of((rows, owner_row.shape[1]), jnp.int32),
+        (),
+    )
     other_target = lax.ppermute(target_kv, "seq", beside)
     other_context = lax.ppermute(context_kv, "seq", beside)
     normed, keep, send = local_call(
@@ -434,15 +451,12 @@
         cost=matmul_cost(rows, half, 2 * width),
     )
     from_other = lax.ppermute(other_send, "seq", across)
-    kv = jnp.concatenate(
-        [
-            (other_sum + received[:, : 2 * packed].astype(jnp.float32)).astype(jnp.bfloat16),
-            (own_sum + from_other.astype(jnp.float32)).astype(jnp.bfloat16),
-        ],
-        axis=0,
+    kv, queries = local_call(
+        kv_body,
+        [shape_of((2 * rows, 2 * packed)), shape_of((2 * rows, packed))],
+        (own_sum, other_sum, from_other, received, q_own),
     )
     kv_beside = lax.ppermute(kv, "seq", beside)
-    queries = jnp.concatenate([q_own, received[:, 2 * packed :]], axis=0)
     attended, send_back = local_call(
         attend_body,
         [shape_of((rows, packed), jnp.float32), shape_of((rows, packed))],
@@ -469,24 +483,26 @@
         first, second = local_call(cut_body, halves, (pred_weight[0],))
     mine = lax.ppermute(first, ("seq", "grp"), ring)
     theirs = lax.ppermute(mine, "seq", beside)
-    early = max(1, len(weights) - 2)
+    early = groups - 3 if groups > 4 else 1
     prediction = local_call(
         functools.partial(predict_body, groups),
         shape_of((rows, width), jnp.float32),
-        (owner_row, pred_hidden[0], *weights[:early]),
+        (match, owner_row, pred_hidden[0], *weights[:early]),
         cost=matmul_cost(rows, early * pred_size, width),
     )
     prediction, opposite = local_call(
         functools.partial(predict_rest_body, groups),
         [shape_of((rows, width), jnp.float32), whole_shape],
-        (owner_row, pred_hidden[0], prediction, mine, theirs, *weights[early:]),
+        (match, owner_row, pred_hidden[0], prediction, mine, theirs, *weights[early:]),
         cost=matmul_cost(rows, (groups - early) * pred_size, width),
     )
     weights.append(opposite)
     targets, grad = local_call(
         functools.partial(finish_body, groups),
         [shape_of((width, rows)), shape_of((rows, pred_size))],
-        (owner_row, mask_row, attended, returned, prediction, pred_hidden[0], *weights),
+        (
+            match, owner_row, mask_row, attended, returned, prediction, pred_hidden[0], *weights
+        ),
         out_specs=[pl.BlockSpec(), pl.BlockSpec()],
         cost=matmul_cost(rows, groups * pred_size, width),
     )

time: 49 us -> 47.3 us (0.965)
  waiting for transfers between devices: 20.2 us -> 16.7 us
  starting transfers between devices: 17.5 us -> 19.3 us
    ppermute x1, waiting for transfers between devices: 3.15 us -> 0.01 us  [paired_shards(): mine = lax.ppermute(first, ('seq', 'grp'), ring)]
    ppermute x1, waiting for transfers between devices: 2.74 us -> 0.01 us  [paired_shards(): received = lax.ppermute(own_send, 'seq', across)]
    ppermute x1, waiting for transfers between devices: 0.01 us -> 1.75 us  [paired_shards(): kv_beside = lax.ppermute(kv, 'seq', beside)]
    ppermute x1, starting transfers between devices: 0.35 us -> 1.58 us  [paired_shards(): mine = lax.ppermute(first, ('seq', 'grp'), ring)]
    ppermute x1, waiting for transfers between devices: 4.91 us -> 5.98 us  [paired_shards(): from_other = lax.ppermute(other_send, 'seq', across)]
    ppermute x1, starting transfers between devices: 0.53 us -> 1.55 us  [paired_shards(): received = lax.ppermute(own_send, 'seq', across)]
    ppermute x1, starting transfers between devices: 1.56 us -> 0.59 us  [paired_shards(): from_other = lax.ppermute(other_send, 'seq', across)]
    ppermute x1, starting transfers between devices: 0.07 us -> 0.57 us  [paired_shards(): kv_beside = lax.ppermute(kv, 'seq', beside)]
  transfers between devices with their start and end apart: 17 -> 17, of which waited for: 6 -> 5; matrix products, arithmetic and copies ran while one was open for 0% -> 0% of each run, Pallas kernels for 14% -> 15%
where the time goes in v4:
time: 47.3 us; the launch traced here: 47.2 us
  starting transfers between devices  19.3 us (41%)
  waiting for transfers between devices  16.7 us (35%)
  Pallas kernels  9.29 us (20%)
  local copies, waits for them, and re-layouts  1.02 us (2%)
  between operations  0.82 us (2%)
    pallas_call x12, Pallas kernels, local_call(): pl.pallas_call(body, out_shape=outs, in_specs=specs or [VM] * len(operand...  9.29 us
    ppermute x1, waiting for transfers between devices, paired_shards(): held = lax.ppermute(pred_weight[0], ('seq', 'grp'), ring)  6.98 us
    ppermute x1, waiting for transfers between devices, paired_shards(): from_other = lax.ppermute(other_send, 'seq', across)  5.98 us
    ppermute x2, starting transfers between devices, paired_shards(): first = lax.ppermute(first, ('seq', 'grp'), ring)  3.98 us
    ppermute x2, starting transfers between devices, paired_shards(): second = lax.ppermute(second, ('seq', 'grp'), ring)  3.65 us
    ppermute x1, starting transfers between devices, paired_shards(): held = lax.ppermute(pred_weight[0], ('seq', 'grp'), ring)  3.1 us
    ppermute x1, waiting for transfers between devices, paired_shards(): kv_beside = lax.ppermute(kv, 'seq', beside)  1.75 us
    ppermute x1, starting transfers between devices, paired_shards(): mine = lax.ppermute(first, ('seq', 'grp'), ring)  1.58 us
  transfers between devices with their start and end apart: 17, of which 5 were waited for; matrix products, arithmetic and copies ran while one was open for 0% of the time, Pallas kernels for 15%

profile of v4, /device:TPU:0, one launch (start us, length us, event | category | flops | bytes accessed | tf_op | source)
XLA Modules:
  0.0 47.2 jit_solution(10155759187929744283)
XLA Ops:
  0.6 3.1 %collective-permute-start.7 = (bf16[704,384]{1,0:T(8,128)(2,1)}, bf16[704,384]{1,0:T(8,128)(2,1)S(1)}, u32[]{:S(2)}, u32[]{:S(2)}) collective-permute-start(bf16[704,384]{1,0:T(8,128)(2,1)} %bitcast.8), channel_id=1, source_target_pairs={{0,2},{2,4},{4,6},{6,7},{7,5},{5,3},{3,1},{1,0},{10,8},{12,10},{14... | collective-permute-start | bytes 1622024 | tf_op jit(solution)/shard_map/ppermute | solution.py:475
  3.7 0.5 %collective-permute-start.1 = (bf16[352,1408]{1,0:T(8,128)(2,1)}, bf16[352,1408]{1,0:T(8,128)(2,1)S(1)}, u32[]{:S(2)}, u32[]{:S(2)}) collective-permute-start(bf16[352,1408]{1,0:T(8,128)(2,1)} %context.1), channel_id=1, source_target_pairs={{0,8},{8,0},{16,24},{24,16},{1,9},{9,1},{17,25},{25,17},{2,10},{10... | collective-permute-start | bytes 2973704 | tf_op jit(solution)/shard_map/ppermute | solution.py:424
  4.2 7.0 %collective-permute-done.7.whole.refs_1_ = bf16[704,384]{1,0:T(8,128)(2,1)S(1)} collective-permute-done((bf16[704,384]{1,0:T(8,128)(2,1)}, bf16[704,384]{1,0:T(8,128)(2,1)S(1)}, u32[]{:S(2)}, u32[]{:S(2)}) %collective-permute-start.7) | collective-permute-done | bytes 540704 | tf_op jit(solution)/shard_map/ppermute | solution.py:475
  11.3 2.1 %collective-permute-start.9 = (bf16[352,384]{1,0:T(8,128)(2,1)S(1)}, bf16[352,384]{1,0:T(8,128)(2,1)S(1)}, u32[]{:S(2)}, u32[]{:S(2)}) collective-permute-start(bf16[352,384]{1,0:T(8,128)(2,1)S(1)} %get-tuple-element.37), channel_id=1, source_target_pairs={{0,2},{2,4},{4,6},{6,7},{7,5},{5,3},{3,1},{1,0},{10,8},{12,10},{14... | collective-permute-start | bytes 811016 | tf_op jit(solution)/shard_map/ppermute | solution.py:478
  13.4 1.6 %collective-permute-start.10 = (bf16[352,384]{1,0:T(8,128)(2,1)S(1)}, bf16[352,384]{1,0:T(8,128)(2,1)S(1)}, u32[]{:S(2)}, u32[]{:S(2)}) collective-permute-start(bf16[352,384]{1,0:T(8,128)(2,1)S(1)} %get-tuple-element.38), channel_id=1, source_target_pairs={{0,2},{2,4},{4,6},{6,7},{7,5},{5,3},{3,1},{1,0},{10,8},{12,10},{14... | collective-permute-start | bytes 811016 | tf_op jit(solution)/shard_map/ppermute | solution.py:479
  15.0 1.0 %copy-done.7 = bf16[1,128,1408]{2,1,0:T(8,128)(2,1)S(1)} copy-done((bf16[1,128,1408]{2,1,0:T(8,128)(2,1)S(1)}, bf16[1,128,1408]{2,1,0:T(8,128)(2,1)}, u32[]{:S(2)}) %copy-start.7) | copy-done | bytes 360472
  16.5 1.6 %collective-permute-start.2 = (bf16[128,704]{1,0:T(8,128)(2,1)S(1)}, bf16[128,704]{1,0:T(8,128)(2,1)S(1)}, u32[]{:S(2)}, u32[]{:S(2)}) collective-permute-start(bf16[128,704]{1,0:T(8,128)(2,1)S(1)} %get-tuple-element.27), channel_id=1, source_target_pairs={{0,16},{8,24},{16,0},{24,8},{1,17},{9,25},{17,1},{25,9},{2,18},{10... | collective-permute-start | bytes 540680 | tf_op jit(solution)/shard_map/ppermute | solution.py:431
  18.0 1.8 %collective-permute-start.12 = (bf16[352,384]{1,0:T(8,128)(2,1)S(1)}, bf16[352,384]{1,0:T(8,128)(2,1)S(1)}, u32[]{:S(2)}, u32[]{:S(2)}) collective-permute-start(bf16[352,384]{1,0:T(8,128)(2,1)S(1)} %collective-permute-done.9.first), channel_id=1, source_target_pairs={{0,2},{2,4},{4,6},{6,7},{7,5},{5,3},{3,1},{1,0},{10,8},{12,10},{14... | collective-permute-start | bytes 811016 | tf_op jit(solution)/shard_map/ppermute | solution.py:478
  19.9 0.8 %collective-permute-done.10.second = bf16[352,384]{1,0:T(8,128)(2,1)S(1)} collective-permute-done((bf16[352,384]{1,0:T(8,128)(2,1)S(1)}, bf16[352,384]{1,0:T(8,128)(2,1)S(1)}, u32[]{:S(2)}, u32[]{:S(2)}) %collective-permute-start.10) | collective-permute-done | bytes 270368 | tf_op jit(solution)/shard_map/ppermute | solution.py:479
  20.7 2.1 %collective-permute-start.15 = (bf16[352,384]{1,0:T(8,128)(2,1)S(1)}, bf16[352,384]{1,0:T(8,128)(2,1)S(1)}, u32[]{:S(2)}, u32[]{:S(2)}) collective-permute-start(bf16[352,384]{1,0:T(8,128)(2,1)S(1)} %collective-permute-done.10.second), channel_id=1, source_target_pairs={{0,2},{2,4},{4,6},{6,7},{7,5},{5,3},{3,1},{1,0},{10,8},{12,10},{14... | collective-permute-start | bytes 811016 | tf_op jit(solution)/shard_map/ppermute | solution.py:479
  22.8 2.2 %shard_map.104 = (bf16[704,1408]{1,0:T(8,128)(2,1)S(1)}, f32[128,768]{1,0:T(8,128)S(1)}, bf16[128,384]{1,0:T(8,128)(2,1)S(1)}, bf16[128,1152]{1,0:T(8,128)(2,1)S(1)}, bf16[352,1408]{1,0:T(8,128)(2,1)}) custom-call(bf16[352,1408]{1,0:T(8,128)(2,1)S(1)} %copy-done.2, bf16[352,1408]{1,0:T(8,128)(2,1)S(1)} %copy-done.3, ...), custom_call_target="tpu_custom_call" | custom-call | flops 507510784 | bytes 3964928 | tf_op jit(solution)/shard_map/pallas_call | solution.py:146
  25.0 1.6 %collective-permute-start.4 = (bf16[128,1152]{1,0:T(8,128)(2,1)S(1)}, bf16[128,1152]{1,0:T(8,128)(2,1)S(1)}, u32[]{:S(2)}, u32[]{:S(2)}) collective-permute-start(bf16[128,1152]{1,0:T(8,128)(2,1)S(1)} %get-tuple-element.31), channel_id=1, source_target_pairs={{0,16},{8,24},{16,0},{24,8},{1,17},{9,25},{17,1},{25,9},{2,18},{10... | collective-permute-start | bytes 884744 | tf_op jit(solution)/shard_map/ppermute | solution.py:446
  27.1 0.6 %collective-permute-start.3 = (bf16[128,768]{1,0:T(8,128)(2,1)S(1)}, bf16[128,768]{1,0:T(8,128)(2,1)S(1)}, u32[]{:S(2)}, u32[]{:S(2)}) collective-permute-start(bf16[128,768]{1,0:T(8,128)(2,1)S(1)} %get-tuple-element.30), channel_id=1, source_target_pairs={{0,16},{8,24},{16,0},{24,8},{1,17},{9,25},{17,1},{25,9},{2,18},{10... | collective-permute-start | bytes 589832 | tf_op jit(solution)/shard_map/ppermute | solution.py:453
  27.8 0.6 %collective-permute-start.11 = (bf16[704,384]{1,0:T(8,128)(2,1)S(1)}, bf16[704,384]{1,0:T(8,128)(2,1)S(1)}, u32[]{:S(2)}, u32[]{:S(2)}) collective-permute-start(bf16[704,384]{1,0:T(8,128)(2,1)S(1)} %shard_map.110.refs_3_), channel_id=1, source_target_pairs={{0,8},{8,0},{16,24},{24,16},{1,9},{9,1},{17,25},{25,17},{2,10},{10... | collective-permute-start | bytes 1622024 | tf_op jit(solution)/shard_map/ppermute | solution.py:481
  28.4 1.6 %collective-permute-start.13 = (bf16[352,384]{1,0:T(8,128)(2,1)S(1)}, bf16[352,384]{1,0:T(8,128)(2,1)S(1)}, u32[]{:S(2)}, u32[]{:S(2)}) collective-permute-start(bf16[352,384]{1,0:T(8,128)(2,1)S(1)} %collective-permute-done.12.first), channel_id=1, source_target_pairs={{0,2},{2,4},{4,6},{6,7},{7,5},{5,3},{3,1},{1,0},{10,8},{12,10},{14... | collective-permute-start | bytes 811016 | tf_op jit(solution)/shard_map/ppermute | solution.py:484
  30.0 6.0 %collective-permute-done.3.from_other = bf16[128,768]{1,0:T(8,128)(2,1)S(1)} collective-permute-done((bf16[128,768]{1,0:T(8,128)(2,1)S(1)}, bf16[128,768]{1,0:T(8,128)(2,1)S(1)}, u32[]{:S(2)}, u32[]{:S(2)}) %collective-permute-start.3) | collective-permute-done | bytes 196640 | tf_op jit(solution)/shard_map/ppermute | solution.py:453
  36.1 0.6 %collective-permute-start.5 = (bf16[256,768]{1,0:T(8,128)(2,1)S(1)}, bf16[256,768]{1,0:T(8,128)(2,1)S(1)}, u32[]{:S(2)}, u32[]{:S(2)}) collective-permute-start(bf16[256,768]{1,0:T(8,128)(2,1)S(1)} %get-tuple-element.34.kv_a), channel_id=1, source_target_pairs={{0,8},{8,0},{16,24},{24,16},{1,9},{9,1},{17,25},{25,17},{2,10},{10... | collective-permute-start | bytes 1179656 | tf_op jit(solution)/shard_map/ppermute | solution.py:459
  36.8 1.7 %collective-permute-done.5.kv_b = bf16[256,768]{1,0:T(8,128)(2,1)S(1)} collective-permute-done((bf16[256,768]{1,0:T(8,128)(2,1)S(1)}, bf16[256,768]{1,0:T(8,128)(2,1)S(1)}, u32[]{:S(2)}, u32[]{:S(2)}) %collective-permute-start.5) | collective-permute-done | bytes 393248 | tf_op jit(solution)/shard_map/ppermute | solution.py:459
  38.5 1.6 %shard_map.108 = (f32[128,384]{1,0:T(8,128)S(1)}, bf16[128,384]{1,0:T(8,128)(2,1)S(1)}) custom-call(bf16[256,384]{1,0:T(8,128)(2,1)S(1)} %get-tuple-element.33.queries, bf16[256,768]{1,0:T(8,128)(2,1)S(1)} %get-tuple-element.34.kv_a, bf16[256,768]{1,0:T(8,128)(2,1)S(1)} %collective-permute-done.5.kv_b), custom_call_target="tpu_custom_call" | custom-call | flops 402653184 | bytes 1572864 | tf_op jit(solution)/shard_map/pallas_call | solution.py:146
  40.1 1.6 %collective-permute-start.6 = (bf16[128,384]{1,0:T(8,128)(2,1)S(1)}, bf16[128,384]{1,0:T(8,128)(2,1)S(1)}, u32[]{:S(2)}, u32[]{:S(2)}) collective-permute-start(bf16[128,384]{1,0:T(8,128)(2,1)S(1)} %get-tuple-element.36), channel_id=1, source_target_pairs={{0,16},{8,24},{16,0},{24,8},{1,17},{9,25},{17,1},{25,9},{2,18},{10... | collective-permute-start | bytes 294920 | tf_op jit(solution)/shard_map/ppermute | solution.py:466
  41.8 1.2 %shard_map.111.earlier = f32[128,704]{1,0:T(8,128)S(1)} custom-call(s32[128,64]{1,0:T(8,128)S(1)} %shard_map.105.match, s32[1,64]{1,0:T(1,128)S(1)} %bitcast.14, bf16[128,384]{1,0:T(8,128)(2,1)S(1)} %bitcast.11, bf16[704,384]{1,0:T(8,128)(2,1)S(1)} %bitcast.9, bf16[704,384]{1,0:T(8,128)(2,1)S(1)} %collective-permute-done.7.whole.refs_1_, ...), custom_call_target="tpu_custom_call" | custom-call | flops 346030080 | bytes 2703360 | tf_op jit(solution)/shard_map/pallas_call | solution.py:146
  43.0 0.9 %shard_map.113 = (f32[128,704]{1,0:T(8,128)S(1)}, bf16[704,384]{1,0:T(8,128)(2,1)S(1)}) custom-call(s32[128,64]{1,0:T(8,128)S(1)} %shard_map.105.match, s32[1,64]{1,0:T(1,128)S(1)} %bitcast.15, bf16[128,384]{1,0:T(8,128)(2,1)S(1)} %bitcast.12, f32[128,704]{1,0:T(8,128)S(1)} %shard_map.111.earlier, bf16[352,384]{1,0:T(8,128)(2,1)S(1)} %collective-permute-done.13.mine, ...), custom_call_target="tpu_custom_call" | custom-call | flops 207618048 | bytes 1622016 | tf_op jit(solution)/shard_map/pallas_call | solution.py:146
  43.9 1.2 %collective-permute-done.6.returned = bf16[128,384]{1,0:T(8,128)(2,1)S(1)} collective-permute-done((bf16[128,384]{1,0:T(8,128)(2,1)S(1)}, bf16[128,384]{1,0:T(8,128)(2,1)S(1)}, u32[]{:S(2)}, u32[]{:S(2)}) %collective-permute-start.6) | collective-permute-done | bytes 98336 | tf_op jit(solution)/shard_map/ppermute | solution.py:466
  45.0 2.1 %shard_map.114 = (bf16[704,128]{1,0:T(8,128)(2,1)}, bf16[128,384]{1,0:T(8,128)(2,1)}) custom-call(s32[128,64]{1,0:T(8,128)S(1)} %shard_map.105.match, s32[1,64]{1,0:T(1,128)S(1)} %bitcast.16, s32[1,64]{1,0:T(1,128)S(1)} %copy-done.6, f32[128,384]{1,0:T(8,128)S(1)} %get-tuple-element.35.attended, bf16[128,384]{1,0:T(8,128)(2,1)S(1)} %collective-permute-done.6.returned, ...), custom_call_target="tpu_custom_call" | custom-call | flops 553648128 | bytes 4325376 | tf_op jit(solution)/shard_map/pallas_call | solution.py:146
  (38 shorter events, 1.4 us)
Async XLA Ops:
  0.6 10.6 %collective-permute-start.7 = (bf16[704,384]{1,0:T(8,128)(2,1)}, bf16[704,384]{1,0:T(8,128)(2,1)S(1)}, u32[]{:S(2)}, u32[]{:S(2)}) collective-permute-start(bf16[704,384]{1,0:T(8,128)(2,1)} %bitcast.8), channel_id=1, source_target_pairs={{0,2},{2,4},{4,6},{6,7},{7,5},{5,3},{3,1},{1,0},{10,8},{12,10},{14... | collective-permute-start | bytes 1622024 | tf_op jit(solution)/shard_map/ppermute | solution.py:475
  3.7 19.0 %collective-permute-start = (bf16[352,1408]{1,0:T(8,128)(2,1)}, bf16[352,1408]{1,0:T(8,128)(2,1)S(1)}, u32[]{:S(2)}, u32[]{:S(2)}) collective-permute-start(bf16[352,1408]{1,0:T(8,128)(2,1)} %target.1), channel_id=1, source_target_pairs={{0,8},{8,0},{16,24},{24,16},{1,9},{9,1},{17,25},{25,17},{2,10},{10... | collective-permute-start | bytes 2973704 | tf_op jit(solution)/shard_map/ppermute | solution.py:423
  3.7 19.0 %collective-permute-start.1 = (bf16[352,1408]{1,0:T(8,128)(2,1)}, bf16[352,1408]{1,0:T(8,128)(2,1)S(1)}, u32[]{:S(2)}, u32[]{:S(2)}) collective-permute-start(bf16[352,1408]{1,0:T(8,128)(2,1)} %context.1), channel_id=1, source_target_pairs={{0,8},{8,0},{16,24},{24,16},{1,9},{9,1},{17,25},{25,17},{2,10},{10... | collective-permute-start | bytes 2973704 | tf_op jit(solution)/shard_map/ppermute | solution.py:424
  11.3 6.7 %collective-permute-start.9 = (bf16[352,384]{1,0:T(8,128)(2,1)S(1)}, bf16[352,384]{1,0:T(8,128)(2,1)S(1)}, u32[]{:S(2)}, u32[]{:S(2)}) collective-permute-start(bf16[352,384]{1,0:T(8,128)(2,1)S(1)} %get-tuple-element.37), channel_id=1, source_target_pairs={{0,2},{2,4},{4,6},{6,7},{7,5},{5,3},{3,1},{1,0},{10,8},{12,10},{14... | collective-permute-start | bytes 811016 | tf_op jit(solution)/shard_map/ppermute | solution.py:478
  13.4 7.3 %collective-permute-start.10 = (bf16[352,384]{1,0:T(8,128)(2,1)S(1)}, bf16[352,384]{1,0:T(8,128)(2,1)S(1)}, u32[]{:S(2)}, u32[]{:S(2)}) collective-permute-start(bf16[352,384]{1,0:T(8,128)(2,1)S(1)} %get-tuple-element.38), channel_id=1, source_target_pairs={{0,2},{2,4},{4,6},{6,7},{7,5},{5,3},{3,1},{1,0},{10,8},{12,10},{14... | collective-permute-start | bytes 811016 | tf_op jit(solution)/shard_map/ppermute | solution.py:479
  16.0 6.8 %copy-start.1 = (bf16[704,1408]{1,0:T(8,128)(2,1)S(1)}, bf16[704,1408]{1,0:T(8,128)(2,1)}, u32[]{:S(2)}) copy-start(bf16[704,1408]{1,0:T(8,128)(2,1)} %query_weight.1) | copy-start | bytes 5947396
  16.0 6.8 %copy-start.2 = (bf16[352,1408]{1,0:T(8,128)(2,1)S(1)}, bf16[352,1408]{1,0:T(8,128)(2,1)}, u32[]{:S(2)}) copy-start(bf16[352,1408]{1,0:T(8,128)(2,1)} %target.1) | copy-start | bytes 2973700
  16.0 6.8 %copy-start.3 = (bf16[352,1408]{1,0:T(8,128)(2,1)S(1)}, bf16[352,1408]{1,0:T(8,128)(2,1)}, u32[]{:S(2)}) copy-start(bf16[352,1408]{1,0:T(8,128)(2,1)} %context.1) | copy-start | bytes 2973700
  16.5 10.1 %collective-permute-start.2 = (bf16[128,704]{1,0:T(8,128)(2,1)S(1)}, bf16[128,704]{1,0:T(8,128)(2,1)S(1)}, u32[]{:S(2)}, u32[]{:S(2)}) collective-permute-start(bf16[128,704]{1,0:T(8,128)(2,1)S(1)} %get-tuple-element.27), channel_id=1, source_target_pairs={{0,16},{8,24},{16,0},{24,8},{1,17},{9,25},{17,1},{25,9},{2,18},{10... | collective-permute-start | bytes 540680 | tf_op jit(solution)/shard_map/ppermute | solution.py:431
  18.0 9.8 %collective-permute-start.12 = (bf16[352,384]{1,0:T(8,128)(2,1)S(1)}, bf16[352,384]{1,0:T(8,128)(2,1)S(1)}, u32[]{:S(2)}, u32[]{:S(2)}) collective-permute-start(bf16[352,384]{1,0:T(8,128)(2,1)S(1)} %collective-permute-done.9.first), channel_id=1, source_target_pairs={{0,2},{2,4},{4,6},{6,7},{7,5},{5,3},{3,1},{1,0},{10,8},{12,10},{14... | collective-permute-start | bytes 811016 | tf_op jit(solution)/shard_map/ppermute | solution.py:478
  20.7 7.7 %collective-permute-start.15 = (bf16[352,384]{1,0:T(8,128)(2,1)S(1)}, bf16[352,384]{1,0:T(8,128)(2,1)S(1)}, u32[]{:S(2)}, u32[]{:S(2)}) collective-permute-start(bf16[352,384]{1,0:T(8,128)(2,1)S(1)} %collective-permute-done.10.second), channel_id=1, source_target_pairs={{0,2},{2,4},{4,6},{6,7},{7,5},{5,3},{3,1},{1,0},{10,8},{12,10},{14... | collective-permute-start | bytes 811016 | tf_op jit(solution)/shard_map/ppermute | solution.py:479
  25.0 11.0 %collective-permute-start.4 = (bf16[128,1152]{1,0:T(8,128)(2,1)S(1)}, bf16[128,1152]{1,0:T(8,128)(2,1)S(1)}, u32[]{:S(2)}, u32[]{:S(2)}) collective-permute-start(bf16[128,1152]{1,0:T(8,128)(2,1)S(1)} %get-tuple-element.31), channel_id=1, source_target_pairs={{0,16},{8,24},{16,0},{24,8},{1,17},{9,25},{17,1},{25,9},{2,18},{10... | collective-permute-start | bytes 884744 | tf_op jit(solution)/shard_map/ppermute | solution.py:446
  27.1 8.9 %collective-permute-start.3 = (bf16[128,768]{1,0:T(8,128)(2,1)S(1)}, bf16[128,768]{1,0:T(8,128)(2,1)S(1)}, u32[]{:S(2)}, u32[]{:S(2)}) collective-permute-start(bf16[128,768]{1,0:T(8,128)(2,1)S(1)} %get-tuple-element.30), channel_id=1, source_target_pairs={{0,16},{8,24},{16,0},{24,8},{1,17},{9,25},{17,1},{25,9},{2,18},{10... | collective-permute-start | bytes 589832 | tf_op jit(solution)/shard_map/ppermute | solution.py:453
  27.7 14.0 %collective-permute-start.8 = (bf16[704,384]{1,0:T(8,128)(2,1)S(1)}, bf16[704,384]{1,0:T(8,128)(2,1)S(1)}, u32[]{:S(2)}, u32[]{:S(2)}) collective-permute-start(bf16[704,384]{1,0:T(8,128)(2,1)S(1)} %collective-permute-done.7.whole.refs_1_), channel_id=1, source_target_pairs={{0,8},{8,0},{16,24},{24,16},{1,9},{9,1},{17,25},{25,17},{2,10},{10... | collective-permute-start | bytes 1622024 | tf_op jit(solution)/shard_map/ppermute | solution.py:481
  27.8 14.0 %copy-start = (bf16[1,704,384]{2,1,0:T(8,128)(2,1)S(1)}, bf16[1,704,384]{2,1,0:T(8,128)(2,1)}, u32[]{:S(2)}) copy-start(bf16[1,704,384]{2,1,0:T(8,128)(2,1)} %param.13) | copy-start | bytes 1622020
  27.8 14.0 %copy-start.4 = (bf16[1,128,384]{2,1,0:T(8,128)(2,1)S(1)}, bf16[1,128,384]{2,1,0:T(8,128)(2,1)}, u32[]{:S(2)}) copy-start(bf16[1,128,384]{2,1,0:T(8,128)(2,1)} %param.12) | copy-start | bytes 294916
  27.8 14.0 %copy-start.5 = (s32[1,64,1]{1,2,0:T(1,128)S(1)}, s32[1,64,1]{1,2,0:T(1,128)}, u32[]{:S(2)}) copy-start(s32[1,64,1]{1,2,0:T(1,128)} %param.15) | copy-start | bytes 772
  27.8 13.9 %collective-permute-start.11 = (bf16[704,384]{1,0:T(8,128)(2,1)S(1)}, bf16[704,384]{1,0:T(8,128)(2,1)S(1)}, u32[]{:S(2)}, u32[]{:S(2)}) collective-permute-start(bf16[704,384]{1,0:T(8,128)(2,1)S(1)} %shard_map.110.refs_3_), channel_id=1, source_target_pairs={{0,8},{8,0},{16,24},{24,16},{1,9},{9,1},{17,25},{25,17},{2,10},{10... | collective-permute-start | bytes 1622024 | tf_op jit(solution)/shard_map/ppermute | solution.py:481
  28.4 8.3 %collective-permute-start.13 = (bf16[352,384]{1,0:T(8,128)(2,1)S(1)}, bf16[352,384]{1,0:T(8,128)(2,1)S(1)}, u32[]{:S(2)}, u32[]{:S(2)}) collective-permute-start(bf16[352,384]{1,0:T(8,128)(2,1)S(1)} %collective-permute-done.12.first), channel_id=1, source_target_pairs={{0,2},{2,4},{4,6},{6,7},{7,5},{5,3},{3,1},{1,0},{10,8},{12,10},{14... | collective-permute-start | bytes 811016 | tf_op jit(solution)/shard_map/ppermute | solution.py:484
  36.0 7.0 %collective-permute-start.16 = (bf16[704,384]{1,0:T(8,128)(2,1)S(1)}, bf16[704,384]{1,0:T(8,128)(2,1)S(1)}, u32[]{:S(2)}, u32[]{:S(2)}) collective-permute-start(bf16[704,384]{1,0:T(8,128)(2,1)S(1)} %shard_map.112.refs_0_.refs_5_), channel_id=1, source_target_pairs={{0,8},{8,0},{16,24},{24,16},{1,9},{9,1},{17,25},{25,17},{2,10},{10... | collective-permute-start | bytes 1622024 | tf_op jit(solution)/shard_map/ppermute | solution.py:481
  36.1 2.4 %collective-permute-start.5 = (bf16[256,768]{1,0:T(8,128)(2,1)S(1)}, bf16[256,768]{1,0:T(8,128)(2,1)S(1)}, u32[]{:S(2)}, u32[]{:S(2)}) collective-permute-start(bf16[256,768]{1,0:T(8,128)(2,1)S(1)} %get-tuple-element.34.kv_a), channel_id=1, source_target_pairs={{0,8},{8,0},{16,24},{24,16},{1,9},{9,1},{17,25},{25,17},{2,10},{10... | collective-permute-start | bytes 1179656 | tf_op jit(solution)/shard_map/ppermute | solution.py:459
  36.7 6.3 %collective-permute-start.14 = (bf16[352,384]{1,0:T(8,128)(2,1)S(1)}, bf16[352,384]{1,0:T(8,128)(2,1)S(1)}, u32[]{:S(2)}, u32[]{:S(2)}) collective-permute-start(bf16[352,384]{1,0:T(8,128)(2,1)S(1)} %collective-permute-done.13.mine), channel_id=1, source_target_pairs={{0,8},{8,0},{16,24},{24,16},{1,9},{9,1},{17,25},{25,17},{2,10},{10... | collective-permute-start | bytes 811016 | tf_op jit(solution)/shard_map/ppermute | solution.py:485
  40.1 4.9 %collective-permute-start.6 = (bf16[128,384]{1,0:T(8,128)(2,1)S(1)}, bf16[128,384]{1,0:T(8,128)(2,1)S(1)}, u32[]{:S(2)}, u32[]{:S(2)}) collective-permute-start(bf16[128,384]{1,0:T(8,128)(2,1)S(1)} %get-tuple-element.36), channel_id=1, source_target_pairs={{0,16},{8,24},{16,0},{24,8},{1,17},{9,25},{17,1},{25,9},{2,18},{10... | collective-permute-start | bytes 294920 | tf_op jit(solution)/shard_map/ppermute | solution.py:466
  41.8 3.3 %copy-start.6 = (s32[1,64]{1,0:T(1,128)S(1)}, s32[1,64]{1,0:T(1,128)}, u32[]{:S(2)}) copy-start(s32[1,64]{1,0:T(1,128)} %mask.1) | copy-start | bytes 772
  (1 other events, 1.0 us)

commit v5 on v4

--- a/solution.py
+++ b/solution.py
@@ -217,11 +217,11 @@
     depth = target.shape[0]
     own_rows = pl.ds(pl.multiple_of(core * depth, 16), depth)
     joined[own_rows, :] = blend(target, context)
+    joined[pl.ds(pl.multiple_of((1 - core) * depth, 16), depth), :] = blend(
+        other_target, other_context
+    )
     store = pltpu.make_async_copy(joined.at[own_rows], stored, sem)
     store.start()
-    joined[pl.ds(pl.multiple_of((1 - core) * depth, 16), depth), :] = blend(
-        other_target, other_context
-    )
     split_product(rows, joined, own, send)
     queries = lax.dot_general(
         normed[...], query_weight[...], (((1,), (1,)), ((), ())), preferred_element_type=jnp.float32
@@ -275,24 +275,31 @@
 def attend_body(queries, kv_a, kv_b, mine, theirs):
     upper_lane = lax.broadcasted_iota(jnp.int32, (1, LANES), 1) >= HEAD
     rows = mine.shape[0]
-    found = [None] * 6
-    for slot in range(6):
-        total = add_keys(queries, (kv_a, kv_b), slot)
-        found[(slot + 1) % 6] = total / pltpu.roll(total, HEAD, 1)
     for t in range(3):
-        joined = jnp.where(upper_lane, found[2 * t + 1], found[2 * t])
+        low = add_keys(queries, (kv_a, kv_b), (2 * t + 5) % 6)
+        high = add_keys(queries, (kv_a, kv_b), 2 * t)
+        sums = pltpu.roll(jnp.where(upper_lane, low, high), HEAD, 1)
+        joined = jnp.where(upper_lane, high, low) / sums
         mine[:, t * LANES : (t + 1) * LANES] = joined[:rows]
         theirs[:, t * LANES : (t + 1) * LANES] = joined[rows:].astype(theirs.dtype)
 
 
-def match_body(match):
-    token = lax.broadcasted_iota(jnp.int32, match.shape, 0) // 2
-    pair = lax.broadcasted_iota(jnp.int32, match.shape, 1)
-    match[...] = (token == pair).astype(match.dtype)
-
-
-def token_values(match, pairs):
-    return jnp.sum(match[...] * pairs[...], axis=1, keepdims=True)
+def token_values(pairs, rows):
+    shape = (rows, pairs.shape[1])
+    token = lax.broadcasted_iota(jnp.int32, shape, 0) // 2
+    pair = lax.broadcasted_iota(jnp.int32, shape, 1)
+    return jnp.sum(jnp.where(token == pair, pairs[...], 0), axis=1, keepdims=True)
+
+
+def hidden_body(owners, mask, hidden, normed, factor, ids):
+    inputs = hidden[...].astype(jnp.float32)
+    rows = inputs.shape[0]
+    center = inputs - jnp.mean(inputs, axis=-1, keepdims=True)
+    inverse = lax.rsqrt(jnp.mean(center * center, axis=-1, keepdims=True) + epsilon)
+    normed[...] = center * inverse
+    live = token_values(mask, rows) == 1
+    factor[...] = jnp.broadcast_to(jnp.where(live, inverse, 0.0), factor.shape)
+    ids[...] = jnp.broadcast_to(token_values(owners, rows), ids.shape)
 
 
 def owner_at(moved, groups):
@@ -318,12 +325,11 @@
     joined[pl.ds(pl.multiple_of((1 - core) * rows, 16), rows), :] = theirs[...]
 
 
-def add_predictions(match, owners, hidden, weights, ids_of):
-    normed = layer_norm(hidden[...].astype(jnp.float32)).astype(jnp.bfloat16)
-    ids = token_values(match, owners)
+def add_predictions(ids, normed, weights, ids_of):
+    values, owner_of = normed[...].astype(jnp.bfloat16), ids[:, :1]
     total = None
     for weight, owner in zip(weights, ids_of):
-        picked = jnp.where(ids == owner, normed, jnp.zeros_like(normed))
+        picked = jnp.where(owner_of == owner, values, jnp.zeros_like(values))
         part = lax.dot_general(
             picked, weight[...], (((1,), (1,)), ((), ())), preferred_element_type=jnp.float32
         )
@@ -331,18 +337,22 @@
     return total
 
 
-def predict_body(groups, match, owners, hidden, *refs):
+def predict_body(groups, ids, normed, *refs):
     weights, prediction = refs[:-1], refs[-1]
-    prediction[...] = add_predictions(match, owners, hidden, weights, slot_owners(groups))
-
-
-def predict_rest_body(groups, match, owners, hidden, earlier, mine, theirs, *refs):
+    prediction[...] = add_predictions(ids, normed, weights, slot_owners(groups))
+
+
+def predict_more_body(groups, done, ids, normed, earlier, *refs):
+    weights, prediction = refs[:-1], refs[-1]
+    places = slot_owners(groups)[done : done + len(weights)]
+    prediction[...] = earlier[...] + add_predictions(ids, normed, weights, places)
+
+
+def predict_rest_body(groups, ids, normed, earlier, mine, theirs, *refs):
     weights, (prediction, joined) = refs[:-2], refs[-2:]
     join_halves(mine, theirs, joined)
     places = slot_owners(groups)[groups - 1 - len(weights) :]
-    prediction[...] = earlier[...] + add_predictions(
-        match, owners, hidden, (*weights, joined), places
-    )
+    prediction[...] = earlier[...] + add_predictions(ids, normed, (*weights, joined), places)
 
 
 def cut_body(whole, first, second):
@@ -356,16 +366,16 @@
     join_halves(first, second, joined)
 
 
-def add_upstream(residual, ids, weights, ids_of):
+def pick_upstream(residual, ids, weights, ids_of):
+    owner_of = jnp.tile(ids[...], (1, weights[0].shape[1] // ids.shape[1]))
     total = None
     for weight, owner in zip(weights, ids_of):
-        picked = jnp.where(ids == owner, residual, jnp.zeros_like(residual))
-        part = jnp.dot(picked, weight[...], preferred_element_type=jnp.float32)
-        total = part if total is None else total + part
+        part = jnp.dot(residual, weight[...], preferred_element_type=jnp.float32)
+        total = part if total is None else jnp.where(owner_of == owner, part, total)
     return total
 
 
-def finish_body(groups, match, owners, mask, attended, returned, prediction, hidden, *refs):
+def finish_body(groups, ids, normed, factor, attended, returned, prediction, *refs):
     weights, (targets, grad) = refs[:-2], refs[-2:]
     chip, _ = chip_and_core()
     width, _ = targets.shape
@@ -381,11 +391,12 @@
     found = (center * lax.rsqrt(variance + epsilon))[:, HEAD:].astype(jnp.bfloat16)
     targets[...] = found.T
     residual = (prediction[...] - found.astype(jnp.float32)).astype(jnp.bfloat16)
-    ids = token_values(match, owners)
-    upstream = add_upstream(residual, ids, weights, slot_owners(groups))
-    inputs = hidden[...].astype(jnp.float32)
-    back = norm_backward(upstream, layer_norm(inputs), inputs)
-    grad[...] = jnp.where(token_values(match, mask) == 1, back, 0.0).astype(grad.dtype)
+    upstream = pick_upstream(residual, ids, weights, slot_owners(groups))
+    values = normed[...]
+    mean = jnp.mean(upstream, axis=-1, keepdims=True)
+    cross = jnp.mean(upstream * values, axis=-1, keepdims=True)
+    scale = jnp.tile(factor[...], (1, values.shape[1] // factor.shape[1]))
+    grad[...] = (scale * (upstream - mean - values * cross)).astype(grad.dtype)
 
 
 def ring_pairs(members, groups):
@@ -415,11 +426,6 @@
     owner_row, mask_row = owners.reshape(1, -1), target_mask.reshape(1, -1)
     sums_shape = shape_of((rows, 2 * packed), jnp.float32)
 
-    match = local_call(
-        match_body,
-        shape_of((rows, owner_row.shape[1]), jnp.int32),
-        (),
-    )
     other_target = lax.ppermute(target_kv, "seq", beside)
     other_context = lax.ppermute(context_kv, "seq", beside)
     normed, keep, send = local_call(
@@ -483,26 +489,40 @@
         first, second = local_call(cut_body, halves, (pred_weight[0],))
     mine = lax.ppermute(first, ("seq", "grp"), ring)
     theirs = lax.ppermute(mine, "seq", beside)
-    early = groups - 3 if groups > 4 else 1
+    early, most = min(3, groups - 1), groups - 1
+    normed_hidden, factor, ids = local_call(
+        hidden_body,
+        [
+            shape_of((rows, pred_size), jnp.float32),
+            shape_of((rows, LANES), jnp.float32),
+            shape_of((rows, LANES), jnp.int32),
+        ],
+        (owner_row, mask_row, pred_hidden[0]),
+    )
     prediction = local_call(
         functools.partial(predict_body, groups),
         shape_of((rows, width), jnp.float32),
-        (match, owner_row, pred_hidden[0], *weights[:early]),
+        (ids, normed_hidden, *weights[:early]),
         cost=matmul_cost(rows, early * pred_size, width),
     )
+    if most > early:
+        prediction = local_call(
+            functools.partial(predict_more_body, groups, early),
+            shape_of((rows, width), jnp.float32),
+            (ids, normed_hidden, prediction, *weights[early:most]),
+            cost=matmul_cost(rows, (most - early) * pred_size, width),
+        )
     prediction, opposite = local_call(
         functools.partial(predict_rest_body, groups),
         [shape_of((rows, width), jnp.float32), whole_shape],
-        (match, owner_row, pred_hidden[0], prediction, mine, theirs, *weights[early:]),
-        cost=matmul_cost(rows, (groups - early) * pred_size, width),
+        (ids, normed_hidden, prediction, mine, theirs),
+        cost=matmul_cost(rows, pred_size, width),
     )
     weights.append(opposite)
     targets, grad = local_call(
         functools.partial(finish_body, groups),
         [shape_of((width, rows)), shape_of((rows, pred_size))],
-        (
-            match, owner_row, mask_row, attended, returned, prediction, pred_hidden[0], *weights
-        ),
+        (ids, normed_hidden, factor, attended, returned, prediction, *weights),
         out_specs=[pl.BlockSpec(), pl.BlockSpec()],
         cost=matmul_cost(rows, groups * pred_size, width),
     )

time: 47.3 us -> 51.9 us (1.097)
  waiting for transfers between devices: 16.7 us -> 22.7 us
  starting transfers between devices: 19.3 us -> 17.6 us
    ppermute x1, waiting for transfers between devices: 0.01 us -> 5.96 us  [paired_shards(): mine = lax.ppermute(first, ('seq', 'grp'), ring)]
    ppermute x1, waiting for transfers between devices: 1.75 us -> 0.01 us  [paired_shards(): kv_beside = lax.ppermute(kv, 'seq', beside)]
    ppermute x1, waiting for transfers between devices: 5.98 us -> 7.48 us  [paired_shards(): from_other = lax.ppermute(other_send, 'seq', across)]
    ppermute x1, starting transfers between devices: 1.58 us -> 0.34 us  [paired_shards(): mine = lax.ppermute(first, ('seq', 'grp'), ring)]
    pallas_call x12 -> x13, Pallas kernels: 9.29 us -> 9.58 us  [local_call(): pl.pallas_call(body, out_shape=outs, in_specs=specs or [VM] * len(operand...]
where the time goes in v5:
time: 51.9 us; the launch traced here: 51.7 us
  waiting for transfers between devices  22.7 us (44%)
  starting transfers between devices  17.6 us (34%)
  Pallas kernels  9.58 us (18%)
  local copies, waits for them, and re-layouts  1.02 us (2%)
  between operations  0.83 us (2%)
    pallas_call x13, Pallas kernels, local_call(): pl.pallas_call(body, out_shape=outs, in_specs=specs or [VM] * len(operand...  9.58 us
    ppermute x1, waiting for transfers between devices, paired_shards(): from_other = lax.ppermute(other_send, 'seq', across)  7.48 us
    ppermute x1, waiting for transfers between devices, paired_shards(): held = lax.ppermute(pred_weight[0], ('seq', 'grp'), ring)  6.98 us
    ppermute x1, waiting for transfers between devices, paired_shards(): mine = lax.ppermute(first, ('seq', 'grp'), ring)  5.96 us
    ppermute x2, starting transfers between devices, paired_shards(): first = lax.ppermute(first, ('seq', 'grp'), ring)  3.98 us
    ppermute x2, starting transfers between devices, paired_shards(): second = lax.ppermute(second, ('seq', 'grp'), ring)  3.65 us
    ppermute x1, starting transfers between devices, paired_shards(): held = lax.ppermute(pred_weight[0], ('seq', 'grp'), ring)  3.1 us
    ppermute x1, starting transfers between devices, paired_shards(): kept_other = lax.ppermute(send, 'seq', across)  1.56 us
  transfers between devices with their start and end apart: 17, of which 5 were waited for; matrix products, arithmetic and copies ran while one was open for 0% of the time, Pallas kernels for 15%

profile of v5, /device:TPU:0, one launch (start us, length us, event | category | flops | bytes accessed | tf_op | source)
XLA Modules:
  0.0 51.7 jit_solution(11958520938166781760)
XLA Ops:
  0.6 3.1 %collective-permute-start.7 = (bf16[704,384]{1,0:T(8,128)(2,1)}, bf16[704,384]{1,0:T(8,128)(2,1)S(1)}, u32[]{:S(2)}, u32[]{:S(2)}) collective-permute-start(bf16[704,384]{1,0:T(8,128)(2,1)} %bitcast.8), channel_id=1, source_target_pairs={{0,2},{2,4},{4,6},{6,7},{7,5},{5,3},{3,1},{1,0},{10,8},{12,10},{14... | collective-permute-start | bytes 1622024 | tf_op jit(solution)/shard_map/ppermute | solution.py:481
  3.7 0.5 collective-permute-start.1
  4.2 7.0 %collective-permute-done.7.refs_1_.whole = bf16[704,384]{1,0:T(8,128)(2,1)S(1)} collective-permute-done((bf16[704,384]{1,0:T(8,128)(2,1)}, bf16[704,384]{1,0:T(8,128)(2,1)S(1)}, u32[]{:S(2)}, u32[]{:S(2)}) %collective-permute-start.7) | collective-permute-done | bytes 540704 | tf_op jit(solution)/shard_map/ppermute | solution.py:481
  11.3 2.1 %collective-permute-start.9 = (bf16[352,384]{1,0:T(8,128)(2,1)S(1)}, bf16[352,384]{1,0:T(8,128)(2,1)S(1)}, u32[]{:S(2)}, u32[]{:S(2)}) collective-permute-start(bf16[352,384]{1,0:T(8,128)(2,1)S(1)} %get-tuple-element.43), channel_id=1, source_target_pairs={{0,2},{2,4},{4,6},{6,7},{7,5},{5,3},{3,1},{1,0},{10,8},{12,10},{14... | collective-permute-start | bytes 811016 | tf_op jit(solution)/shard_map/ppermute | solution.py:484
  13.4 1.6 %collective-permute-start.10 = (bf16[352,384]{1,0:T(8,128)(2,1)S(1)}, bf16[352,384]{1,0:T(8,128)(2,1)S(1)}, u32[]{:S(2)}, u32[]{:S(2)}) collective-permute-start(bf16[352,384]{1,0:T(8,128)(2,1)S(1)} %get-tuple-element.44), channel_id=1, source_target_pairs={{0,2},{2,4},{4,6},{6,7},{7,5},{5,3},{3,1},{1,0},{10,8},{12,10},{14... | collective-permute-start | bytes 811016 | tf_op jit(solution)/shard_map/ppermute | solution.py:485
  15.0 1.0 %copy-done.7 = bf16[1,128,1408]{2,1,0:T(8,128)(2,1)S(1)} copy-done((bf16[1,128,1408]{2,1,0:T(8,128)(2,1)S(1)}, bf16[1,128,1408]{2,1,0:T(8,128)(2,1)}, u32[]{:S(2)}) %copy-start.7) | copy-done | bytes 360472
  16.0 0.5 shard_map.103
  16.5 1.6 %collective-permute-start.2 = (bf16[128,704]{1,0:T(8,128)(2,1)S(1)}, bf16[128,704]{1,0:T(8,128)(2,1)S(1)}, u32[]{:S(2)}, u32[]{:S(2)}) collective-permute-start(bf16[128,704]{1,0:T(8,128)(2,1)S(1)} %get-tuple-element.33), channel_id=1, source_target_pairs={{0,16},{8,24},{16,0},{24,8},{1,17},{9,25},{17,1},{25,9},{2,18},{10... | collective-permute-start | bytes 540680 | tf_op jit(solution)/shard_map/ppermute | solution.py:437
  18.0 1.8 %collective-permute-start.12 = (bf16[352,384]{1,0:T(8,128)(2,1)S(1)}, bf16[352,384]{1,0:T(8,128)(2,1)S(1)}, u32[]{:S(2)}, u32[]{:S(2)}) collective-permute-start(bf16[352,384]{1,0:T(8,128)(2,1)S(1)} %collective-permute-done.9.first), channel_id=1, source_target_pairs={{0,2},{2,4},{4,6},{6,7},{7,5},{5,3},{3,1},{1,0},{10,8},{12,10},{14... | collective-permute-start | bytes 811016 | tf_op jit(solution)/shard_map/ppermute | solution.py:484
  19.9 0.8 %collective-permute-done.10.second = bf16[352,384]{1,0:T(8,128)(2,1)S(1)} collective-permute-done((bf16[352,384]{1,0:T(8,128)(2,1)S(1)}, bf16[352,384]{1,0:T(8,128)(2,1)S(1)}, u32[]{:S(2)}, u32[]{:S(2)}) %collective-permute-start.10) | collective-permute-done | bytes 270368 | tf_op jit(solution)/shard_map/ppermute | solution.py:485
  20.7 2.1 %collective-permute-start.13 = (bf16[352,384]{1,0:T(8,128)(2,1)S(1)}, bf16[352,384]{1,0:T(8,128)(2,1)S(1)}, u32[]{:S(2)}, u32[]{:S(2)}) collective-permute-start(bf16[352,384]{1,0:T(8,128)(2,1)S(1)} %collective-permute-done.10.second), channel_id=1, source_target_pairs={{0,2},{2,4},{4,6},{6,7},{7,5},{5,3},{3,1},{1,0},{10,8},{12,10},{14... | collective-permute-start | bytes 811016 | tf_op jit(solution)/shard_map/ppermute | solution.py:485
  22.8 2.6 %shard_map.104 = (bf16[704,1408]{1,0:T(8,128)(2,1)S(1)}, f32[128,768]{1,0:T(8,128)S(1)}, bf16[128,384]{1,0:T(8,128)(2,1)S(1)}, bf16[128,1152]{1,0:T(8,128)(2,1)S(1)}, bf16[352,1408]{1,0:T(8,128)(2,1)}) custom-call(bf16[352,1408]{1,0:T(8,128)(2,1)S(1)} %copy-done.2, bf16[352,1408]{1,0:T(8,128)(2,1)S(1)} %copy-done.3, ...), custom_call_target="tpu_custom_call" | custom-call | flops 507510784 | bytes 3964928 | tf_op jit(solution)/shard_map/pallas_call | solution.py:146
  25.4 1.6 %collective-permute-start.4 = (bf16[128,1152]{1,0:T(8,128)(2,1)S(1)}, bf16[128,1152]{1,0:T(8,128)(2,1)S(1)}, u32[]{:S(2)}, u32[]{:S(2)}) collective-permute-start(bf16[128,1152]{1,0:T(8,128)(2,1)S(1)} %get-tuple-element.37), channel_id=1, source_target_pairs={{0,16},{8,24},{16,0},{24,8},{1,17},{9,25},{17,1},{25,9},{2,18},{10... | collective-permute-start | bytes 884744 | tf_op jit(solution)/shard_map/ppermute | solution.py:452
  26.9 0.5 shard_map.106
  27.4 0.6 %collective-permute-start.3 = (bf16[128,768]{1,0:T(8,128)(2,1)S(1)}, bf16[128,768]{1,0:T(8,128)(2,1)S(1)}, u32[]{:S(2)}, u32[]{:S(2)}) collective-permute-start(bf16[128,768]{1,0:T(8,128)(2,1)S(1)} %get-tuple-element.36), channel_id=1, source_target_pairs={{0,16},{8,24},{16,0},{24,8},{1,17},{9,25},{17,1},{25,9},{2,18},{10... | collective-permute-start | bytes 589832 | tf_op jit(solution)/shard_map/ppermute | solution.py:459
  28.2 0.6 %collective-permute-start.11 = (bf16[704,384]{1,0:T(8,128)(2,1)S(1)}, bf16[704,384]{1,0:T(8,128)(2,1)S(1)}, u32[]{:S(2)}, u32[]{:S(2)}) collective-permute-start(bf16[704,384]{1,0:T(8,128)(2,1)S(1)} %shard_map.111.refs_0_.refs_3_), channel_id=1, source_target_pairs={{0,8},{8,0},{16,24},{24,16},{1,9},{9,1},{17,25},{25,17},{2,10},{10... | collective-permute-start | bytes 1622024 | tf_op jit(solution)/shard_map/ppermute | solution.py:487
  28.9 7.5 %collective-permute-done.3.from_other = bf16[128,768]{1,0:T(8,128)(2,1)S(1)} collective-permute-done((bf16[128,768]{1,0:T(8,128)(2,1)S(1)}, bf16[128,768]{1,0:T(8,128)(2,1)S(1)}, u32[]{:S(2)}, u32[]{:S(2)}) %collective-permute-start.3) | collective-permute-done | bytes 196640 | tf_op jit(solution)/shard_map/ppermute | solution.py:459
  36.9 6.0 %collective-permute-done.15.mine = bf16[352,384]{1,0:T(8,128)(2,1)S(1)} collective-permute-done((bf16[352,384]{1,0:T(8,128)(2,1)S(1)}, bf16[352,384]{1,0:T(8,128)(2,1)S(1)}, u32[]{:S(2)}, u32[]{:S(2)}) %collective-permute-start.15) | collective-permute-done | bytes 270368 | tf_op jit(solution)/shard_map/ppermute | solution.py:490
  42.9 1.6 %shard_map.108 = (f32[128,384]{1,0:T(8,128)S(1)}, bf16[128,384]{1,0:T(8,128)(2,1)S(1)}) custom-call(bf16[256,384]{1,0:T(8,128)(2,1)S(1)} %get-tuple-element.39.queries, bf16[256,768]{1,0:T(8,128)(2,1)S(1)} %get-tuple-element.40.kv_a, bf16[256,768]{1,0:T(8,128)(2,1)S(1)} %collective-permute-done.5.kv_b), custom_call_target="tpu_custom_call" | custom-call | flops 402653184 | bytes 1572864 | tf_op jit(solution)/shard_map/pallas_call | solution.py:146
  44.4 1.6 %collective-permute-start.6 = (bf16[128,384]{1,0:T(8,128)(2,1)S(1)}, bf16[128,384]{1,0:T(8,128)(2,1)S(1)}, u32[]{:S(2)}, u32[]{:S(2)}) collective-permute-start(bf16[128,384]{1,0:T(8,128)(2,1)S(1)} %get-tuple-element.42), channel_id=1, source_target_pairs={{0,16},{8,24},{16,0},{24,8},{1,17},{9,25},{17,1},{25,9},{2,18},{10... | collective-permute-start | bytes 294920 | tf_op jit(solution)/shard_map/ppermute | solution.py:472
  46.2 0.7 %shard_map.109.earlier = f32[128,704]{1,0:T(8,128)S(1)} custom-call(s32[128,128]{1,0:T(8,128)S(1)} %get-tuple-element.29.ids, f32[128,384]{1,0:T(8,128)S(1)} %get-tuple-element.30.normed, bf16[704,384]{1,0:T(8,128)(2,1)S(1)} %bitcast.9, bf16[704,384]{1,0:T(8,128)(2,1)S(1)} %collective-permute-done.7.refs_1_.whole, ...), custom_call_target="tpu_custom_call" | custom-call | flops 207618048 | bytes 1622016 | tf_op jit(solution)/shard_map/pallas_call | solution.py:146
  47.0 0.9 %shard_map.113.earlier = f32[128,704]{1,0:T(8,128)S(1)} custom-call(s32[128,128]{1,0:T(8,128)S(1)} %get-tuple-element.29.ids, f32[128,384]{1,0:T(8,128)S(1)} %get-tuple-element.30.normed, f32[128,704]{1,0:T(8,128)S(1)} %shard_map.109.earlier, bf16[704,384]{1,0:T(8,128)(2,1)S(1)} %shard_map.111.refs_0_.refs_3_, ...), custom_call_target="tpu_custom_call" | custom-call | flops 276824064 | bytes 2162688 | tf_op jit(solution)/shard_map/pallas_call | solution.py:146
  48.3 1.4 %collective-permute-done.6.returned = bf16[128,384]{1,0:T(8,128)(2,1)S(1)} collective-permute-done((bf16[128,384]{1,0:T(8,128)(2,1)S(1)}, bf16[128,384]{1,0:T(8,128)(2,1)S(1)}, u32[]{:S(2)}, u32[]{:S(2)}) %collective-permute-start.6) | collective-permute-done | bytes 98336 | tf_op jit(solution)/shard_map/ppermute | solution.py:472
  49.7 2.0 %shard_map.115 = (bf16[704,128]{1,0:T(8,128)(2,1)}, bf16[128,384]{1,0:T(8,128)(2,1)}) custom-call(s32[128,128]{1,0:T(8,128)S(1)} %get-tuple-element.29.ids, f32[128,384]{1,0:T(8,128)S(1)} %get-tuple-element.30.normed, f32[128,128]{1,0:T(8,128)S(1)} %get-tuple-element.31.factor, f32[128,384]{1,0:T(8,128)S(1)} %get-tuple-element.41.attended, ...), custom_call_target="tpu_custom_call" | custom-call | flops 553648128 | bytes 4325376 | tf_op jit(solution)/shard_map/pallas_call | solution.py:146
  (39 shorter events, 1.4 us)
Async XLA Ops:
  0.6 10.6 %collective-permute-start.7 = (bf16[704,384]{1,0:T(8,128)(2,1)}, bf16[704,384]{1,0:T(8,128)(2,1)S(1)}, u32[]{:S(2)}, u32[]{:S(2)}) collective-permute-start(bf16[704,384]{1,0:T(8,128)(2,1)} %bitcast.8), channel_id=1, source_target_pairs={{0,2},{2,4},{4,6},{6,7},{7,5},{5,3},{3,1},{1,0},{10,8},{12,10},{14... | collective-permute-start | bytes 1622024 | tf_op jit(solution)/shard_map/ppermute | solution.py:481
  3.7 19.0 %collective-permute-start = (bf16[352,1408]{1,0:T(8,128)(2,1)}, bf16[352,1408]{1,0:T(8,128)(2,1)S(1)}, u32[]{:S(2)}, u32[]{:S(2)}) collective-permute-start(bf16[352,1408]{1,0:T(8,128)(2,1)} %target.1), channel_id=1, source_target_pairs={{0,8},{8,0},{16,24},{24,16},{1,9},{9,1},{17,25},{25,17},{2,10},{10... | collective-permute-start | bytes 2973704 | tf_op jit(solution)/shard_map/ppermute | solution.py:429
  3.7 19.0 %collective-permute-start.1 = (bf16[352,1408]{1,0:T(8,128)(2,1)}, bf16[352,1408]{1,0:T(8,128)(2,1)S(1)}, u32[]{:S(2)}, u32[]{:S(2)}) collective-permute-start(bf16[352,1408]{1,0:T(8,128)(2,1)} %context.1), channel_id=1, source_target_pairs={{0,8},{8,0},{16,24},{24,16},{1,9},{9,1},{17,25},{25,17},{2,10},{10... | collective-permute-start | bytes 2973704 | tf_op jit(solution)/shard_map/ppermute | solution.py:430
  11.3 6.7 %collective-permute-start.9 = (bf16[352,384]{1,0:T(8,128)(2,1)S(1)}, bf16[352,384]{1,0:T(8,128)(2,1)S(1)}, u32[]{:S(2)}, u32[]{:S(2)}) collective-permute-start(bf16[352,384]{1,0:T(8,128)(2,1)S(1)} %get-tuple-element.43), channel_id=1, source_target_pairs={{0,2},{2,4},{4,6},{6,7},{7,5},{5,3},{3,1},{1,0},{10,8},{12,10},{14... | collective-permute-start | bytes 811016 | tf_op jit(solution)/shard_map/ppermute | solution.py:484
  13.4 7.3 %collective-permute-start.10 = (bf16[352,384]{1,0:T(8,128)(2,1)S(1)}, bf16[352,384]{1,0:T(8,128)(2,1)S(1)}, u32[]{:S(2)}, u32[]{:S(2)}) collective-permute-start(bf16[352,384]{1,0:T(8,128)(2,1)S(1)} %get-tuple-element.44), channel_id=1, source_target_pairs={{0,2},{2,4},{4,6},{6,7},{7,5},{5,3},{3,1},{1,0},{10,8},{12,10},{14... | collective-permute-start | bytes 811016 | tf_op jit(solution)/shard_map/ppermute | solution.py:485
  16.0 6.8 %copy-start.1 = (bf16[704,1408]{1,0:T(8,128)(2,1)S(1)}, bf16[704,1408]{1,0:T(8,128)(2,1)}, u32[]{:S(2)}) copy-start(bf16[704,1408]{1,0:T(8,128)(2,1)} %query_weight.1) | copy-start | bytes 5947396
  16.0 6.8 %copy-start.2 = (bf16[352,1408]{1,0:T(8,128)(2,1)S(1)}, bf16[352,1408]{1,0:T(8,128)(2,1)}, u32[]{:S(2)}) copy-start(bf16[352,1408]{1,0:T(8,128)(2,1)} %target.1) | copy-start | bytes 2973700
  16.0 6.8 %copy-start.3 = (bf16[352,1408]{1,0:T(8,128)(2,1)S(1)}, bf16[352,1408]{1,0:T(8,128)(2,1)}, u32[]{:S(2)}) copy-start(bf16[352,1408]{1,0:T(8,128)(2,1)} %context.1) | copy-start | bytes 2973700
  16.5 10.5 %collective-permute-start.2 = (bf16[128,704]{1,0:T(8,128)(2,1)S(1)}, bf16[128,704]{1,0:T(8,128)(2,1)S(1)}, u32[]{:S(2)}, u32[]{:S(2)}) collective-permute-start(bf16[128,704]{1,0:T(8,128)(2,1)S(1)} %get-tuple-element.33), channel_id=1, source_target_pairs={{0,16},{8,24},{16,0},{24,8},{1,17},{9,25},{17,1},{25,9},{2,18},{10... | collective-permute-start | bytes 540680 | tf_op jit(solution)/shard_map/ppermute | solution.py:437
  18.0 10.1 %collective-permute-start.12 = (bf16[352,384]{1,0:T(8,128)(2,1)S(1)}, bf16[352,384]{1,0:T(8,128)(2,1)S(1)}, u32[]{:S(2)}, u32[]{:S(2)}) collective-permute-start(bf16[352,384]{1,0:T(8,128)(2,1)S(1)} %collective-permute-done.9.first), channel_id=1, source_target_pairs={{0,2},{2,4},{4,6},{6,7},{7,5},{5,3},{3,1},{1,0},{10,8},{12,10},{14... | collective-permute-start | bytes 811016 | tf_op jit(solution)/shard_map/ppermute | solution.py:484
  20.7 8.1 %collective-permute-start.13 = (bf16[352,384]{1,0:T(8,128)(2,1)S(1)}, bf16[352,384]{1,0:T(8,128)(2,1)S(1)}, u32[]{:S(2)}, u32[]{:S(2)}) collective-permute-start(bf16[352,384]{1,0:T(8,128)(2,1)S(1)} %collective-permute-done.10.second), channel_id=1, source_target_pairs={{0,2},{2,4},{4,6},{6,7},{7,5},{5,3},{3,1},{1,0},{10,8},{12,10},{14... | collective-permute-start | bytes 811016 | tf_op jit(solution)/shard_map/ppermute | solution.py:485
  25.4 11.3 %collective-permute-start.4 = (bf16[128,1152]{1,0:T(8,128)(2,1)S(1)}, bf16[128,1152]{1,0:T(8,128)(2,1)S(1)}, u32[]{:S(2)}, u32[]{:S(2)}) collective-permute-start(bf16[128,1152]{1,0:T(8,128)(2,1)S(1)} %get-tuple-element.37), channel_id=1, source_target_pairs={{0,16},{8,24},{16,0},{24,8},{1,17},{9,25},{17,1},{25,9},{2,18},{10... | collective-permute-start | bytes 884744 | tf_op jit(solution)/shard_map/ppermute | solution.py:452
  27.4 9.0 %collective-permute-start.3 = (bf16[128,768]{1,0:T(8,128)(2,1)S(1)}, bf16[128,768]{1,0:T(8,128)(2,1)S(1)}, u32[]{:S(2)}, u32[]{:S(2)}) collective-permute-start(bf16[128,768]{1,0:T(8,128)(2,1)S(1)} %get-tuple-element.36), channel_id=1, source_target_pairs={{0,16},{8,24},{16,0},{24,8},{1,17},{9,25},{17,1},{25,9},{2,18},{10... | collective-permute-start | bytes 589832 | tf_op jit(solution)/shard_map/ppermute | solution.py:459
  28.0 18.2 %collective-permute-start.8 = (bf16[704,384]{1,0:T(8,128)(2,1)S(1)}, bf16[704,384]{1,0:T(8,128)(2,1)S(1)}, u32[]{:S(2)}, u32[]{:S(2)}) collective-permute-start(bf16[704,384]{1,0:T(8,128)(2,1)S(1)} %collective-permute-done.7.refs_1_.whole), channel_id=1, source_target_pairs={{0,8},{8,0},{16,24},{24,16},{1,9},{9,1},{17,25},{25,17},{2,10},{10... | collective-permute-start | bytes 1622024 | tf_op jit(solution)/shard_map/ppermute | solution.py:487
  28.1 17.9 %copy-start.4 = (bf16[1,128,384]{2,1,0:T(8,128)(2,1)S(1)}, bf16[1,128,384]{2,1,0:T(8,128)(2,1)}, u32[]{:S(2)}) copy-start(bf16[1,128,384]{2,1,0:T(8,128)(2,1)} %param.12) | copy-start | bytes 294916
  28.1 17.9 %copy-start.5 = (s32[1,64,1]{1,2,0:T(1,128)S(1)}, s32[1,64,1]{1,2,0:T(1,128)}, u32[]{:S(2)}) copy-start(s32[1,64,1]{1,2,0:T(1,128)} %param.15) | copy-start | bytes 772
  28.1 17.9 %copy-start.6 = (s32[1,64]{1,0:T(1,128)S(1)}, s32[1,64]{1,0:T(1,128)}, u32[]{:S(2)}) copy-start(s32[1,64]{1,0:T(1,128)} %mask.1) | copy-start | bytes 772
  28.1 18.1 %copy-start = (bf16[1,704,384]{2,1,0:T(8,128)(2,1)S(1)}, bf16[1,704,384]{2,1,0:T(8,128)(2,1)}, u32[]{:S(2)}) copy-start(bf16[1,704,384]{2,1,0:T(8,128)(2,1)} %param.13) | copy-start | bytes 1622020
  28.2 18.8 %collective-permute-start.11 = (bf16[704,384]{1,0:T(8,128)(2,1)S(1)}, bf16[704,384]{1,0:T(8,128)(2,1)S(1)}, u32[]{:S(2)}, u32[]{:S(2)}) collective-permute-start(bf16[704,384]{1,0:T(8,128)(2,1)S(1)} %shard_map.111.refs_0_.refs_3_), channel_id=1, source_target_pairs={{0,8},{8,0},{16,24},{24,16},{1,9},{9,1},{17,25},{25,17},{2,10},{10... | collective-permute-start | bytes 1622024 | tf_op jit(solution)/shard_map/ppermute | solution.py:487
  28.8 18.2 %collective-permute-start.14 = (bf16[704,384]{1,0:T(8,128)(2,1)S(1)}, bf16[704,384]{1,0:T(8,128)(2,1)S(1)}, u32[]{:S(2)}, u32[]{:S(2)}) collective-permute-start(bf16[704,384]{1,0:T(8,128)(2,1)S(1)} %shard_map.112.refs_2_.refs_5_), channel_id=1, source_target_pairs={{0,8},{8,0},{16,24},{24,16},{1,9},{9,1},{17,25},{25,17},{2,10},{10... | collective-permute-start | bytes 1622024 | tf_op jit(solution)/shard_map/ppermute | solution.py:487
  36.4 6.5 %collective-permute-start.15 = (bf16[352,384]{1,0:T(8,128)(2,1)S(1)}, bf16[352,384]{1,0:T(8,128)(2,1)S(1)}, u32[]{:S(2)}, u32[]{:S(2)}) collective-permute-start(bf16[352,384]{1,0:T(8,128)(2,1)S(1)} %collective-permute-done.12.first), channel_id=1, source_target_pairs={{0,2},{2,4},{4,6},{6,7},{7,5},{5,3},{3,1},{1,0},{10,8},{12,10},{14... | collective-permute-start | bytes 811016 | tf_op jit(solution)/shard_map/ppermute | solution.py:490
  36.8 6.0 %collective-permute-start.5 = (bf16[256,768]{1,0:T(8,128)(2,1)S(1)}, bf16[256,768]{1,0:T(8,128)(2,1)S(1)}, u32[]{:S(2)}, u32[]{:S(2)}) collective-permute-start(bf16[256,768]{1,0:T(8,128)(2,1)S(1)} %get-tuple-element.40.kv_a), channel_id=1, source_target_pairs={{0,8},{8,0},{16,24},{24,16},{1,9},{9,1},{17,25},{25,17},{2,10},{10... | collective-permute-start | bytes 1179656 | tf_op jit(solution)/shard_map/ppermute | solution.py:465
  42.8 5.0 %collective-permute-start.16 = (bf16[352,384]{1,0:T(8,128)(2,1)S(1)}, bf16[352,384]{1,0:T(8,128)(2,1)S(1)}, u32[]{:S(2)}, u32[]{:S(2)}) collective-permute-start(bf16[352,384]{1,0:T(8,128)(2,1)S(1)} %collective-permute-done.15.mine), channel_id=1, source_target_pairs={{0,8},{8,0},{16,24},{24,16},{1,9},{9,1},{17,25},{25,17},{2,10},{10... | collective-permute-start | bytes 811016 | tf_op jit(solution)/shard_map/ppermute | solution.py:491
  44.4 5.3 %collective-permute-start.6 = (bf16[128,384]{1,0:T(8,128)(2,1)S(1)}, bf16[128,384]{1,0:T(8,128)(2,1)S(1)}, u32[]{:S(2)}, u32[]{:S(2)}) collective-permute-start(bf16[128,384]{1,0:T(8,128)(2,1)S(1)} %get-tuple-element.42), channel_id=1, source_target_pairs={{0,16},{8,24},{16,0},{24,8},{1,17},{9,25},{17,1},{25,9},{2,18},{10... | collective-permute-start | bytes 294920 | tf_op jit(solution)/shard_map/ppermute | solution.py:472
  (1 other events, 1.0 us)

commit v6 on v5

--- a/solution.py
+++ b/solution.py
@@ -202,26 +202,15 @@
         other[:, t * LANES : (t + 1) * LANES] = theirs[t].astype(jnp.bfloat16)
 
 
-def blend(target, context):
-    return (
-        keep_rate * target[...].astype(jnp.float32)
-        + (1.0 - keep_rate) * context[...].astype(jnp.float32)
-    ).astype(jnp.bfloat16)
-
-
 def first_partial_body(
-    target, context, other_target, other_context, rows, normed, query_weight,
-    joined, own, q_own, send, stored, sem,
+    own_weight, other_weight, rows, normed, query_weight, joined, own, q_own, send, stored, sem
 ):
     chip, core = chip_and_core()
-    depth = target.shape[0]
-    own_rows = pl.ds(pl.multiple_of(core * depth, 16), depth)
-    joined[own_rows, :] = blend(target, context)
-    joined[pl.ds(pl.multiple_of((1 - core) * depth, 16), depth), :] = blend(
-        other_target, other_context
-    )
-    store = pltpu.make_async_copy(joined.at[own_rows], stored, sem)
+    depth = own_weight.shape[0]
+    store = pltpu.make_async_copy(own_weight, stored, sem)
     store.start()
+    joined[pl.ds(pl.multiple_of(core * depth, 16), depth), :] = own_weight[...]
+    joined[pl.ds(pl.multiple_of((1 - core) * depth, 16), depth), :] = other_weight[...]
     split_product(rows, joined, own, send)
     queries = lax.dot_general(
         normed[...], query_weight[...], (((1,), (1,)), ((), ())), preferred_element_type=jnp.float32
@@ -426,14 +415,16 @@
     owner_row, mask_row = owners.reshape(1, -1), target_mask.reshape(1, -1)
     sums_shape = shape_of((rows, 2 * packed), jnp.float32)
 
-    other_target = lax.ppermute(target_kv, "seq", beside)
-    other_context = lax.ppermute(context_kv, "seq", beside)
+    new_kv = (
+        keep_rate * target_kv.astype(jnp.float32)
+        + (1.0 - keep_rate) * context_kv.astype(jnp.float32)
+    ).astype(jnp.bfloat16)
     normed, keep, send = local_call(
         norm_body,
         [shape_of((rows, features)), shape_of((rows, half)), shape_of((rows, half))],
         (tokens[0],),
-        cost=pl.CostEstimate(flops=1 << 33, bytes_accessed=1 << 20, transcendentals=0),
-    )
+    )
+    other_kv = lax.ppermute(new_kv, "seq", beside)
     kept_other = lax.ppermute(send, "seq", across)
     joined, own_sum, q_own, own_send, stored_kv = local_call(
         first_partial_body,
@@ -444,7 +435,7 @@
             shape_of((rows, 3 * packed)),
             shape_of(target_kv.shape),
         ],
-        (target_kv, context_kv, other_target, other_context, keep, normed, query_weight),
+        (new_kv, other_kv, keep, normed, query_weight),
         out_specs=[VM] * 4 + [HBM],
         scratch=[pltpu.SemaphoreType.DMA],
         cost=matmul_cost(rows, half, 4 * width),

time: 51.9 us -> 53.4 us (1.029)
  other arithmetic: 0 us -> 2.01 us
  waiting for transfers between devices: 22.7 us -> 24.3 us
  local copies, waits for them, and re-layouts: 1.02 us -> 0.03 us
  Pallas kernels: 9.58 us -> 8.66 us
    convert_element_type x0 -> x1, other arithmetic: none -> 2.01 us  [paired_shards(): new_kv = (keep_rate * target_kv.astype(jnp.float32) + (1.0 - keep_rate) *...]
    unnamed x16 -> x12, local copies, waits for them, and re-layouts: 1.02 us -> 0.03 us
    pallas_call x13, Pallas kernels: 9.58 us -> 8.66 us  [local_call(): pl.pallas_call(body, out_shape=outs, in_specs=specs or [VM] * len(operand...]
    ppermute x2, waiting for transfers between devices: 0.01 us -> 0.77 us  [paired_shards(): first = lax.ppermute(first, ('seq', 'grp'), ring)]
    ppermute x1, waiting for transfers between devices: 7.48 us -> 8.08 us  [paired_shards(): from_other = lax.ppermute(other_send, 'seq', across)]
  transfers between devices with their start and end apart: 17 -> 16, of which waited for: 5 -> 6; matrix products, arithmetic and copies ran while one was open for 0% -> 0% of each run, Pallas kernels for 15% -> 13%
where the time goes in v6:
time: 53.4 us; the launch traced here: 53.3 us
  waiting for transfers between devices  24.3 us (46%)
  starting transfers between devices  17.5 us (33%)
  Pallas kernels  8.66 us (16%)
  other arithmetic  2.01 us (4%)
  between operations  0.81 us (2%)
    pallas_call x13, Pallas kernels, local_call(): pl.pallas_call(body, out_shape=outs, in_specs=specs or [VM] * len(operand...  8.66 us
    ppermute x1, waiting for transfers between devices, paired_shards(): from_other = lax.ppermute(other_send, 'seq', across)  8.08 us
    ppermute x1, waiting for transfers between devices, paired_shards(): held = lax.ppermute(pred_weight[0], ('seq', 'grp'), ring)  7.28 us
    ppermute x1, waiting for transfers between devices, paired_shards(): mine = lax.ppermute(first, ('seq', 'grp'), ring)  5.85 us
    ppermute x2, starting transfers between devices, paired_shards(): first = lax.ppermute(first, ('seq', 'grp'), ring)  4.21 us
    ppermute x2, starting transfers between devices, paired_shards(): second = lax.ppermute(second, ('seq', 'grp'), ring)  3.65 us
    ppermute x1, starting transfers between devices, paired_shards(): held = lax.ppermute(pred_weight[0], ('seq', 'grp'), ring)  2.63 us
    convert_element_type x1, other arithmetic, paired_shards(): new_kv = (keep_rate * target_kv.astype(jnp.float32) + (1.0 - keep_rate) *...  2.01 us
  transfers between devices with their start and end apart: 16, of which 6 were waited for; matrix products, arithmetic and copies ran while one was open for 0% of the time, Pallas kernels for 13%

profile of v6, /device:TPU:0, one launch (start us, length us, event | category | flops | bytes accessed | tf_op | source)
XLA Modules:
  0.0 53.3 jit_solution(9560757073589799584)
XLA Ops:
  0.7 2.0 %add_convert_fusion.own_weight = bf16[352,1408]{1,0:T(8,128)(2,1)S(1)} fusion(bf16[352,1408]{1,0:T(8,128)(2,1)} %param.10, bf16[352,1408]{1,0:T(8,128)(2,1)} %param.9), kind=kLoop, calls=%fused_computation | loop fusion | flops 2973696 | bytes 2973696 | tf_op jit(solution)/shard_map/convert_element_type | solution.py:421
  2.7 0.6 %collective-permute-start = (bf16[352,1408]{1,0:T(8,128)(2,1)S(1)}, bf16[352,1408]{1,0:T(8,128)(2,1)S(1)}, u32[]{:S(2)}, u32[]{:S(2)}) collective-permute-start(bf16[352,1408]{1,0:T(8,128)(2,1)S(1)} %add_convert_fusion.own_weight), channel_id=1, source_target_pairs={{0,8},{8,0},{16,24},{24,16},{1,9},{9,1},{17,25},{25,17},{2,10},{10... | collective-permute-start | bytes 2973704 | tf_op jit(solution)/shard_map/ppermute | solution.py:427
  3.2 2.6 %collective-permute-start.6 = (bf16[704,384]{1,0:T(8,128)(2,1)S(1)}, bf16[704,384]{1,0:T(8,128)(2,1)S(1)}, u32[]{:S(2)}, u32[]{:S(2)}) collective-permute-start(bf16[704,384]{1,0:T(8,128)(2,1)S(1)} %bitcast.8), channel_id=1, source_target_pairs={{0,2},{2,4},{4,6},{6,7},{7,5},{5,3},{3,1},{1,0},{10,8},{12,10},{14... | collective-permute-start | bytes 1622024 | tf_op jit(solution)/shard_map/ppermute | solution.py:472
  5.9 7.3 %collective-permute-done.6.refs_1_.whole = bf16[704,384]{1,0:T(8,128)(2,1)S(1)} collective-permute-done((bf16[704,384]{1,0:T(8,128)(2,1)S(1)}, bf16[704,384]{1,0:T(8,128)(2,1)S(1)}, u32[]{:S(2)}, u32[]{:S(2)}) %collective-permute-start.6) | collective-permute-done | bytes 540704 | tf_op jit(solution)/shard_map/ppermute | solution.py:472
  13.2 2.1 %collective-permute-start.8 = (bf16[352,384]{1,0:T(8,128)(2,1)S(1)}, bf16[352,384]{1,0:T(8,128)(2,1)S(1)}, u32[]{:S(2)}, u32[]{:S(2)}) collective-permute-start(bf16[352,384]{1,0:T(8,128)(2,1)S(1)} %get-tuple-element.43), channel_id=1, source_target_pairs={{0,2},{2,4},{4,6},{6,7},{7,5},{5,3},{3,1},{1,0},{10,8},{12,10},{14... | collective-permute-start | bytes 811016 | tf_op jit(solution)/shard_map/ppermute | solution.py:475
  15.3 1.6 %collective-permute-start.9 = (bf16[352,384]{1,0:T(8,128)(2,1)S(1)}, bf16[352,384]{1,0:T(8,128)(2,1)S(1)}, u32[]{:S(2)}, u32[]{:S(2)}) collective-permute-start(bf16[352,384]{1,0:T(8,128)(2,1)S(1)} %get-tuple-element.44), channel_id=1, source_target_pairs={{0,2},{2,4},{4,6},{6,7},{7,5},{5,3},{3,1},{1,0},{10,8},{12,10},{14... | collective-permute-start | bytes 811016 | tf_op jit(solution)/shard_map/ppermute | solution.py:476
  17.4 1.6 %collective-permute-start.1 = (bf16[128,704]{1,0:T(8,128)(2,1)S(1)}, bf16[128,704]{1,0:T(8,128)(2,1)S(1)}, u32[]{:S(2)}, u32[]{:S(2)}) collective-permute-start(bf16[128,704]{1,0:T(8,128)(2,1)S(1)} %get-tuple-element.33), channel_id=1, source_target_pairs={{0,16},{8,24},{16,0},{24,8},{1,17},{9,25},{17,1},{25,9},{2,18},{10... | collective-permute-start | bytes 540680 | tf_op jit(solution)/shard_map/ppermute | solution.py:428
  18.9 0.8 %collective-permute-done.8.first = bf16[352,384]{1,0:T(8,128)(2,1)S(1)} collective-permute-done((bf16[352,384]{1,0:T(8,128)(2,1)S(1)}, bf16[352,384]{1,0:T(8,128)(2,1)S(1)}, u32[]{:S(2)}, u32[]{:S(2)}) %collective-permute-start.8) | collective-permute-done | bytes 270368 | tf_op jit(solution)/shard_map/ppermute | solution.py:475
  19.7 2.1 %collective-permute-start.11 = (bf16[352,384]{1,0:T(8,128)(2,1)S(1)}, bf16[352,384]{1,0:T(8,128)(2,1)S(1)}, u32[]{:S(2)}, u32[]{:S(2)}) collective-permute-start(bf16[352,384]{1,0:T(8,128)(2,1)S(1)} %collective-permute-done.8.first), channel_id=1, source_target_pairs={{0,2},{2,4},{4,6},{6,7},{7,5},{5,3},{3,1},{1,0},{10,8},{12,10},{14... | collective-permute-start | bytes 811016 | tf_op jit(solution)/shard_map/ppermute | solution.py:475
  21.8 0.8 %collective-permute-done.9.second = bf16[352,384]{1,0:T(8,128)(2,1)S(1)} collective-permute-done((bf16[352,384]{1,0:T(8,128)(2,1)S(1)}, bf16[352,384]{1,0:T(8,128)(2,1)S(1)}, u32[]{:S(2)}, u32[]{:S(2)}) %collective-permute-start.9) | collective-permute-done | bytes 270368 | tf_op jit(solution)/shard_map/ppermute | solution.py:476
  22.6 2.1 %collective-permute-start.12 = (bf16[352,384]{1,0:T(8,128)(2,1)S(1)}, bf16[352,384]{1,0:T(8,128)(2,1)S(1)}, u32[]{:S(2)}, u32[]{:S(2)}) collective-permute-start(bf16[352,384]{1,0:T(8,128)(2,1)S(1)} %collective-permute-done.9.second), channel_id=1, source_target_pairs={{0,2},{2,4},{4,6},{6,7},{7,5},{5,3},{3,1},{1,0},{10,8},{12,10},{14... | collective-permute-start | bytes 811016 | tf_op jit(solution)/shard_map/ppermute | solution.py:476
  24.7 1.7 %shard_map.104 = (bf16[704,1408]{1,0:T(8,128)(2,1)S(1)}, f32[128,768]{1,0:T(8,128)S(1)}, bf16[128,384]{1,0:T(8,128)(2,1)S(1)}, bf16[128,1152]{1,0:T(8,128)(2,1)S(1)}, bf16[352,1408]{1,0:T(8,128)(2,1)}) custom-call(bf16[352,1408]{1,0:T(8,128)(2,1)S(1)} %add_convert_fusion.own_weight, bf16[352,1408]{1,0:T(8,128)(2,1)S(1)} %collective-permute-done.other_weight, ...), custom_call_target="tpu_custom_call" | custom-call | flops 507510784 | bytes 3964928 | tf_op jit(solution)/shard_map/pallas_call | solution.py:146
  26.4 1.6 %collective-permute-start.3 = (bf16[128,1152]{1,0:T(8,128)(2,1)S(1)}, bf16[128,1152]{1,0:T(8,128)(2,1)S(1)}, u32[]{:S(2)}, u32[]{:S(2)}) collective-permute-start(bf16[128,1152]{1,0:T(8,128)(2,1)S(1)} %get-tuple-element.37), channel_id=1, source_target_pairs={{0,16},{8,24},{16,0},{24,8},{1,17},{9,25},{17,1},{25,9},{2,18},{10... | collective-permute-start | bytes 884744 | tf_op jit(solution)/shard_map/ppermute | solution.py:443
  27.9 0.5 shard_map.106
  28.4 0.6 %collective-permute-start.2 = (bf16[128,768]{1,0:T(8,128)(2,1)S(1)}, bf16[128,768]{1,0:T(8,128)(2,1)S(1)}, u32[]{:S(2)}, u32[]{:S(2)}) collective-permute-start(bf16[128,768]{1,0:T(8,128)(2,1)S(1)} %get-tuple-element.36), channel_id=1, source_target_pairs={{0,16},{8,24},{16,0},{24,8},{1,17},{9,25},{17,1},{25,9},{2,18},{10... | collective-permute-start | bytes 589832 | tf_op jit(solution)/shard_map/ppermute | solution.py:450
  29.1 0.6 %collective-permute-start.10 = (bf16[704,384]{1,0:T(8,128)(2,1)S(1)}, bf16[704,384]{1,0:T(8,128)(2,1)S(1)}, u32[]{:S(2)}, u32[]{:S(2)}) collective-permute-start(bf16[704,384]{1,0:T(8,128)(2,1)S(1)} %shard_map.111.refs_0_.refs_3_), channel_id=1, source_target_pairs={{0,8},{8,0},{16,24},{24,16},{1,9},{9,1},{17,25},{25,17},{2,10},{10... | collective-permute-start | bytes 1622024 | tf_op jit(solution)/shard_map/ppermute | solution.py:478
  29.9 8.1 %collective-permute-done.2.from_other = bf16[128,768]{1,0:T(8,128)(2,1)S(1)} collective-permute-done((bf16[128,768]{1,0:T(8,128)(2,1)S(1)}, bf16[128,768]{1,0:T(8,128)(2,1)S(1)}, u32[]{:S(2)}, u32[]{:S(2)}) %collective-permute-start.2) | collective-permute-done | bytes 196640 | tf_op jit(solution)/shard_map/ppermute | solution.py:450
  38.6 5.9 %collective-permute-done.14.mine = bf16[352,384]{1,0:T(8,128)(2,1)S(1)} collective-permute-done((bf16[352,384]{1,0:T(8,128)(2,1)S(1)}, bf16[352,384]{1,0:T(8,128)(2,1)S(1)}, u32[]{:S(2)}, u32[]{:S(2)}) %collective-permute-start.14) | collective-permute-done | bytes 270368 | tf_op jit(solution)/shard_map/ppermute | solution.py:481
  44.4 1.6 %shard_map.108 = (f32[128,384]{1,0:T(8,128)S(1)}, bf16[128,384]{1,0:T(8,128)(2,1)S(1)}) custom-call(bf16[256,384]{1,0:T(8,128)(2,1)S(1)} %get-tuple-element.39.queries, bf16[256,768]{1,0:T(8,128)(2,1)S(1)} %get-tuple-element.40.kv_a, bf16[256,768]{1,0:T(8,128)(2,1)S(1)} %collective-permute-done.4.kv_b), custom_call_target="tpu_custom_call" | custom-call | flops 402653184 | bytes 1572864 | tf_op jit(solution)/shard_map/pallas_call | solution.py:146
  46.0 1.6 %collective-permute-start.5 = (bf16[128,384]{1,0:T(8,128)(2,1)S(1)}, bf16[128,384]{1,0:T(8,128)(2,1)S(1)}, u32[]{:S(2)}, u32[]{:S(2)}) collective-permute-start(bf16[128,384]{1,0:T(8,128)(2,1)S(1)} %get-tuple-element.42), channel_id=1, source_target_pairs={{0,16},{8,24},{16,0},{24,8},{1,17},{9,25},{17,1},{25,9},{2,18},{10... | collective-permute-start | bytes 294920 | tf_op jit(solution)/shard_map/ppermute | solution.py:463
  47.8 0.7 %shard_map.109.earlier = f32[128,704]{1,0:T(8,128)S(1)} custom-call(s32[128,128]{1,0:T(8,128)S(1)} %get-tuple-element.29.ids, f32[128,384]{1,0:T(8,128)S(1)} %get-tuple-element.30.normed, bf16[704,384]{1,0:T(8,128)(2,1)S(1)} %bitcast.9, bf16[704,384]{1,0:T(8,128)(2,1)S(1)} %collective-permute-done.6.refs_1_.whole, ...), custom_call_target="tpu_custom_call" | custom-call | flops 207618048 | bytes 1622016 | tf_op jit(solution)/shard_map/pallas_call | solution.py:146
  48.5 0.9 %shard_map.113.earlier = f32[128,704]{1,0:T(8,128)S(1)} custom-call(s32[128,128]{1,0:T(8,128)S(1)} %get-tuple-element.29.ids, f32[128,384]{1,0:T(8,128)S(1)} %get-tuple-element.30.normed, f32[128,704]{1,0:T(8,128)S(1)} %shard_map.109.earlier, bf16[704,384]{1,0:T(8,128)(2,1)S(1)} %shard_map.111.refs_0_.refs_3_, ...), custom_call_target="tpu_custom_call" | custom-call | flops 276824064 | bytes 2162688 | tf_op jit(solution)/shard_map/pallas_call | solution.py:146
  49.8 1.4 %collective-permute-done.5.returned = bf16[128,384]{1,0:T(8,128)(2,1)S(1)} collective-permute-done((bf16[128,384]{1,0:T(8,128)(2,1)S(1)}, bf16[128,384]{1,0:T(8,128)(2,1)S(1)}, u32[]{:S(2)}, u32[]{:S(2)}) %collective-permute-start.5) | collective-permute-done | bytes 98336 | tf_op jit(solution)/shard_map/ppermute | solution.py:463
  51.3 2.0 %shard_map.115 = (bf16[704,128]{1,0:T(8,128)(2,1)}, bf16[128,384]{1,0:T(8,128)(2,1)}) custom-call(s32[128,128]{1,0:T(8,128)S(1)} %get-tuple-element.29.ids, f32[128,384]{1,0:T(8,128)S(1)} %get-tuple-element.30.normed, f32[128,128]{1,0:T(8,128)S(1)} %get-tuple-element.31.factor, f32[128,384]{1,0:T(8,128)S(1)} %get-tuple-element.41.attended, ...), custom_call_target="tpu_custom_call" | custom-call | flops 553648128 | bytes 4325376 | tf_op jit(solution)/shard_map/pallas_call | solution.py:146
  (34 shorter events, 2.0 us)
Async XLA Ops:
  0.6 2.6 %copy-start = (bf16[1,704,384]{2,1,0:T(8,128)(2,1)S(1)}, bf16[1,704,384]{2,1,0:T(8,128)(2,1)}, u32[]{:S(2)}) copy-start(bf16[1,704,384]{2,1,0:T(8,128)(2,1)} %param.13) | copy-start | bytes 1622020
  0.6 16.3 %copy-start.2 = (bf16[1,128,1408]{2,1,0:T(8,128)(2,1)S(1)}, bf16[1,128,1408]{2,1,0:T(8,128)(2,1)}, u32[]{:S(2)}) copy-start(bf16[1,128,1408]{2,1,0:T(8,128)(2,1)} %param.8) | copy-start | bytes 1081348
  0.7 24.0 %copy-start.1 = (bf16[704,1408]{1,0:T(8,128)(2,1)S(1)}, bf16[704,1408]{1,0:T(8,128)(2,1)}, u32[]{:S(2)}) copy-start(bf16[704,1408]{1,0:T(8,128)(2,1)} %query_weight.1) | copy-start | bytes 5947396
  2.7 22.0 %collective-permute-start = (bf16[352,1408]{1,0:T(8,128)(2,1)S(1)}, bf16[352,1408]{1,0:T(8,128)(2,1)S(1)}, u32[]{:S(2)}, u32[]{:S(2)}) collective-permute-start(bf16[352,1408]{1,0:T(8,128)(2,1)S(1)} %add_convert_fusion.own_weight), channel_id=1, source_target_pairs={{0,8},{8,0},{16,24},{24,16},{1,9},{9,1},{17,25},{25,17},{2,10},{10... | collective-permute-start | bytes 2973704 | tf_op jit(solution)/shard_map/ppermute | solution.py:427
  3.2 9.9 %collective-permute-start.6 = (bf16[704,384]{1,0:T(8,128)(2,1)S(1)}, bf16[704,384]{1,0:T(8,128)(2,1)S(1)}, u32[]{:S(2)}, u32[]{:S(2)}) collective-permute-start(bf16[704,384]{1,0:T(8,128)(2,1)S(1)} %bitcast.8), channel_id=1, source_target_pairs={{0,2},{2,4},{4,6},{6,7},{7,5},{5,3},{3,1},{1,0},{10,8},{12,10},{14... | collective-permute-start | bytes 1622024 | tf_op jit(solution)/shard_map/ppermute | solution.py:472
  13.2 6.5 %collective-permute-start.8 = (bf16[352,384]{1,0:T(8,128)(2,1)S(1)}, bf16[352,384]{1,0:T(8,128)(2,1)S(1)}, u32[]{:S(2)}, u32[]{:S(2)}) collective-permute-start(bf16[352,384]{1,0:T(8,128)(2,1)S(1)} %get-tuple-element.43), channel_id=1, source_target_pairs={{0,2},{2,4},{4,6},{6,7},{7,5},{5,3},{3,1},{1,0},{10,8},{12,10},{14... | collective-permute-start | bytes 811016 | tf_op jit(solution)/shard_map/ppermute | solution.py:475
  15.3 7.3 %collective-permute-start.9 = (bf16[352,384]{1,0:T(8,128)(2,1)S(1)}, bf16[352,384]{1,0:T(8,128)(2,1)S(1)}, u32[]{:S(2)}, u32[]{:S(2)}) collective-permute-start(bf16[352,384]{1,0:T(8,128)(2,1)S(1)} %get-tuple-element.44), channel_id=1, source_target_pairs={{0,2},{2,4},{4,6},{6,7},{7,5},{5,3},{3,1},{1,0},{10,8},{12,10},{14... | collective-permute-start | bytes 811016 | tf_op jit(solution)/shard_map/ppermute | solution.py:476
  17.4 10.5 %collective-permute-start.1 = (bf16[128,704]{1,0:T(8,128)(2,1)S(1)}, bf16[128,704]{1,0:T(8,128)(2,1)S(1)}, u32[]{:S(2)}, u32[]{:S(2)}) collective-permute-start(bf16[128,704]{1,0:T(8,128)(2,1)S(1)} %get-tuple-element.33), channel_id=1, source_target_pairs={{0,16},{8,24},{16,0},{24,8},{1,17},{9,25},{17,1},{25,9},{2,18},{10... | collective-permute-start | bytes 540680 | tf_op jit(solution)/shard_map/ppermute | solution.py:428
  19.7 9.4 %collective-permute-start.11 = (bf16[352,384]{1,0:T(8,128)(2,1)S(1)}, bf16[352,384]{1,0:T(8,128)(2,1)S(1)}, u32[]{:S(2)}, u32[]{:S(2)}) collective-permute-start(bf16[352,384]{1,0:T(8,128)(2,1)S(1)} %collective-permute-done.8.first), channel_id=1, source_target_pairs={{0,2},{2,4},{4,6},{6,7},{7,5},{5,3},{3,1},{1,0},{10,8},{12,10},{14... | collective-permute-start | bytes 811016 | tf_op jit(solution)/shard_map/ppermute | solution.py:475
  22.6 7.1 %collective-permute-start.12 = (bf16[352,384]{1,0:T(8,128)(2,1)S(1)}, bf16[352,384]{1,0:T(8,128)(2,1)S(1)}, u32[]{:S(2)}, u32[]{:S(2)}) collective-permute-start(bf16[352,384]{1,0:T(8,128)(2,1)S(1)} %collective-permute-done.9.second), channel_id=1, source_target_pairs={{0,2},{2,4},{4,6},{6,7},{7,5},{5,3},{3,1},{1,0},{10,8},{12,10},{14... | collective-permute-start | bytes 811016 | tf_op jit(solution)/shard_map/ppermute | solution.py:476
  26.4 11.9 %collective-permute-start.3 = (bf16[128,1152]{1,0:T(8,128)(2,1)S(1)}, bf16[128,1152]{1,0:T(8,128)(2,1)S(1)}, u32[]{:S(2)}, u32[]{:S(2)}) collective-permute-start(bf16[128,1152]{1,0:T(8,128)(2,1)S(1)} %get-tuple-element.37), channel_id=1, source_target_pairs={{0,16},{8,24},{16,0},{24,8},{1,17},{9,25},{17,1},{25,9},{2,18},{10... | collective-permute-start | bytes 884744 | tf_op jit(solution)/shard_map/ppermute | solution.py:443
  28.4 9.5 %collective-permute-start.2 = (bf16[128,768]{1,0:T(8,128)(2,1)S(1)}, bf16[128,768]{1,0:T(8,128)(2,1)S(1)}, u32[]{:S(2)}, u32[]{:S(2)}) collective-permute-start(bf16[128,768]{1,0:T(8,128)(2,1)S(1)} %get-tuple-element.36), channel_id=1, source_target_pairs={{0,16},{8,24},{16,0},{24,8},{1,17},{9,25},{17,1},{25,9},{2,18},{10... | collective-permute-start | bytes 589832 | tf_op jit(solution)/shard_map/ppermute | solution.py:450
  29.0 18.8 %collective-permute-start.7 = (bf16[704,384]{1,0:T(8,128)(2,1)S(1)}, bf16[704,384]{1,0:T(8,128)(2,1)S(1)}, u32[]{:S(2)}, u32[]{:S(2)}) collective-permute-start(bf16[704,384]{1,0:T(8,128)(2,1)S(1)} %collective-permute-done.6.refs_1_.whole), channel_id=1, source_target_pairs={{0,8},{8,0},{16,24},{24,16},{1,9},{9,1},{17,25},{25,17},{2,10},{10... | collective-permute-start | bytes 1622024 | tf_op jit(solution)/shard_map/ppermute | solution.py:478
  29.1 18.5 %copy-start.3 = (bf16[1,128,384]{2,1,0:T(8,128)(2,1)S(1)}, bf16[1,128,384]{2,1,0:T(8,128)(2,1)}, u32[]{:S(2)}) copy-start(bf16[1,128,384]{2,1,0:T(8,128)(2,1)} %param.12) | copy-start | bytes 294916
  29.1 18.5 %copy-start.4 = (s32[1,64,1]{1,2,0:T(1,128)S(1)}, s32[1,64,1]{1,2,0:T(1,128)}, u32[]{:S(2)}) copy-start(s32[1,64,1]{1,2,0:T(1,128)} %param.15) | copy-start | bytes 772
  29.1 18.5 %copy-start.5 = (s32[1,64]{1,0:T(1,128)S(1)}, s32[1,64]{1,0:T(1,128)}, u32[]{:S(2)}) copy-start(s32[1,64]{1,0:T(1,128)} %mask.1) | copy-start | bytes 772
  29.1 19.4 %collective-permute-start.10 = (bf16[704,384]{1,0:T(8,128)(2,1)S(1)}, bf16[704,384]{1,0:T(8,128)(2,1)S(1)}, u32[]{:S(2)}, u32[]{:S(2)}) collective-permute-start(bf16[704,384]{1,0:T(8,128)(2,1)S(1)} %shard_map.111.refs_0_.refs_3_), channel_id=1, source_target_pairs={{0,8},{8,0},{16,24},{24,16},{1,9},{9,1},{17,25},{25,17},{2,10},{10... | collective-permute-start | bytes 1622024 | tf_op jit(solution)/shard_map/ppermute | solution.py:478
  29.8 18.8 %collective-permute-start.13 = (bf16[704,384]{1,0:T(8,128)(2,1)S(1)}, bf16[704,384]{1,0:T(8,128)(2,1)S(1)}, u32[]{:S(2)}, u32[]{:S(2)}) collective-permute-start(bf16[704,384]{1,0:T(8,128)(2,1)S(1)} %shard_map.112.refs_2_.refs_5_), channel_id=1, source_target_pairs={{0,8},{8,0},{16,24},{24,16},{1,9},{9,1},{17,25},{25,17},{2,10},{10... | collective-permute-start | bytes 1622024 | tf_op jit(solution)/shard_map/ppermute | solution.py:478
  37.9 6.5 %collective-permute-start.14 = (bf16[352,384]{1,0:T(8,128)(2,1)S(1)}, bf16[352,384]{1,0:T(8,128)(2,1)S(1)}, u32[]{:S(2)}, u32[]{:S(2)}) collective-permute-start(bf16[352,384]{1,0:T(8,128)(2,1)S(1)} %collective-permute-done.11.first), channel_id=1, source_target_pairs={{0,2},{2,4},{4,6},{6,7},{7,5},{5,3},{3,1},{1,0},{10,8},{12,10},{14... | collective-permute-start | bytes 811016 | tf_op jit(solution)/shard_map/ppermute | solution.py:481
  38.4 6.0 %collective-permute-start.4 = (bf16[256,768]{1,0:T(8,128)(2,1)S(1)}, bf16[256,768]{1,0:T(8,128)(2,1)S(1)}, u32[]{:S(2)}, u32[]{:S(2)}) collective-permute-start(bf16[256,768]{1,0:T(8,128)(2,1)S(1)} %get-tuple-element.40.kv_a), channel_id=1, source_target_pairs={{0,8},{8,0},{16,24},{24,16},{1,9},{9,1},{17,25},{25,17},{2,10},{10... | collective-permute-start | bytes 1179656 | tf_op jit(solution)/shard_map/ppermute | solution.py:456
  44.4 5.0 %collective-permute-start.15 = (bf16[352,384]{1,0:T(8,128)(2,1)S(1)}, bf16[352,384]{1,0:T(8,128)(2,1)S(1)}, u32[]{:S(2)}, u32[]{:S(2)}) collective-permute-start(bf16[352,384]{1,0:T(8,128)(2,1)S(1)} %collective-permute-done.14.mine), channel_id=1, source_target_pairs={{0,8},{8,0},{16,24},{24,16},{1,9},{9,1},{17,25},{25,17},{2,10},{10... | collective-permute-start | bytes 811016 | tf_op jit(solution)/shard_map/ppermute | solution.py:482
  46.0 5.3 %collective-permute-start.5 = (bf16[128,384]{1,0:T(8,128)(2,1)S(1)}, bf16[128,384]{1,0:T(8,128)(2,1)S(1)}, u32[]{:S(2)}, u32[]{:S(2)}) collective-permute-start(bf16[128,384]{1,0:T(8,128)(2,1)S(1)} %get-tuple-element.42), channel_id=1, source_target_pairs={{0,16},{8,24},{16,0},{24,8},{1,17},{9,25},{17,1},{25,9},{2,18},{10... | collective-permute-start | bytes 294920 | tf_op jit(solution)/shard_map/ppermute | solution.py:463

commit v7 on v5

--- a/solution.py
+++ b/solution.py
@@ -217,11 +217,11 @@
     depth = target.shape[0]
     own_rows = pl.ds(pl.multiple_of(core * depth, 16), depth)
     joined[own_rows, :] = blend(target, context)
+    store = pltpu.make_async_copy(joined.at[own_rows], stored, sem)
+    store.start()
     joined[pl.ds(pl.multiple_of((1 - core) * depth, 16), depth), :] = blend(
         other_target, other_context
     )
-    store = pltpu.make_async_copy(joined.at[own_rows], stored, sem)
-    store.start()
     split_product(rows, joined, own, send)
     queries = lax.dot_general(
         normed[...], query_weight[...], (((1,), (1,)), ((), ())), preferred_element_type=jnp.float32
@@ -272,14 +272,27 @@
     return total
 
 
-def attend_body(queries, kv_a, kv_b, mine, theirs):
+def attend_body(queries, kv_a, kv_b, mine, theirs, last):
+    chip, _ = chip_and_core()
     upper_lane = lax.broadcasted_iota(jnp.int32, (1, LANES), 1) >= HEAD
     rows = mine.shape[0]
+    found = [None] * 6
+
+    @pl.when(chip == 0)
+    def _():
+        last[...] = jnp.zeros_like(last)
+
+    @pl.when(chip != 0)
+    def _():
+        total = add_keys(queries, (kv_a, kv_b), 5)
+        last[...] = total / pltpu.roll(total, HEAD, 1)
+
+    for slot in range(5):
+        total = add_keys(queries, (kv_a, kv_b), slot)
+        found[slot + 1] = total / pltpu.roll(total, HEAD, 1)
+    found[0] = last[...]
     for t in range(3):
-        low = add_keys(queries, (kv_a, kv_b), (2 * t + 5) % 6)
-        high = add_keys(queries, (kv_a, kv_b), 2 * t)
-        sums = pltpu.roll(jnp.where(upper_lane, low, high), HEAD, 1)
-        joined = jnp.where(upper_lane, high, low) / sums
+        joined = jnp.where(upper_lane, found[2 * t + 1], found[2 * t])
         mine[:, t * LANES : (t + 1) * LANES] = joined[:rows]
         theirs[:, t * LANES : (t + 1) * LANES] = joined[rows:].astype(theirs.dtype)
 
@@ -311,7 +324,7 @@
 
 def slot_owners(groups):
     _, core = chip_and_core()
-    sign = 2 * core - 1
+    sign = 1 - 2 * core
     owners = [owner_at(0, groups)]
     for step in range(1, groups // 2):
         owners += [owner_at(sign * step, groups), owner_at(-sign * step, groups)]
@@ -405,7 +418,7 @@
     for member in range(members):
         for i in range(groups):
             a, b = order[i], order[(i + 1) % groups]
-            a, b = (a, b) if member % 2 == 0 else (b, a)
+            a, b = (b, a) if member % 2 == 0 else (a, b)
             pairs.append((member * groups + a, member * groups + b))
     return pairs
 
@@ -467,6 +480,7 @@
         attend_body,
         [shape_of((rows, packed), jnp.float32), shape_of((rows, packed))],
         (queries, kv, kv_beside),
+        scratch=[pltpu.VMEM((2 * rows, LANES), jnp.float32)],
         cost=matmul_cost(2 * rows, 12 * LANES, 4 * rows, 12 * rows * 4 * rows),
     )
     returned = lax.ppermute(send_back, "seq", across)

time: 51.9 us -> 51.5 us (level)
  Pallas kernels: 9.58 us -> 9.04 us
    pallas_call x13, Pallas kernels: 9.58 us -> 9.04 us  [local_call(): pl.pallas_call(body, out_shape=outs, in_specs=specs or [VM] * len(operand...]
  transfers between devices with their start and end apart: 17 -> 17, of which waited for: 5 -> 5; matrix products, arithmetic and copies ran while one was open for 0% -> 0% of each run, Pallas kernels for 15% -> 14%
where the time goes in v7:
time: 51.5 us; the launch traced here: 51.4 us
  waiting for transfers between devices  22.9 us (44%)
  starting transfers between devices  17.6 us (34%)
  Pallas kernels  9.04 us (18%)
  local copies, waits for them, and re-layouts  1.02 us (2%)
  between operations  0.83 us (2%)
    pallas_call x13, Pallas kernels, local_call(): pl.pallas_call(body, out_shape=outs, in_specs=specs or [VM] * len(operand...  9.04 us
    ppermute x1, waiting for transfers between devices, paired_shards(): from_other = lax.ppermute(other_send, 'seq', across)  7.58 us
    ppermute x1, waiting for transfers between devices, paired_shards(): held = lax.ppermute(pred_weight[0], ('seq', 'grp'), ring)  7.09 us
    ppermute x1, waiting for transfers between devices, paired_shards(): mine = lax.ppermute(first, ('seq', 'grp'), ring)  6.06 us
    ppermute x2, starting transfers between devices, paired_shards(): first = lax.ppermute(first, ('seq', 'grp'), ring)  3.86 us
    ppermute x2, starting transfers between devices, paired_shards(): second = lax.ppermute(second, ('seq', 'grp'), ring)  3.54 us
    ppermute x1, starting transfers between devices, paired_shards(): held = lax.ppermute(pred_weight[0], ('seq', 'grp'), ring)  3.05 us
    ppermute x1, starting transfers between devices, paired_shards(): returned = lax.ppermute(send_back, 'seq', across)  2 us
  transfers between devices with their start and end apart: 17, of which 5 were waited for; matrix products, arithmetic and copies ran while one was open for 0% of the time, Pallas kernels for 14%

profile of v7, /device:TPU:0, one launch (start us, length us, event | category | flops | bytes accessed | tf_op | source)
XLA Modules:
  0.0 51.4 jit_solution(9882036223563227235)
XLA Ops:
  0.6 3.0 %collective-permute-start.7 = (bf16[704,384]{1,0:T(8,128)(2,1)}, bf16[704,384]{1,0:T(8,128)(2,1)S(1)}, u32[]{:S(2)}, u32[]{:S(2)}) collective-permute-start(bf16[704,384]{1,0:T(8,128)(2,1)} %bitcast.8), channel_id=1, source_target_pairs={{2,0},{4,2},{6,4},{7,6},{5,7},{3,5},{1,3},{0,1},{8,10},{10,12},{12... | collective-permute-start | bytes 1622024 | tf_op jit(solution)/shard_map/ppermute | solution.py:495
  3.7 0.5 collective-permute-start.1
  4.2 7.1 %collective-permute-done.7.refs_1_.whole = bf16[704,384]{1,0:T(8,128)(2,1)S(1)} collective-permute-done((bf16[704,384]{1,0:T(8,128)(2,1)}, bf16[704,384]{1,0:T(8,128)(2,1)S(1)}, u32[]{:S(2)}, u32[]{:S(2)}) %collective-permute-start.7) | collective-permute-done | bytes 540704 | tf_op jit(solution)/shard_map/ppermute | solution.py:495
  11.3 2.0 %collective-permute-start.9 = (bf16[352,384]{1,0:T(8,128)(2,1)S(1)}, bf16[352,384]{1,0:T(8,128)(2,1)S(1)}, u32[]{:S(2)}, u32[]{:S(2)}) collective-permute-start(bf16[352,384]{1,0:T(8,128)(2,1)S(1)} %get-tuple-element.43), channel_id=1, source_target_pairs={{2,0},{4,2},{6,4},{7,6},{5,7},{3,5},{1,3},{0,1},{8,10},{10,12},{12... | collective-permute-start | bytes 811016 | tf_op jit(solution)/shard_map/ppermute | solution.py:498
  13.3 1.6 %collective-permute-start.10 = (bf16[352,384]{1,0:T(8,128)(2,1)S(1)}, bf16[352,384]{1,0:T(8,128)(2,1)S(1)}, u32[]{:S(2)}, u32[]{:S(2)}) collective-permute-start(bf16[352,384]{1,0:T(8,128)(2,1)S(1)} %get-tuple-element.44), channel_id=1, source_target_pairs={{2,0},{4,2},{6,4},{7,6},{5,7},{3,5},{1,3},{0,1},{8,10},{10,12},{12... | collective-permute-start | bytes 811016 | tf_op jit(solution)/shard_map/ppermute | solution.py:499
  14.9 1.0 %copy-done.7 = bf16[1,128,1408]{2,1,0:T(8,128)(2,1)S(1)} copy-done((bf16[1,128,1408]{2,1,0:T(8,128)(2,1)S(1)}, bf16[1,128,1408]{2,1,0:T(8,128)(2,1)}, u32[]{:S(2)}) %copy-start.7) | copy-done | bytes 360472
  15.9 0.5 shard_map.103
  16.4 1.6 %collective-permute-start.2 = (bf16[128,704]{1,0:T(8,128)(2,1)S(1)}, bf16[128,704]{1,0:T(8,128)(2,1)S(1)}, u32[]{:S(2)}, u32[]{:S(2)}) collective-permute-start(bf16[128,704]{1,0:T(8,128)(2,1)S(1)} %get-tuple-element.33), channel_id=1, source_target_pairs={{0,16},{8,24},{16,0},{24,8},{1,17},{9,25},{17,1},{25,9},{2,18},{10... | collective-permute-start | bytes 540680 | tf_op jit(solution)/shard_map/ppermute | solution.py:450
  18.0 1.9 %collective-permute-start.12 = (bf16[352,384]{1,0:T(8,128)(2,1)S(1)}, bf16[352,384]{1,0:T(8,128)(2,1)S(1)}, u32[]{:S(2)}, u32[]{:S(2)}) collective-permute-start(bf16[352,384]{1,0:T(8,128)(2,1)S(1)} %collective-permute-done.9.first), channel_id=1, source_target_pairs={{2,0},{4,2},{6,4},{7,6},{5,7},{3,5},{1,3},{0,1},{8,10},{10,12},{12... | collective-permute-start | bytes 811016 | tf_op jit(solution)/shard_map/ppermute | solution.py:498
  19.8 0.9 %collective-permute-done.10.second = bf16[352,384]{1,0:T(8,128)(2,1)S(1)} collective-permute-done((bf16[352,384]{1,0:T(8,128)(2,1)S(1)}, bf16[352,384]{1,0:T(8,128)(2,1)S(1)}, u32[]{:S(2)}, u32[]{:S(2)}) %collective-permute-start.10) | collective-permute-done | bytes 270368 | tf_op jit(solution)/shard_map/ppermute | solution.py:499
  20.7 2.0 %collective-permute-start.13 = (bf16[352,384]{1,0:T(8,128)(2,1)S(1)}, bf16[352,384]{1,0:T(8,128)(2,1)S(1)}, u32[]{:S(2)}, u32[]{:S(2)}) collective-permute-start(bf16[352,384]{1,0:T(8,128)(2,1)S(1)} %collective-permute-done.10.second), channel_id=1, source_target_pairs={{2,0},{4,2},{6,4},{7,6},{5,7},{3,5},{1,3},{0,1},{8,10},{10,12},{12... | collective-permute-start | bytes 811016 | tf_op jit(solution)/shard_map/ppermute | solution.py:499
  22.7 2.2 %shard_map.104 = (bf16[704,1408]{1,0:T(8,128)(2,1)S(1)}, f32[128,768]{1,0:T(8,128)S(1)}, bf16[128,384]{1,0:T(8,128)(2,1)S(1)}, bf16[128,1152]{1,0:T(8,128)(2,1)S(1)}, bf16[352,1408]{1,0:T(8,128)(2,1)}) custom-call(bf16[352,1408]{1,0:T(8,128)(2,1)S(1)} %copy-done.2, bf16[352,1408]{1,0:T(8,128)(2,1)S(1)} %copy-done.3, ...), custom_call_target="tpu_custom_call" | custom-call | flops 507510784 | bytes 3964928 | tf_op jit(solution)/shard_map/pallas_call | solution.py:146
  25.0 1.6 %collective-permute-start.4 = (bf16[128,1152]{1,0:T(8,128)(2,1)S(1)}, bf16[128,1152]{1,0:T(8,128)(2,1)S(1)}, u32[]{:S(2)}, u32[]{:S(2)}) collective-permute-start(bf16[128,1152]{1,0:T(8,128)(2,1)S(1)} %get-tuple-element.37), channel_id=1, source_target_pairs={{0,16},{8,24},{16,0},{24,8},{1,17},{9,25},{17,1},{25,9},{2,18},{10... | collective-permute-start | bytes 884744 | tf_op jit(solution)/shard_map/ppermute | solution.py:465
  26.5 0.5 shard_map.106
  27.0 0.6 %collective-permute-start.3 = (bf16[128,768]{1,0:T(8,128)(2,1)S(1)}, bf16[128,768]{1,0:T(8,128)(2,1)S(1)}, u32[]{:S(2)}, u32[]{:S(2)}) collective-permute-start(bf16[128,768]{1,0:T(8,128)(2,1)S(1)} %get-tuple-element.36), channel_id=1, source_target_pairs={{0,16},{8,24},{16,0},{24,8},{1,17},{9,25},{17,1},{25,9},{2,18},{10... | collective-permute-start | bytes 589832 | tf_op jit(solution)/shard_map/ppermute | solution.py:472
  27.8 0.6 %collective-permute-start.11 = (bf16[704,384]{1,0:T(8,128)(2,1)S(1)}, bf16[704,384]{1,0:T(8,128)(2,1)S(1)}, u32[]{:S(2)}, u32[]{:S(2)}) collective-permute-start(bf16[704,384]{1,0:T(8,128)(2,1)S(1)} %shard_map.111.refs_0_.refs_3_), channel_id=1, source_target_pairs={{0,8},{8,0},{16,24},{24,16},{1,9},{9,1},{17,25},{25,17},{2,10},{10... | collective-permute-start | bytes 1622024 | tf_op jit(solution)/shard_map/ppermute | solution.py:501
  28.5 7.6 %collective-permute-done.3.from_other = bf16[128,768]{1,0:T(8,128)(2,1)S(1)} collective-permute-done((bf16[128,768]{1,0:T(8,128)(2,1)S(1)}, bf16[128,768]{1,0:T(8,128)(2,1)S(1)}, u32[]{:S(2)}, u32[]{:S(2)}) %collective-permute-start.3) | collective-permute-done | bytes 196640 | tf_op jit(solution)/shard_map/ppermute | solution.py:472
  36.5 6.1 %collective-permute-done.15.mine = bf16[352,384]{1,0:T(8,128)(2,1)S(1)} collective-permute-done((bf16[352,384]{1,0:T(8,128)(2,1)S(1)}, bf16[352,384]{1,0:T(8,128)(2,1)S(1)}, u32[]{:S(2)}, u32[]{:S(2)}) %collective-permute-start.15) | collective-permute-done | bytes 270368 | tf_op jit(solution)/shard_map/ppermute | solution.py:504
  42.5 1.4 %shard_map.108 = (f32[128,384]{1,0:T(8,128)S(1)}, bf16[128,384]{1,0:T(8,128)(2,1)S(1)}) custom-call(bf16[256,384]{1,0:T(8,128)(2,1)S(1)} %get-tuple-element.39.queries, bf16[256,768]{1,0:T(8,128)(2,1)S(1)} %get-tuple-element.40.kv_a, bf16[256,768]{1,0:T(8,128)(2,1)S(1)} %collective-permute-done.5.kv_b), custom_call_target="tpu_custom_call" | custom-call | flops 402653184 | bytes 1572864 | tf_op jit(solution)/shard_map/pallas_call | solution.py:146
  43.9 2.0 %collective-permute-start.6 = (bf16[128,384]{1,0:T(8,128)(2,1)S(1)}, bf16[128,384]{1,0:T(8,128)(2,1)S(1)}, u32[]{:S(2)}, u32[]{:S(2)}) collective-permute-start(bf16[128,384]{1,0:T(8,128)(2,1)S(1)} %get-tuple-element.42), channel_id=1, source_target_pairs={{0,16},{8,24},{16,0},{24,8},{1,17},{9,25},{17,1},{25,9},{2,18},{10... | collective-permute-start | bytes 294920 | tf_op jit(solution)/shard_map/ppermute | solution.py:486
  46.2 0.7 %shard_map.109.earlier = f32[128,704]{1,0:T(8,128)S(1)} custom-call(s32[128,128]{1,0:T(8,128)S(1)} %get-tuple-element.29.ids, f32[128,384]{1,0:T(8,128)S(1)} %get-tuple-element.30.normed, bf16[704,384]{1,0:T(8,128)(2,1)S(1)} %bitcast.9, bf16[704,384]{1,0:T(8,128)(2,1)S(1)} %collective-permute-done.7.refs_1_.whole, ...), custom_call_target="tpu_custom_call" | custom-call | flops 207618048 | bytes 1622016 | tf_op jit(solution)/shard_map/pallas_call | solution.py:146
  46.9 0.9 %shard_map.113.earlier = f32[128,704]{1,0:T(8,128)S(1)} custom-call(s32[128,128]{1,0:T(8,128)S(1)} %get-tuple-element.29.ids, f32[128,384]{1,0:T(8,128)S(1)} %get-tuple-element.30.normed, f32[128,704]{1,0:T(8,128)S(1)} %shard_map.109.earlier, bf16[704,384]{1,0:T(8,128)(2,1)S(1)} %shard_map.111.refs_0_.refs_3_, ...), custom_call_target="tpu_custom_call" | custom-call | flops 276824064 | bytes 2162688 | tf_op jit(solution)/shard_map/pallas_call | solution.py:146
  48.2 1.2 %collective-permute-done.6.returned = bf16[128,384]{1,0:T(8,128)(2,1)S(1)} collective-permute-done((bf16[128,384]{1,0:T(8,128)(2,1)S(1)}, bf16[128,384]{1,0:T(8,128)(2,1)S(1)}, u32[]{:S(2)}, u32[]{:S(2)}) %collective-permute-start.6) | collective-permute-done | bytes 98336 | tf_op jit(solution)/shard_map/ppermute | solution.py:486
  49.4 2.0 %shard_map.115 = (bf16[704,128]{1,0:T(8,128)(2,1)}, bf16[128,384]{1,0:T(8,128)(2,1)}) custom-call(s32[128,128]{1,0:T(8,128)S(1)} %get-tuple-element.29.ids, f32[128,384]{1,0:T(8,128)S(1)} %get-tuple-element.30.normed, f32[128,128]{1,0:T(8,128)S(1)} %get-tuple-element.31.factor, f32[128,384]{1,0:T(8,128)S(1)} %get-tuple-element.41.attended, ...), custom_call_target="tpu_custom_call" | custom-call | flops 553648128 | bytes 4325376 | tf_op jit(solution)/shard_map/pallas_call | solution.py:146
  (39 shorter events, 1.3 us)
Async XLA Ops:
  0.6 10.7 %collective-permute-start.7 = (bf16[704,384]{1,0:T(8,128)(2,1)}, bf16[704,384]{1,0:T(8,128)(2,1)S(1)}, u32[]{:S(2)}, u32[]{:S(2)}) collective-permute-start(bf16[704,384]{1,0:T(8,128)(2,1)} %bitcast.8), channel_id=1, source_target_pairs={{2,0},{4,2},{6,4},{7,6},{5,7},{3,5},{1,3},{0,1},{8,10},{10,12},{12... | collective-permute-start | bytes 1622024 | tf_op jit(solution)/shard_map/ppermute | solution.py:495
  3.7 19.0 %collective-permute-start = (bf16[352,1408]{1,0:T(8,128)(2,1)}, bf16[352,1408]{1,0:T(8,128)(2,1)S(1)}, u32[]{:S(2)}, u32[]{:S(2)}) collective-permute-start(bf16[352,1408]{1,0:T(8,128)(2,1)} %target.1), channel_id=1, source_target_pairs={{0,8},{8,0},{16,24},{24,16},{1,9},{9,1},{17,25},{25,17},{2,10},{10... | collective-permute-start | bytes 2973704 | tf_op jit(solution)/shard_map/ppermute | solution.py:442
  3.7 19.0 %collective-permute-start.1 = (bf16[352,1408]{1,0:T(8,128)(2,1)}, bf16[352,1408]{1,0:T(8,128)(2,1)S(1)}, u32[]{:S(2)}, u32[]{:S(2)}) collective-permute-start(bf16[352,1408]{1,0:T(8,128)(2,1)} %context.1), channel_id=1, source_target_pairs={{0,8},{8,0},{16,24},{24,16},{1,9},{9,1},{17,25},{25,17},{2,10},{10... | collective-permute-start | bytes 2973704 | tf_op jit(solution)/shard_map/ppermute | solution.py:443
  11.3 6.6 %collective-permute-start.9 = (bf16[352,384]{1,0:T(8,128)(2,1)S(1)}, bf16[352,384]{1,0:T(8,128)(2,1)S(1)}, u32[]{:S(2)}, u32[]{:S(2)}) collective-permute-start(bf16[352,384]{1,0:T(8,128)(2,1)S(1)} %get-tuple-element.43), channel_id=1, source_target_pairs={{2,0},{4,2},{6,4},{7,6},{5,7},{3,5},{1,3},{0,1},{8,10},{10,12},{12... | collective-permute-start | bytes 811016 | tf_op jit(solution)/shard_map/ppermute | solution.py:498
  13.3 7.4 %collective-permute-start.10 = (bf16[352,384]{1,0:T(8,128)(2,1)S(1)}, bf16[352,384]{1,0:T(8,128)(2,1)S(1)}, u32[]{:S(2)}, u32[]{:S(2)}) collective-permute-start(bf16[352,384]{1,0:T(8,128)(2,1)S(1)} %get-tuple-element.44), channel_id=1, source_target_pairs={{2,0},{4,2},{6,4},{7,6},{5,7},{3,5},{1,3},{0,1},{8,10},{10,12},{12... | collective-permute-start | bytes 811016 | tf_op jit(solution)/shard_map/ppermute | solution.py:499
  15.9 6.8 %copy-start.1 = (bf16[704,1408]{1,0:T(8,128)(2,1)S(1)}, bf16[704,1408]{1,0:T(8,128)(2,1)}, u32[]{:S(2)}) copy-start(bf16[704,1408]{1,0:T(8,128)(2,1)} %query_weight.1) | copy-start | bytes 5947396
  15.9 6.8 %copy-start.2 = (bf16[352,1408]{1,0:T(8,128)(2,1)S(1)}, bf16[352,1408]{1,0:T(8,128)(2,1)}, u32[]{:S(2)}) copy-start(bf16[352,1408]{1,0:T(8,128)(2,1)} %target.1) | copy-start | bytes 2973700
  15.9 6.8 %copy-start.3 = (bf16[352,1408]{1,0:T(8,128)(2,1)S(1)}, bf16[352,1408]{1,0:T(8,128)(2,1)}, u32[]{:S(2)}) copy-start(bf16[352,1408]{1,0:T(8,128)(2,1)} %context.1) | copy-start | bytes 2973700
  16.4 10.1 %collective-permute-start.2 = (bf16[128,704]{1,0:T(8,128)(2,1)S(1)}, bf16[128,704]{1,0:T(8,128)(2,1)S(1)}, u32[]{:S(2)}, u32[]{:S(2)}) collective-permute-start(bf16[128,704]{1,0:T(8,128)(2,1)S(1)} %get-tuple-element.33), channel_id=1, source_target_pairs={{0,16},{8,24},{16,0},{24,8},{1,17},{9,25},{17,1},{25,9},{2,18},{10... | collective-permute-start | bytes 540680 | tf_op jit(solution)/shard_map/ppermute | solution.py:450
  18.0 9.8 %collective-permute-start.12 = (bf16[352,384]{1,0:T(8,128)(2,1)S(1)}, bf16[352,384]{1,0:T(8,128)(2,1)S(1)}, u32[]{:S(2)}, u32[]{:S(2)}) collective-permute-start(bf16[352,384]{1,0:T(8,128)(2,1)S(1)} %collective-permute-done.9.first), channel_id=1, source_target_pairs={{2,0},{4,2},{6,4},{7,6},{5,7},{3,5},{1,3},{0,1},{8,10},{10,12},{12... | collective-permute-start | bytes 811016 | tf_op jit(solution)/shard_map/ppermute | solution.py:498
  20.7 7.6 %collective-permute-start.13 = (bf16[352,384]{1,0:T(8,128)(2,1)S(1)}, bf16[352,384]{1,0:T(8,128)(2,1)S(1)}, u32[]{:S(2)}, u32[]{:S(2)}) collective-permute-start(bf16[352,384]{1,0:T(8,128)(2,1)S(1)} %collective-permute-done.10.second), channel_id=1, source_target_pairs={{2,0},{4,2},{6,4},{7,6},{5,7},{3,5},{1,3},{0,1},{8,10},{10,12},{12... | collective-permute-start | bytes 811016 | tf_op jit(solution)/shard_map/ppermute | solution.py:499
  25.0 11.3 %collective-permute-start.4 = (bf16[128,1152]{1,0:T(8,128)(2,1)S(1)}, bf16[128,1152]{1,0:T(8,128)(2,1)S(1)}, u32[]{:S(2)}, u32[]{:S(2)}) collective-permute-start(bf16[128,1152]{1,0:T(8,128)(2,1)S(1)} %get-tuple-element.37), channel_id=1, source_target_pairs={{0,16},{8,24},{16,0},{24,8},{1,17},{9,25},{17,1},{25,9},{2,18},{10... | collective-permute-start | bytes 884744 | tf_op jit(solution)/shard_map/ppermute | solution.py:465
  27.0 9.1 %collective-permute-start.3 = (bf16[128,768]{1,0:T(8,128)(2,1)S(1)}, bf16[128,768]{1,0:T(8,128)(2,1)S(1)}, u32[]{:S(2)}, u32[]{:S(2)}) collective-permute-start(bf16[128,768]{1,0:T(8,128)(2,1)S(1)} %get-tuple-element.36), channel_id=1, source_target_pairs={{0,16},{8,24},{16,0},{24,8},{1,17},{9,25},{17,1},{25,9},{2,18},{10... | collective-permute-start | bytes 589832 | tf_op jit(solution)/shard_map/ppermute | solution.py:472
  27.6 18.5 %collective-permute-start.8 = (bf16[704,384]{1,0:T(8,128)(2,1)S(1)}, bf16[704,384]{1,0:T(8,128)(2,1)S(1)}, u32[]{:S(2)}, u32[]{:S(2)}) collective-permute-start(bf16[704,384]{1,0:T(8,128)(2,1)S(1)} %collective-permute-done.7.refs_1_.whole), channel_id=1, source_target_pairs={{0,8},{8,0},{16,24},{24,16},{1,9},{9,1},{17,25},{25,17},{2,10},{10... | collective-permute-start | bytes 1622024 | tf_op jit(solution)/shard_map/ppermute | solution.py:501
  27.7 18.2 %copy-start.4 = (bf16[1,128,384]{2,1,0:T(8,128)(2,1)S(1)}, bf16[1,128,384]{2,1,0:T(8,128)(2,1)}, u32[]{:S(2)}) copy-start(bf16[1,128,384]{2,1,0:T(8,128)(2,1)} %param.12) | copy-start | bytes 294916
  27.7 18.2 %copy-start.5 = (s32[1,64,1]{1,2,0:T(1,128)S(1)}, s32[1,64,1]{1,2,0:T(1,128)}, u32[]{:S(2)}) copy-start(s32[1,64,1]{1,2,0:T(1,128)} %param.15) | copy-start | bytes 772
  27.7 18.2 %copy-start.6 = (s32[1,64]{1,0:T(1,128)S(1)}, s32[1,64]{1,0:T(1,128)}, u32[]{:S(2)}) copy-start(s32[1,64]{1,0:T(1,128)} %mask.1) | copy-start | bytes 772
  27.7 18.4 %copy-start = (bf16[1,704,384]{2,1,0:T(8,128)(2,1)S(1)}, bf16[1,704,384]{2,1,0:T(8,128)(2,1)}, u32[]{:S(2)}) copy-start(bf16[1,704,384]{2,1,0:T(8,128)(2,1)} %param.13) | copy-start | bytes 1622020
  27.8 19.1 %collective-permute-start.11 = (bf16[704,384]{1,0:T(8,128)(2,1)S(1)}, bf16[704,384]{1,0:T(8,128)(2,1)S(1)}, u32[]{:S(2)}, u32[]{:S(2)}) collective-permute-start(bf16[704,384]{1,0:T(8,128)(2,1)S(1)} %shard_map.111.refs_0_.refs_3_), channel_id=1, source_target_pairs={{0,8},{8,0},{16,24},{24,16},{1,9},{9,1},{17,25},{25,17},{2,10},{10... | collective-permute-start | bytes 1622024 | tf_op jit(solution)/shard_map/ppermute | solution.py:501
  28.4 18.5 %collective-permute-start.14 = (bf16[704,384]{1,0:T(8,128)(2,1)S(1)}, bf16[704,384]{1,0:T(8,128)(2,1)S(1)}, u32[]{:S(2)}, u32[]{:S(2)}) collective-permute-start(bf16[704,384]{1,0:T(8,128)(2,1)S(1)} %shard_map.112.refs_2_.refs_5_), channel_id=1, source_target_pairs={{0,8},{8,0},{16,24},{24,16},{1,9},{9,1},{17,25},{25,17},{2,10},{10... | collective-permute-start | bytes 1622024 | tf_op jit(solution)/shard_map/ppermute | solution.py:501
  36.1 6.5 %collective-permute-start.15 = (bf16[352,384]{1,0:T(8,128)(2,1)S(1)}, bf16[352,384]{1,0:T(8,128)(2,1)S(1)}, u32[]{:S(2)}, u32[]{:S(2)}) collective-permute-start(bf16[352,384]{1,0:T(8,128)(2,1)S(1)} %collective-permute-done.12.first), channel_id=1, source_target_pairs={{2,0},{4,2},{6,4},{7,6},{5,7},{3,5},{1,3},{0,1},{8,10},{10,12},{12... | collective-permute-start | bytes 811016 | tf_op jit(solution)/shard_map/ppermute | solution.py:504
  36.4 6.1 %collective-permute-start.5 = (bf16[256,768]{1,0:T(8,128)(2,1)S(1)}, bf16[256,768]{1,0:T(8,128)(2,1)S(1)}, u32[]{:S(2)}, u32[]{:S(2)}) collective-permute-start(bf16[256,768]{1,0:T(8,128)(2,1)S(1)} %get-tuple-element.40.kv_a), channel_id=1, source_target_pairs={{0,8},{8,0},{16,24},{24,16},{1,9},{9,1},{17,25},{25,17},{2,10},{10... | collective-permute-start | bytes 1179656 | tf_op jit(solution)/shard_map/ppermute | solution.py:478
  42.5 5.3 %collective-permute-start.16 = (bf16[352,384]{1,0:T(8,128)(2,1)S(1)}, bf16[352,384]{1,0:T(8,128)(2,1)S(1)}, u32[]{:S(2)}, u32[]{:S(2)}) collective-permute-start(bf16[352,384]{1,0:T(8,128)(2,1)S(1)} %collective-permute-done.15.mine), channel_id=1, source_target_pairs={{0,8},{8,0},{16,24},{24,16},{1,9},{9,1},{17,25},{25,17},{2,10},{10... | collective-permute-start | bytes 811016 | tf_op jit(solution)/shard_map/ppermute | solution.py:505
  43.9 5.5 %collective-permute-start.6 = (bf16[128,384]{1,0:T(8,128)(2,1)S(1)}, bf16[128,384]{1,0:T(8,128)(2,1)S(1)}, u32[]{:S(2)}, u32[]{:S(2)}) collective-permute-start(bf16[128,384]{1,0:T(8,128)(2,1)S(1)} %get-tuple-element.42), channel_id=1, source_target_pairs={{0,16},{8,24},{16,0},{24,8},{1,17},{9,25},{17,1},{25,9},{2,18},{10... | collective-permute-start | bytes 294920 | tf_op jit(solution)/shard_map/ppermute | solution.py:486
  (1 other events, 1.0 us)
